TPU v7x, 32 devices: a whole 2x2x4 slice. The times are simulated.
32 devices in a mesh: grp: 4 (over y, x), dev: 8 (over z, core).
Axes of the slice: x: 2, y: 2, z: 4, core: 2. Of those that a mesh axis runs over, the one named last changes fastest.
Arguments:
- features: bfloat16 [4096, 768], P(('grp', 'dev')), may hold values from -6 to 6
- neighbours: int32 [4096, 25], P(('grp', 'dev')), may hold values from 0 to 4095, as said below
- neighbour_mask: int32 [4096, 25], P(('grp', 'dev')), may hold values from 0 to 1, as said below
- layer2_position: int32 [4096], P(('grp', 'dev')), may hold values from 0 to 4095, as said below
- self_weight1: bfloat16 [768, 1024], replicated, may hold values from -0.21875 to 0.21875
- neigh_weight1: bfloat16 [768, 1024], replicated, may hold values from -0.4375 to 0.4375
- self_weight2: bfloat16 [1024, 1024], replicated, may hold values from -0.1875 to 0.1875
- neigh_weight2: bfloat16 [1024, 1024], replicated, may hold values from -0.375 to 0.375
Outputs:
- embeddings: bfloat16 [4096, 1024], P(('grp', 'dev'))
Inputs may be any that keep to these rules, and one draw needn't show every extreme that they name: `neighbours`: node n is owned by device n // 128 (devices numbered grp-major). Slot 0 of every node is valid. Of one device's nodes, at most 6 valid slots name nodes of any one other device, and exactly 6 do for some other device; 93 slots of one device name other devices' nodes, all of them valid. Invalid slots hold ids of the device's own nodes. `neighbour_mask`: values 0 or 1; 1 at slot 0 and wherever the neighbour lies on another device. A permutation of the nodes; a node's new owner, layer2_position // 128, is in the same group as its old one. One device hands exactly 32 nodes to each owner of its group whose index within the group differs from its own by an even number, and none to the others.
All inputs are finite; a program needn't handle non-finite values.
Results may differ from a plain program's by a relative error of at most 0.0052.
Values may be sent and summed in bfloat16 or wider, within the bound.
No kernel may reach another device: no remote copies, remote signals or barrier semaphores. Data moves between devices by JAX's collectives and lax.ppermute only.
A program may use at most 64 MiB of HBM per device.

v0:
```python
import jax
import jax.numpy as jnp
from jax import lax
from jax.sharding import PartitionSpec as P

CAP = 6


def slot_of(owners, usable, peer_count, capacity):
    item_count = owners.shape[0]
    sort_key = jnp.where(usable, owners, peer_count)
    ordering = jnp.argsort(sort_key, stable=True)
    per_owner = jnp.zeros((peer_count + 1,), jnp.int32).at[sort_key].add(1)
    starts = jnp.cumsum(per_owner) - per_owner
    ranked = jnp.arange(item_count, dtype=jnp.int32) - starts[sort_key[ordering]]
    ranks = jnp.zeros((item_count,), jnp.int32).at[ordering].set(ranked)
    return jnp.where(usable, owners * capacity + ranks, peer_count * capacity)


def serve_rows(source, asked_rows, asked_live):
    picked = source[asked_rows]
    return jnp.where(asked_live[..., None], picked, jnp.zeros_like(picked))


def mean_of(source, answer, adjacency, degree_count):
    width = source.shape[1]
    lookup = jnp.concatenate([source, answer.reshape(-1, width)], axis=0)
    summed = jnp.dot(adjacency, lookup, preferred_element_type=jnp.float32)
    return (summed / degree_count[:, None]).astype(jnp.bfloat16)


def body(
    features,
    neighbours,
    neighbour_mask,
    layer2_position,
    self_weight1,
    neigh_weight1,
    self_weight2,
    neigh_weight2,
):
    row_count, degree = neighbours.shape
    groups = lax.axis_size("grp")
    members = lax.axis_size("dev")
    peer_count = groups * members
    own_index = lax.axis_index("grp") * members + lax.axis_index("dev")
    flat_ids = neighbours.reshape(-1)
    usable = neighbour_mask.reshape(-1) > 0
    owners = flat_ids // row_count
    local_row = flat_ids % row_count
    remote = usable & (owners != own_index)
    slots = slot_of(owners, remote, peer_count, CAP)
    request = jnp.full((peer_count * CAP + 1,), -1, jnp.int32).at[slots].set(local_row)
    request = request[:-1].reshape(groups, members, CAP)
    asked = lax.all_to_all(
        lax.all_to_all(request, "dev", split_axis=1, concat_axis=1, tiled=True),
        "grp",
        split_axis=0,
        concat_axis=0,
        tiled=True,
    )
    asked_live = asked >= 0
    asked_rows = jnp.maximum(asked, 0)
    lookup_rows = row_count + peer_count * CAP
    table_index = jnp.where(remote, row_count + slots, jnp.where(usable, local_row, 0))
    table_index = jnp.minimum(table_index, lookup_rows - 1)
    node_index = jnp.arange(row_count * degree, dtype=jnp.int32) // degree
    slot_weight = jnp.where(usable, 1.0, 0.0).astype(jnp.bfloat16)
    adjacency = (
        jnp.zeros((row_count, lookup_rows), jnp.bfloat16)
        .at[node_index, table_index]
        .add(slot_weight)
    )
    degree_count = jnp.sum(neighbour_mask, axis=1).astype(jnp.float32)
    reply_first = serve_rows(features, asked_rows, asked_live)
    answer_first = lax.all_to_all(
        lax.all_to_all(reply_first, "dev", split_axis=1, concat_axis=1, tiled=True),
        "grp",
        split_axis=0,
        concat_axis=0,
        tiled=True,
    )
    own_first = jnp.dot(features, self_weight1, preferred_element_type=jnp.float32)
    mean_first = mean_of(features, answer_first, adjacency, degree_count)
    hidden = jax.nn.relu(
        own_first + jnp.dot(mean_first, neigh_weight1, preferred_element_type=jnp.float32)
    ).astype(jnp.bfloat16)
    reply_second = serve_rows(hidden, asked_rows, asked_live)
    answer_second = lax.all_to_all(
        lax.all_to_all(reply_second, "dev", split_axis=1, concat_axis=1, tiled=True),
        "grp",
        split_axis=0,
        concat_axis=0,
        tiled=True,
    )
    own_second = jnp.dot(hidden, self_weight2, preferred_element_type=jnp.float32)
    mean_second = mean_of(hidden, answer_second, adjacency, degree_count)
    final = (
        own_second + jnp.dot(mean_second, neigh_weight2, preferred_element_type=jnp.float32)
    ).astype(jnp.bfloat16)
    width = final.shape[1]
    capacity_two = 2 * row_count // members
    target = layer2_position // row_count % members
    every_row = jnp.ones((row_count,), jnp.bool_)
    moves = slot_of(target, every_row, members, capacity_two)
    outgoing = (
        jnp.zeros((members * capacity_two + 1, width), jnp.bfloat16)
        .at[moves]
        .set(final)[:-1]
        .reshape(members, capacity_two, width)
    )
    places = (
        jnp.full((members * capacity_two + 1,), -1, jnp.int32)
        .at[moves]
        .set(layer2_position % row_count)[:-1]
        .reshape(members, capacity_two)
    )
    arrived, arrived_places = (
        lax.all_to_all(outgoing, "dev", split_axis=0, concat_axis=0, tiled=True),
        lax.all_to_all(places, "dev", split_axis=0, concat_axis=0, tiled=True),
    )
    flat_places = arrived_places.reshape(-1)
    landing = jnp.where(flat_places >= 0, flat_places, row_count)
    embeddings = (
        jnp.zeros((row_count + 1, width), jnp.bfloat16)
        .at[landing]
        .set(arrived.reshape(-1, width))[:-1]
    )
    return embeddings


def solution(mesh):
    return jax.shard_map(
        body,
        mesh=mesh,
        in_specs=(
            P(("grp", "dev"), None),
            P(("grp", "dev"), None),
            P(("grp", "dev"), None),
            P(("grp", "dev")),
            P(),
            P(),
            P(),
            P(),
        ),
        out_specs=P(("grp", "dev"), None),
        check_vma=False,
    )
```

profile of v0, /device:TPU:0, one launch (start us, length us, event | category | flops | bytes accessed | tf_op | source)
XLA Modules:
  0.0 236.5 jit_solution(16811880666225135218)
XLA Ops:
  0.0 0.9 broadcast_compare_fusion.1
  0.9 0.1 copy.30
  1.0 0.2 gt.18
  1.2 0.2 gt.17
  1.5 0.8 copy.31
  2.3 0.2 reshape.288
  2.5 0.2 reshape.287
  2.8 23.3 %scatter_custom_fusion.3 = s32[33]{0:T(128)S(1)} fusion(s32[3200]{0:T(1024)S(1)} %fusion.31, s32[3200]{0:T(1024)S(1)} %ne.122, s32[]{:T(128)} %constant.61.clone.1), kind=kCustom, calls=%fused_computation.144 | custom fusion | flops 3200 | bytes 136 | tf_op jit(solution)/shard_map/scatter-add | solution.py:13
  26.4 0.7 fusion.54
  27.2 0.7 fusion.53
  27.9 5.8 %sort.35 = (s32[3200]{0:T(1024)}, s32[3200]{0:T(1024)S(1)}) sort(s32[3200]{0:T(1024)S(1)} %fusion.33, s32[3200]{0:T(1024)S(1)} %iota.21), dimensions={0}, to_apply=%region_5.6 | sort | flops 38400 | bytes 51200 | tf_op jit(solution)/shard_map/jit(argsort)/sort | solution.py:12
  33.8 16.9 %gather_fusion.1 = s32[3200]{0:T(1024)S(1)} fusion(s32[3200]{0:T(1024)S(1)} %fusion.33, s32[4096]{0:T(1024)S(1)} %pad_clamp_fusion), kind=kCustom, calls=%fused_computation.1 | custom fusion | bytes 38400 | tf_op jit(solution)/shard_map/gather | solution.py:15
  50.7 4.5 %fusion.30 = (s32[3200]{0:T(1024)S(1)}, s32[3200,1]{0,1:T(1,128)S(1)}) fusion(s32[]{:T(128)} %bitcast.43, s32[]{:T(128)} %bitcast.44, s32[]{:T(128)} %bitcast.45, s32[]{:T(128)} %bitcast.46, s32[]{:T(128)} %bitcast.47, s32[]{:T(128)} %bitcast.49, s32[]{:T(128)} %bitcast.48, s32[3200]{0:T(1024)S(1)} %gather_fusion.1), kind=kLoop, calls=%fused_computation.102 | loop fusion | flops 48000 | bytes 38428 | tf_op jit(solution)/shard_map/gather | solution.py:15
  55.2 1.0 compare_reduce_fusion.25
  56.2 16.4 %select_subtract_fusion = s32[3200]{0:T(1024)S(1)} fusion(pred[3200]{0:T(1024)(128)(4,1)S(1)} %get-tuple-element.34, pred[3200]{0:T(1024)(128)(4,1)S(1)} %get-tuple-element.33, pred[3200]{0:T(1024)(128)(4,1)S(1)} %get-tuple-element.32, pred[3200]{0:T(1024)(128)(4,1)S(1)} %get-tuple-element.31, pred[3200]{0:T(1024)(128)(4,1)S(1)} %get-tuple-element.30, ...), kind=kLoop, calls=%fused_computation.96 | loop fusion | flops 86400 | bytes 108904 | tf_op jit(solution)/shard_map/sub | solution.py:15
  72.6 15.8 %scatter_custom_fusion.4 = s32[3200]{0:T(1024)S(1)} fusion(s32[3200]{0:T(1024)S(1)} %compare_select_fusion.11, s32[3200]{0:T(1024)S(1)} %select_subtract_fusion, s32[]{:T(128)} %constant.61.clone.1), kind=kCustom, calls=%fused_computation.109 | custom fusion | bytes 12804 | tf_op jit(solution)/shard_map/scatter | solution.py:16
  88.5 15.8 %scatter_custom_fusion.5 = s32[193]{0:T(256)S(1)} fusion(s32[3200]{0:T(1024)S(1)} %get-tuple-element.40, s32[3200]{0:T(1024)S(1)} %get-tuple-element.41, s32[]{:T(128)} %constant.59.clone.1), kind=kCustom, calls=%fused_computation.142 | custom fusion | bytes 776 | tf_op jit(solution)/shard_map/scatter | solution.py:53
  104.5 0.6 copy.35
  105.1 6.4 %all-to-all-start.1 = ((s32[4,8,6]{2,0,1:T(4,128)}), s32[4,8,6]{2,0,1:T(4,128)S(1)}, u32[]{:S(2)}, u32[]{:S(2)}) async-start(s32[4,8,6]{2,0,1:T(4,128)} %copy.35), calls=%async_computation.1 | async-start | bytes 32768 | tf_op jit(solution)/shard_map/all_to_all | solution.py:56
  111.5 2.6 %sort.34 = (s32[128]{0:T(128)}, s32[128]{0:T(128)S(1)}) sort(s32[128]{0:T(128)S(1)} %get-tuple-element.38, s32[128]{0:T(128)S(1)} %iota.18), dimensions={0}, to_apply=%region_0.1 | sort | flops 896 | bytes 2048 | tf_op jit(solution)/shard_map/jit(argsort)/sort | solution.py:12
  114.3 2.8 %all-to-all-done.1 = s32[4,8,6]{2,0,1:T(4,128)S(1)} async-done(((s32[4,8,6]{2,0,1:T(4,128)}), s32[4,8,6]{2,0,1:T(4,128)S(1)}, u32[]{:S(2)}, u32[]{:S(2)}) %all-to-all-start.1) | async-done | bytes 800 | tf_op jit(solution)/shard_map/all_to_all | solution.py:56
  117.1 0.6 copy.36
  117.7 3.7 %all-to-all-start.2 = ((s32[4,8,6]{2,1,0:T(8,128)}), s32[4,8,6]{2,1,0:T(8,128)S(1)}, u32[]{:S(2)}, u32[]{:S(2)}) async-start(s32[4,8,6]{2,1,0:T(8,128)} %copy.36), calls=%async_computation.2 | async-start | bytes 32768 | tf_op jit(solution)/shard_map/all_to_all | solution.py:55
  121.5 1.4 scatter_custom_fusion
  122.9 0.2 reduce-window.18
  123.1 1.2 gather_fusion
  124.3 1.8 all-to-all-done.2
  126.3 1.0 gather_fusion.2
  127.6 0.9 copy.37
  128.5 3.6 %all-to-all-start.3 = ((bf16[4,8,6,768]{3,0,2,1:T(4,128)(2,1)}), bf16[4,8,6,768]{3,0,2,1:T(4,128)(2,1)S(1)}, u32[]{:S(2)}, u32[]{:S(2)}) async-start(bf16[4,8,6,768]{3,0,2,1:T(4,128)(2,1)} %copy.37), calls=%async_computation.3 | async-start | bytes 589824 | tf_op jit(solution)/shard_map/all_to_all | solution.py:77
  132.2 29.3 %scatter_custom_fusion.8 = bf16[40960]{0:T(1024)(128)(2,1)} fusion(s32[3200]{0:T(1024)S(1)} %broadcast_select_fusion.2, bf16[3200]{0:T(1024)(128)(2,1)S(1)} %select_convert_fusion, bf16[]{:T(256)} %constant.56.clone.1), kind=kCustom, calls=%fused_computation.80 | custom fusion | flops 3200 | bytes 81922
  161.6 0.8 copy.38
  162.4 3.5 %all-to-all-start.4 = ((bf16[4,8,6,768]{3,1,2,0:T(8,128)(2,1)}), bf16[4,8,6,768]{3,1,2,0:T(8,128)(2,1)S(1)}, u32[]{:S(2)}, u32[]{:S(2)}) async-start(bf16[4,8,6,768]{3,1,2,0:T(8,128)(2,1)} %copy.38), calls=%async_computation.4 | async-start | bytes 589824 | tf_op jit(solution)/shard_map/all_to_all | solution.py:76
  165.8 1.8 fusion.56
  167.6 4.4 %all-to-all-done.4 = bf16[4,8,6,768]{3,1,2,0:T(8,128)(2,1)S(1)} async-done(((bf16[4,8,6,768]{3,1,2,0:T(8,128)(2,1)}), bf16[4,8,6,768]{3,1,2,0:T(8,128)(2,1)S(1)}, u32[]{:S(2)}, u32[]{:S(2)}) %all-to-all-start.4) | async-done | bytes 294944 | tf_op jit(solution)/shard_map/all_to_all | solution.py:76
  172.1 0.8 reshape.292
  172.9 2.1 fusion.2
  175.0 1.0 gather_fusion.3
  176.1 0.1 reshape.381
  176.3 1.0 copy.40
  177.4 4.8 %all-to-all-start.5 = ((bf16[4,8,6,1024]{3,0,2,1:T(4,128)(2,1)}), bf16[4,8,6,1024]{3,0,2,1:T(4,128)(2,1)S(1)}, u32[]{:S(2)}, u32[]{:S(2)}) async-start(bf16[4,8,6,1024]{3,0,2,1:T(4,128)(2,1)} %copy.40), calls=%async_computation.5 | async-start | bytes 786432 | tf_op jit(solution)/shard_map/all_to_all | solution.py:90
  182.2 0.7 fusion.55
  182.9 5.8 %fusion.39 = s32[128]{0:T(128)S(1)} fusion(s32[128]{0:T(128)S(1)} %gather_fusion, s32[]{:T(128)} %bitcast.7, s32[]{:T(128)} %bitcast.8, s32[]{:T(128)} %bitcast.9, s32[]{:T(128)} %bitcast.10, s32[]{:T(128)} %bitcast.11, s32[]{:T(128)} %bitcast.13, s32[]{:T(128)} %bitcast.12, s32[]{:T(128)} %bitcast.4, s32[]{:T(128)} %bitcast.6), kind=kLoop, calls=%fused_computation.139 | loop fusion | flops 2560 | bytes 1060 | tf_op jit(solution)/shard_map/sub | solution.py:15
  188.7 1.0 scatter_custom_fusion.1
  189.7 1.0 scatter_custom_fusion.2
  190.6 0.7 all_to_all.27
  191.3 3.4 %all-to-all-done.5 = bf16[4,8,6,1024]{3,0,2,1:T(4,128)(2,1)S(1)} async-done(((bf16[4,8,6,1024]{3,0,2,1:T(4,128)(2,1)}), bf16[4,8,6,1024]{3,0,2,1:T(4,128)(2,1)S(1)}, u32[]{:S(2)}, u32[]{:S(2)}) %all-to-all-start.5) | async-done | bytes 393248 | tf_op jit(solution)/shard_map/all_to_all | solution.py:90
  194.7 1.0 copy.41
  195.6 3.5 %all-to-all-start.6 = ((bf16[4,8,6,1024]{3,1,2,0:T(8,128)(2,1)}), bf16[4,8,6,1024]{3,1,2,0:T(8,128)(2,1)S(1)}, u32[]{:S(2)}, u32[]{:S(2)}) async-start(bf16[4,8,6,1024]{3,1,2,0:T(8,128)(2,1)} %copy.41), calls=%async_computation.6 | async-start | bytes 786432 | tf_op jit(solution)/shard_map/all_to_all | solution.py:89
  199.1 1.2 fusion.57
  200.4 5.0 %all-to-all-done.6 = bf16[4,8,6,1024]{3,1,2,0:T(8,128)(2,1)S(1)} async-done(((bf16[4,8,6,1024]{3,1,2,0:T(8,128)(2,1)}), bf16[4,8,6,1024]{3,1,2,0:T(8,128)(2,1)S(1)}, u32[]{:S(2)}, u32[]{:S(2)}) %all-to-all-start.6) | async-done | bytes 393248 | tf_op jit(solution)/shard_map/all_to_all | solution.py:89
  205.4 3.4 %all-to-all-start = ((s32[8,1,32]{2,1,0:T(1,128)}), s32[8,1,32]{2,1,0:T(1,128)S(1)}, u32[]{:S(2)}, u32[]{:S(2)}) async-start(s32[8,1,32]{2,1,0:T(1,128)} %all_to_all.27), calls=%async_computation | async-start | bytes 8192 | tf_op jit(solution)/shard_map/all_to_all | solution.py:120
  208.8 0.2 copy.42
  209.0 0.1 reshape.293
  209.1 2.4 fusion.3
  211.5 1.3 scatter_custom_fusion.6
  212.8 0.8 slice.68
  213.6 0.7 all-to-all-done
  214.3 4.4 %all-to-all-start.7 = ((bf16[8,32,1024]{2,1,0:T(8,128)(2,1)}), bf16[8,32,1024]{2,1,0:T(8,128)(2,1)S(1)}, u32[]{:S(2)}, u32[]{:S(2)}) async-start(bf16[8,32,1024]{2,1,0:T(8,128)(2,1)} %bitcast.51), calls=%async_computation.7 | async-start | bytes 1048576 | tf_op jit(solution)/shard_map/all_to_all | solution.py:119
  218.8 0.5 broadcast.653
  219.3 0.7 reduce.64
  220.0 14.1 %all-to-all-done.7 = bf16[8,32,1024]{2,1,0:T(8,128)(2,1)S(1)} async-done(((bf16[8,32,1024]{2,1,0:T(8,128)(2,1)}), bf16[8,32,1024]{2,1,0:T(8,128)(2,1)S(1)}, u32[]{:S(2)}, u32[]{:S(2)}) %all-to-all-start.7) | async-done | bytes 524320 | tf_op jit(solution)/shard_map/all_to_all | solution.py:119
  234.1 1.7 scatter_custom_fusion.7
  235.8 0.7 slice.69
  (53 shorter events, 1.6 us)
Async XLA Ops:
  0.0 199.1 %copy-start = (bf16[1024,1024]{1,0:T(8,128)(2,1)S(1)}, bf16[1024,1024]{1,0:T(8,128)(2,1)}, u32[]{:S(2)}) copy-start(bf16[1024,1024]{1,0:T(8,128)(2,1)} %param.14) | copy-start | bytes 6291460
  33.7 77.8 %copy-start.6 = (s32[128]{0:T(128)S(1)}, s32[128]{0:T(128)}, u32[]{:S(2)}) copy-start(s32[128]{0:T(128)} %param.11) | copy-start | bytes 1540
  33.7 80.4 %copy-start.5 = (s32[2]{0:T(128)S(1)}, s32[2]{0:T(128)}, u32[]{:S(2)}) copy-start(s32[2]{0:T(128)} %constant.130) | copy-start | bytes 28
  33.7 87.7 %copy-start.3 = (s32[128,25]{0,1:T(8,128)S(1)}, s32[128,25]{0,1:T(8,128)}, u32[]{:S(2)}) copy-start(s32[128,25]{0,1:T(8,128)} %param.10) | copy-start | bytes 38404
  50.7 75.6 %copy-start.1 = (bf16[128,768]{1,0:T(8,128)(2,1)S(1)}, bf16[128,768]{1,0:T(8,128)(2,1)}, u32[]{:S(2)}) copy-start(bf16[128,768]{1,0:T(8,128)(2,1)} %param.8) | copy-start | bytes 589828
  105.1 12.0 %all-to-all-start.1 = ((s32[4,8,6]{2,0,1:T(4,128)}), s32[4,8,6]{2,0,1:T(4,128)S(1)}, u32[]{:S(2)}, u32[]{:S(2)}) async-start(s32[4,8,6]{2,0,1:T(4,128)} %copy.35), calls=%async_computation.1 | async-start | bytes 32768 | tf_op jit(solution)/shard_map/all_to_all | solution.py:56
  117.7 8.4 %all-to-all-start.2 = ((s32[4,8,6]{2,1,0:T(8,128)}), s32[4,8,6]{2,1,0:T(8,128)S(1)}, u32[]{:S(2)}, u32[]{:S(2)}) async-start(s32[4,8,6]{2,1,0:T(8,128)} %copy.36), calls=%async_computation.2 | async-start | bytes 32768 | tf_op jit(solution)/shard_map/all_to_all | solution.py:55
  127.3 4.8 %copy-start.4 = (s32[2]{0:T(128)S(1)}, s32[2]{0:T(128)}, u32[]{:S(2)}) copy-start(s32[2]{0:T(128)} %constant.127) | copy-start | bytes 28
  128.5 33.1 %all-to-all-start.3 = ((bf16[4,8,6,768]{3,0,2,1:T(4,128)(2,1)}), bf16[4,8,6,768]{3,0,2,1:T(4,128)(2,1)S(1)}, u32[]{:S(2)}, u32[]{:S(2)}) async-start(bf16[4,8,6,768]{3,0,2,1:T(4,128)(2,1)} %copy.37), calls=%async_computation.3 | async-start | bytes 589824 | tf_op jit(solution)/shard_map/all_to_all | solution.py:77
  162.4 9.7 %all-to-all-start.4 = ((bf16[4,8,6,768]{3,1,2,0:T(8,128)(2,1)}), bf16[4,8,6,768]{3,1,2,0:T(8,128)(2,1)S(1)}, u32[]{:S(2)}, u32[]{:S(2)}) async-start(bf16[4,8,6,768]{3,1,2,0:T(8,128)(2,1)} %copy.38), calls=%async_computation.4 | async-start | bytes 589824 | tf_op jit(solution)/shard_map/all_to_all | solution.py:76
  177.4 17.3 %all-to-all-start.5 = ((bf16[4,8,6,1024]{3,0,2,1:T(4,128)(2,1)}), bf16[4,8,6,1024]{3,0,2,1:T(4,128)(2,1)S(1)}, u32[]{:S(2)}, u32[]{:S(2)}) async-start(bf16[4,8,6,1024]{3,0,2,1:T(4,128)(2,1)} %copy.40), calls=%async_computation.5 | async-start | bytes 786432 | tf_op jit(solution)/shard_map/all_to_all | solution.py:90
  195.6 9.7 %all-to-all-start.6 = ((bf16[4,8,6,1024]{3,1,2,0:T(8,128)(2,1)}), bf16[4,8,6,1024]{3,1,2,0:T(8,128)(2,1)S(1)}, u32[]{:S(2)}, u32[]{:S(2)}) async-start(bf16[4,8,6,1024]{3,1,2,0:T(8,128)(2,1)} %copy.41), calls=%async_computation.6 | async-start | bytes 786432 | tf_op jit(solution)/shard_map/all_to_all | solution.py:89
  200.4 8.8 %copy-start.2 = (bf16[40960]{0:T(1024)(128)(2,1)S(1)}, bf16[40960]{0:T(1024)(128)(2,1)}, u32[]{:S(2)}) copy-start(bf16[40960]{0:T(1024)(128)(2,1)} %scatter_custom_fusion.8) | copy-start | bytes 245764
  205.4 9.0 %all-to-all-start = ((s32[8,1,32]{2,1,0:T(1,128)}), s32[8,1,32]{2,1,0:T(1,128)S(1)}, u32[]{:S(2)}, u32[]{:S(2)}) async-start(s32[8,1,32]{2,1,0:T(1,128)} %all_to_all.27), calls=%async_computation | async-start | bytes 8192 | tf_op jit(solution)/shard_map/all_to_all | solution.py:120
  214.3 19.7 %all-to-all-start.7 = ((bf16[8,32,1024]{2,1,0:T(8,128)(2,1)}), bf16[8,32,1024]{2,1,0:T(8,128)(2,1)S(1)}, u32[]{:S(2)}, u32[]{:S(2)}) async-start(bf16[8,32,1024]{2,1,0:T(8,128)(2,1)} %bitcast.51), calls=%async_computation.7 | async-start | bytes 1048576 | tf_op jit(solution)/shard_map/all_to_all | solution.py:119
where the time goes:
time: 238 us; the launch traced here: 236 us
  other arithmetic  92.8 us (39%)
  local copies, waits for them, and re-layouts  70.4 us (30%)
  starting transfers between devices  33.1 us (14%)
  waiting for transfers between devices  32.2 us (14%)
  matrix products  7.52 us (3%)
    unnamed x4, other arithmetic  29.6 us
    scatter-add x2, other arithmetic, slot_of(): per_owner = jnp.zeros((peer_count + 1,), jnp.int32).at[sort_key].add(1)  24.7 us
    sub x2, other arithmetic, slot_of(): jnp.arange(item_count, dtype=jnp.int32) - starts[sort_key[ordering]]  22.2 us
    gather x2, local copies, waits for them, and re-layouts, slot_of(): sort_key[ordering]  18.2 us
    scatter x2, local copies, waits for them, and re-layouts, slot_of(): ranks = jnp.zeros((item_count,), jnp.int32).at[ordering].set(ranked)  16.8 us
    scatter x1, local copies, waits for them, and re-layouts, body(): jnp.full((peer_count * CAP + 1,), -1, jnp.int32).at[slots].set(local_row)  15.8 us
    all_to_all x1, waiting for transfers between devices, body(): lax.all_to_all(outgoing, 'dev', split_axis=0, concat_axis=0, tiled=True)  14.1 us
    sort x2, other arithmetic, slot_of(): ordering = jnp.argsort(sort_key, stable=True)  8.39 us
  transfers between devices with their start and end apart: 8, of which 7 were waited for; matrix products, arithmetic and copies ran while one was open for 22% of the time, Pallas kernels for 0%

commit v1 on v0

v1 whole, which is shorter than its diff:
```python
import functools

import jax
import jax.numpy as jnp
from jax import lax
from jax.experimental import pallas as pl
from jax.experimental.pallas import tpu as pltpu
from jax.sharding import PartitionSpec as P

CAP = 6
BOTH = ("grp", "dev")
F32 = jnp.float32
BF16 = jnp.bfloat16
I32 = jnp.int32


def divide(values, by):
    if by & (by - 1) == 0:
        return values >> (by.bit_length() - 1)
    return (values * (-(-(1 << 16) // by))) >> 16


def iota(shape, dim):
    return lax.broadcasted_iota(I32, shape, dim)


def bits(condition):
    return jnp.where(condition, 1.0, 0.0)


def earlier(count):
    return bits(iota((count, count), 0) < iota((count, count), 1)).astype(BF16)


def dot(left, right):
    return jnp.dot(left, right, preferred_element_type=F32)


def dot_lanes(left, right):
    return lax.dot_general(left, right, (((1,), (1,)), ((), ())), preferred_element_type=F32)


def whole(n):
    return [pl.BlockSpec(memory_space=pltpu.VMEM)] * n


def call(kernel, outs, operands, flops, name, limit=24 << 20):
    moved = sum(a.size * a.dtype.itemsize for a in (*operands, *outs))
    return pl.pallas_call(
        kernel,
        out_shape=outs,
        in_specs=whole(len(operands)),
        out_specs=whole(len(outs)) if isinstance(outs, (list, tuple)) else whole(1)[0],
        compiler_params=pltpu.CompilerParams(vmem_limit_bytes=limit),
        cost_estimate=pl.CostEstimate(flops=flops, bytes_accessed=moved, transcendentals=0),
        name=name,
    )(*operands)


def ask_kernel(members, peers, ids_ref, mask_ref, pos_ref, ask_ref, key_ref, local_ref, span_ref, wide):
    rows, degree = ids_ref.shape
    own = lax.axis_index("grp") * members + lax.axis_index("dev")
    wide[...] = jnp.zeros_like(wide)
    wide[:, :degree] = jnp.where(mask_ref[...] > 0, ids_ref[...], -1)
    slots = wide[...].T
    owner = divide(slots, rows)
    row = slots - owner * rows
    live = slots >= 0
    here = owner == own
    key = jnp.where(live & jnp.logical_not(here), owner, -1)
    peer = iota((peers, rows), 0)
    total = jnp.zeros((peers, rows), I32)
    for s in range(degree):
        total += jnp.where(key[s : s + 1] == peer, 1, 0)
    before = dot(total.astype(F32).astype(BF16), earlier(rows)).astype(I32)
    width = (rows - 1).bit_length()
    per_word = 30 // width if width <= 10 else 1
    per_word = min(per_word, CAP, 24 // width)
    words = -(-CAP // per_word)
    packed = [jnp.zeros((peers, rows), I32) for _ in range(words)]
    running = before
    for s in range(degree):
        hit = key[s : s + 1] == peer
        for w in range(words):
            shift = running - w * per_word
            fits = hit & (shift >= 0) & (shift < per_word)
            packed[w] += jnp.where(fits, row[s : s + 1] << (jnp.clip(shift, 0, per_word - 1) * width), 0)
        running += jnp.where(hit, 1, 0)
    lane = iota((peers, rows), 1)
    wanted = jnp.zeros((peers, rows), I32)
    for w in range(words):
        word = jnp.sum(packed[w].astype(F32), axis=1, keepdims=True).astype(I32)
        slot = lane - w * per_word
        mine = (slot >= 0) & (slot < per_word) & (lane < CAP)
        word = jnp.broadcast_to(word, (peers, rows))
        wanted += jnp.where(mine, (word >> (jnp.clip(slot, 0, per_word - 1) * width)) & ((1 << width) - 1), 0)
    pos = pos_ref[...]
    place = jnp.where(divide(pos, rows) == peer, (pos & (rows - 1)) + 1, 0) if rows & (rows - 1) == 0 else jnp.where(
        divide(pos, rows) == peer, pos - divide(pos, rows) * rows + 1, 0
    )
    ask_ref[...] = (place + wanted * (2 * rows)).reshape(peers, 1, rows)
    key_ref[...] = key
    local_ref[...] = jnp.where(live & here, row, -1)
    span_ref[0] = before
    span_ref[1] = total


def plan_kernel(
    members, peers, degree, key_ref, local_ref, span_ref, mask_ref, pos_ref, features_ref, weight_ref,
    near_ref, far_ref, near_moved_ref, far_moved_ref, move_ref, order_ref, count_ref, sum_ref, own_ref,
):
    rows = features_ref.shape[0]
    capacity = 2 * rows // members
    local = local_ref[...]
    node = iota((rows, rows), 0)
    near = jnp.zeros((rows, rows), F32)
    for s in range(degree):
        near += bits(local[s : s + 1] == node)
    near = near.T.astype(BF16)
    near_ref[...] = near
    before, total = span_ref[0], span_ref[1]
    far = [bits((before <= k) & (k < before + total)).astype(BF16) for k in range(CAP)]
    far = jnp.concatenate(far, axis=0)
    size = peers * CAP
    line = iota((size, size), 0)
    peer = divide(line, CAP)
    order = bits(iota((size, size), 1) == (line - peer * CAP) * peers + peer).astype(BF16)
    order_ref[...] = order
    far = dot(order, far).T.astype(BF16)
    far_ref[...] = far
    pos = pos_ref[...]
    owner = divide(pos, rows)
    member = owner - lax.axis_index("grp") * members
    line = iota((rows, rows), 0)
    step = divide(line, capacity)
    target = lax.axis_index("dev") + 2 * step
    target = jnp.where(target >= members, target - members, target)
    goes = target == member
    place = dot(bits(goes).astype(BF16), earlier(rows))
    move = bits(goes & (place.astype(I32) == line - step * capacity)).astype(BF16)
    move_ref[...] = move
    near_moved_ref[...] = dot(move, near).astype(BF16)
    far_moved_ref[...] = dot(move, far).astype(BF16)
    count = jnp.sum(mask_ref[...].astype(F32), axis=1, keepdims=True)
    count_ref[0] = jnp.broadcast_to(count, (rows, 128))
    moved = dot(move, jnp.broadcast_to(count, (rows, 128)).astype(BF16))
    count_ref[1] = moved
    features = features_ref[...]
    sum_ref[...] = dot(near, features)
    own_ref[...] = dot(features, weight_ref[...])


def store_rows(reply_ref, rows):
    peers, pairs, two, width = reply_ref.shape
    reply_ref[...] = rows.reshape(peers, pairs, two, width)


def serve_kernel(asked_ref, order_ref, source_ref, reply_ref, pick_ref):
    peers, _, rows = asked_ref.shape
    asked = asked_ref[...].reshape(peers, rows)
    wanted = divide(asked, 2 * rows)
    lane = iota((peers, rows), 1)
    picks = [bits(wanted[:, k : k + 1] == lane).astype(BF16) for k in range(CAP)]
    pick = dot(order_ref[...], jnp.concatenate(picks, axis=0)).astype(BF16)
    pick_ref[...] = pick
    store_rows(reply_ref, dot(pick, source_ref[...]).astype(BF16))


def place_kernel(members, asked_ref, place_ref):
    _, _, rows = asked_ref.shape
    capacity = 2 * rows // members
    me = lax.axis_index("dev")
    first = lax.axis_index("grp") * members
    line = iota((rows, rows), 0)
    step = divide(line, capacity)
    result = jnp.zeros((rows, rows), F32)
    before = earlier(rows)
    for q in range(members // 2):
        source = me - 2 * q
        source = first + jnp.where(source < 0, source + members, source)
        sent = asked_ref[source] & (2 * rows - 1)
        valid = jnp.broadcast_to(sent > 0, (rows, rows))
        rank = dot(bits(valid).astype(BF16), before).astype(I32)
        lands = bits(sent - 1 == line).astype(BF16)
        comes = bits(valid & (step == q) & (rank == line - step * capacity)).astype(BF16)
        result += dot_lanes(lands, comes)
    place_ref[...] = result.astype(BF16)


def layer_one_kernel(answer_ref, far_ref, sum_ref, own_ref, count_ref, weight_ref, pick_ref, hidden_ref, reply_ref):
    peers, pairs, two, width = answer_ref.shape
    answer = answer_ref[...].reshape(peers * pairs * two, width)
    summed = sum_ref[...] + dot(far_ref[...], answer)
    mean = (summed / count_ref[0][:, :1]).astype(BF16)
    hidden = jnp.maximum(own_ref[...] + dot(mean, weight_ref[...]), 0.0).astype(BF16)
    hidden_ref[...] = hidden
    store_rows(reply_ref, dot(pick_ref[...], hidden).astype(BF16))


def own_two_kernel(hidden_ref, near_ref, move_ref, weight_ref, sum_ref, own_ref):
    hidden = hidden_ref[...]
    sum_ref[...] = dot(near_ref[...], hidden)
    own_ref[...] = dot(dot(move_ref[...], hidden).astype(BF16), weight_ref[...])


def layer_two_kernel(answer_ref, far_ref, sum_ref, own_ref, count_ref, weight_ref, *final_refs):
    peers, pairs, two, width = answer_ref.shape
    answer = answer_ref[...].reshape(peers * pairs * two, width)
    summed = sum_ref[...] + dot(far_ref[...], answer)
    mean = (summed / count_ref[1][:, :1]).astype(BF16)
    final = (own_ref[...] + dot(mean, weight_ref[...])).astype(BF16)
    capacity = final_refs[0].shape[0]
    for q, ref in enumerate(final_refs):
        ref[...] = final[q * capacity : (q + 1) * capacity]


def scatter_kernel(place_ref, *refs):
    out_ref = refs[-1]
    arrived = jnp.concatenate([ref[...] for ref in refs[:-1]], axis=0)
    out_ref[...] = dot(place_ref[...], arrived).astype(BF16)


def body(features, neighbours, neighbour_mask, layer2_position, self_weight1, neigh_weight1, self_weight2, neigh_weight2):
    rows, degree = neighbours.shape
    members = lax.axis_size("dev")
    peers = lax.axis_size("grp") * members
    width_in, width = self_weight1.shape
    steps = members // 2
    capacity = rows // steps
    size = peers * CAP
    shape = jax.ShapeDtypeStruct
    pos = layer2_position.reshape(1, rows)

    ask, key, local, span = pl.pallas_call(
        functools.partial(ask_kernel, members, peers),
        out_shape=(
            shape((peers, 1, rows), I32),
            shape((rows, rows), I32),
            shape((rows, rows), I32),
            shape((2, peers, rows), I32),
        ),
        in_specs=whole(3),
        out_specs=whole(4),
        scratch_shapes=[pltpu.VMEM((rows, rows), I32)],
        compiler_params=pltpu.CompilerParams(vmem_limit_bytes=16 << 20),
        name="ask",
    )(neighbours, neighbour_mask, pos)
    asked = lax.all_to_all(ask, BOTH, 0, 0, tiled=True)
    near, far, near_moved, far_moved, move, order, count, sum_one, own_one = call(
        functools.partial(plan_kernel, members, peers, degree),
        (
            shape((rows, rows), BF16),
            shape((rows, size), BF16),
            shape((rows, rows), BF16),
            shape((rows, size), BF16),
            shape((rows, rows), BF16),
            shape((size, size), BF16),
            shape((2, rows, 128), F32),
            shape((rows, width_in), F32),
            shape((rows, width), F32),
        ),
        (key, local, span, neighbour_mask, pos, features, self_weight1),
        2 * rows * width_in * (rows + width),
        "plan",
        limit=40 << 20,
    )
    reply, pick = call(
        serve_kernel,
        (shape((peers, CAP // 2, 2, width_in), BF16), shape((size, rows), BF16)),
        (asked, order, features),
        2 * size * rows * width_in,
        "serve",
    )
    answer = lax.all_to_all(reply, BOTH, 0, 0, tiled=True)
    place = pl.pallas_call(
        functools.partial(place_kernel, members),
        out_shape=shape((rows, rows), BF16),
        in_specs=whole(1),
        out_specs=whole(1)[0],
        compiler_params=pltpu.CompilerParams(vmem_limit_bytes=16 << 20),
        cost_estimate=pl.CostEstimate(flops=4 * steps * rows**3, bytes_accessed=4 * peers * rows, transcendentals=0),
        name="place",
    )(asked)
    hidden, reply_two = call(
        layer_one_kernel,
        (shape((rows, width), BF16), shape((peers, CAP // 2, 2, width), BF16)),
        (answer, far, sum_one, own_one, count, neigh_weight1, pick),
        2 * rows * width_in * (size + width) + 2 * size * rows * width,
        "layer_one",
    )
    answer_two = lax.all_to_all(reply_two, BOTH, 0, 0, tiled=True)
    sum_two, own_two = call(
        own_two_kernel,
        (shape((rows, width), F32), shape((rows, width), F32)),
        (hidden, near_moved, move, self_weight2),
        2 * rows * width * (2 * rows + width),
        "own_two",
    )
    finals = call(
        layer_two_kernel,
        tuple(shape((capacity, width), BF16) for _ in range(steps)),
        (answer_two, far_moved, sum_two, own_two, count, neigh_weight2),
        2 * rows * width * (size + width),
        "layer_two",
    )
    arrived = [finals[0]]
    for q in range(1, steps):
        arrived.append(lax.ppermute(finals[q], "dev", [(i, (i + 2 * q) % members) for i in range(members)]))
    return pl.pallas_call(
        scatter_kernel,
        out_shape=shape((rows, width), BF16),
        in_specs=whole(1 + steps),
        out_specs=whole(1)[0],
        compiler_params=pltpu.CompilerParams(vmem_limit_bytes=16 << 20),
        cost_estimate=pl.CostEstimate(flops=2 * rows * rows * width, bytes_accessed=4 * rows * width, transcendentals=0),
        name="scatter",
    )(place, *arrived)


def solution(mesh):
    return jax.shard_map(
        body,
        mesh=mesh,
        in_specs=(
            P(BOTH, None),
            P(BOTH, None),
            P(BOTH, None),
            P(BOTH),
            P(),
            P(),
            P(),
            P(),
        ),
        out_specs=P(BOTH, None),
        check_vma=False,
    )
```

time: 238 us -> 65.6 us (0.28)
  other arithmetic: 92.8 us -> 0 us
  local copies, waits for them, and re-layouts: 70.4 us -> 13.7 us
  starting transfers between devices: 33.1 us -> 13.9 us
  waiting for transfers between devices: 32.2 us -> 14 us
  blocking collectives: 0 us -> 15.9 us
  matrix products: 7.52 us -> 0 us
  Pallas kernels: 0 us -> 7.38 us
    scatter x6 -> x0, local copies, waits for them, and re-layouts: 36.6 us -> none  [the longest x2 16.8 us: slot_of(): ranks = jnp.zeros((item_count,), jnp.int32).at[ordering].set(ranked)]
    unnamed x4 -> x0, other arithmetic: 29.6 us -> none
    scatter-add x2 -> x0, other arithmetic: 24.7 us -> none  [slot_of(): per_owner = jnp.zeros((peer_count + 1,), jnp.int32).at[sort_key].add(1)]
    all_to_all x8 -> x2, starting transfers between devices: 33.1 us -> 10.1 us  [the longest x1 7.33 us: body(): asked = lax.all_to_all(ask, BOTH, 0, 0, tiled=True)]
    gather x9 -> x0, local copies, waits for them, and re-layouts: 22.6 us -> none  [the longest x2 18.2 us: slot_of(): sort_key[ordering]]
    all_to_all x8 -> x2, waiting for transfers between devices: 32.2 us -> 9.76 us  [the longest x1 8.72 us: body(): answer_two = lax.all_to_all(reply_two, BOTH, 0, 0, tiled=True)]
    sub x4 -> x0, other arithmetic: 22.2 us -> none  [the longest x2 22.2 us: slot_of(): jnp.arange(item_count, dtype=jnp.int32) - starts[sort_key[ordering]]]
    all_to_all x0 -> x1, blocking collectives: none -> 15.9 us  [body(): answer = lax.all_to_all(reply, BOTH, 0, 0, tiled=True)]
  transfers between devices with their start and end apart: 8 -> 5, of which waited for: 7 -> 4; matrix products, arithmetic and copies ran while one was open for 22% -> 0% of each run, Pallas kernels for 0% -> 4%
where the time goes in v1:
time: 65.6 us; the launch traced here: 65 us
  blocking collectives  15.9 us (24%)
  waiting for transfers between devices  14 us (21%)
  starting transfers between devices  13.9 us (21%)
  local copies, waits for them, and re-layouts  13.7 us (21%)
  Pallas kernels  7.38 us (11%)
    all_to_all x1, blocking collectives, body(): answer = lax.all_to_all(reply, BOTH, 0, 0, tiled=True)  15.9 us
    unnamed x38, local copies, waits for them, and re-layouts  13.7 us
    all_to_all x1, waiting for transfers between devices, body(): answer_two = lax.all_to_all(reply_two, BOTH, 0, 0, tiled=True)  8.72 us
    all_to_all x1, starting transfers between devices, body(): asked = lax.all_to_all(ask, BOTH, 0, 0, tiled=True)  7.33 us
    pallas_call x5, Pallas kernels, call(): pl.pallas_call(kernel, out_shape=outs, in_specs=whole(len(operands)), out...  4.61 us
    ppermute x3, waiting for transfers between devices, body(): lax.ppermute(finals[q], 'dev', [(i, (i + 2 * q) % members) for i in range...  4.26 us
    ppermute x3, starting transfers between devices, body(): lax.ppermute(finals[q], 'dev', [(i, (i + 2 * q) % members) for i in range...  3.87 us
    all_to_all x1, starting transfers between devices, body(): answer_two = lax.all_to_all(reply_two, BOTH, 0, 0, tiled=True)  2.73 us
  transfers between devices with their start and end apart: 5, of which 4 were waited for; matrix products, arithmetic and copies ran while one was open for 0% of the time, Pallas kernels for 4%

profile of v1, /device:TPU:0, one launch (start us, length us, event | category | flops | bytes accessed | tf_op | source)
XLA Modules:
  0.0 65.0 jit_solution(13163143582946870199)
XLA Ops:
  0.0 0.0 copy-start.5
  0.0 0.9 %copy.10.mask_ref = s32[128,25]{1,0:T(8,128)S(1)} copy(s32[128,25]{0,1:T(8,128)} %param.10) | data formatting | bytes 25600 | tf_op args[2]
  0.9 0.8 %copy.9.ids_ref = s32[128,25]{1,0:T(8,128)S(1)} copy(s32[128,25]{0,1:T(8,128)} %param.9) | data formatting | bytes 25600 | tf_op args[1]
  1.7 0.0 copy-start.16
  1.7 0.6 copy-done.16
  2.3 1.3 %ask.1 = (s32[32,1,128]{2,1,0:T(1,128)}, s32[128,128]{1,0:T(8,128)S(1)}, s32[128,128]{1,0:T(8,128)S(1)}, s32[2,32,128]{2,1,0:T(8,128)S(1)}) custom-call(s32[128,25]{1,0:T(8,128)S(1)} %copy.9.ids_ref, s32[128,25]{1,0:T(8,128)S(1)} %copy.10.mask_ref, s32[1,128]{1,0:T(1,128)S(1)} %bitcast.1), custom_call_target="tpu_custom_call" | custom-call | tf_op jit(solution)/shard_map/ask/pallas_call | solution.py:234
  3.7 7.3 %all-to-all-start = ((s32[32,1,128]{2,1,0:T(1,128)}), s32[32,1,128]{2,1,0:T(1,128)S(1)}, u32[]{:S(2)}, u32[]{:S(2)}) async-start(s32[32,1,128]{2,1,0:T(1,128)} %get-tuple-element.27), calls=%async_computation | async-start | bytes 32768 | tf_op jit(solution)/shard_map/all_to_all | solution.py:248
  11.0 0.0 copy-start.2
  11.0 1.4 %copy-done.2 = bf16[768,1024]{1,0:T(8,128)(2,1)S(1)} copy-done((bf16[768,1024]{1,0:T(8,128)(2,1)S(1)}, bf16[768,1024]{1,0:T(8,128)(2,1)}, u32[]{:S(2)}) %copy-start.2) | copy-done | bytes 1572888
  12.4 0.0 copy-start.4
  12.4 0.9 %copy-done.4 = bf16[128,768]{1,0:T(8,128)(2,1)S(1)} copy-done((bf16[128,768]{1,0:T(8,128)(2,1)S(1)}, bf16[128,768]{1,0:T(8,128)(2,1)}, u32[]{:S(2)}) %copy-start.4) | copy-done | bytes 196632
  13.3 0.0 copy-start.17
  13.3 0.7 %copy-done.17 = s32[128]{0:T(128)S(1)} copy-done((s32[128]{0:T(128)S(1)}, s32[128]{0:T(128)}, u32[]{:S(2)}) %copy-start.17) | copy-done | bytes 536
  14.0 0.0 copy-start.3
  14.0 1.3 %plan.1 = (bf16[128,128]{1,0:T(8,128)(2,1)}, bf16[128,192]{1,0:T(8,128)(2,1)S(1)}, bf16[128,128]{1,0:T(8,128)(2,1)S(1)}, bf16[128,192]{1,0:T(8,128)(2,1)S(1)}, b...) custom-call(s32[128,128]{1,0:T(8,128)S(1)} %get-tuple-element.28.key, ...), custom_call_target="tpu_custom_call" | custom-call | flops 226492416 | bytes 3265536 | tf_op jit(solution)/shard_map/plan/pallas_call | solution.py:49
  15.3 0.0 copy-start.10
  15.3 0.6 copy-done.10
  15.9 0.0 copy-start.12
  15.9 0.6 copy-done.12
  16.5 0.0 copy-start.14
  16.5 0.6 copy-done.14
  17.1 0.0 copy-start.6
  17.1 1.0 %all-to-all-done.asked_ref = s32[32,1,128]{2,1,0:T(1,128)S(1)} async-done(((s32[32,1,128]{2,1,0:T(1,128)}), s32[32,1,128]{2,1,0:T(1,128)S(1)}, u32[]{:S(2)}, u32[]{:S(2)}) %all-to-all-start) | async-done | bytes 16416 | tf_op jit(solution)/shard_map/all_to_all | solution.py:248
  18.2 0.0 copy-done.5
  18.2 0.6 serve.1
  18.8 15.9 %all_to_all.15.answer_ref = bf16[32,3,2,768]{3,2,1,0:T(2,128)(2,1)S(1)} all-to-all(bf16[32,3,2,768]{3,2,1,0:T(2,128)(2,1)S(1)} %get-tuple-element.32), channel_id=1, replica_groups=mesh['grp'=4,'dev'=8] {'grp','dev'}, dimensions={0} | all-to-all | bytes 589824 | tf_op jit(solution)/shard_map/all_to_all | solution.py:274
  34.7 0.0 copy-done.6
  34.7 0.0 copy-done.3
  34.7 1.5 %layer_one.1 = (bf16[128,1024]{1,0:T(8,128)(2,1)S(1)}, bf16[32,3,2,1024]{3,2,1,0:T(2,128)(2,1)}) custom-call(bf16[32,3,2,768]{3,2,1,0:T(2,128)(2,1)S(1)} %all_to_all.15.answer_ref, bf16[128,192]{1,0:T(8,128)(2,1)S(1)} %get-tuple-element.33.far_ref, f32[128,768]{1,0:T(8,128)S(1)} %get-tuple-element.34.sum_ref, f32[128,1024]{1,0:T(8,128)S(1)} %get-tuple-element.35.own_ref, ...), custom_call_target="tpu_custom_call" | custom-call | flops 289406976 | bytes 3670016 | tf_op jit(solution)/shard_map/layer_one/pallas_call | solution.py:49
  36.2 0.0 copy-start.8
  36.2 0.7 %copy-done.8 = bf16[128,1024]{1,0:T(8,128)(2,1)} copy-done((bf16[128,1024]{1,0:T(8,128)(2,1)}, bf16[128,1024]{1,0:T(8,128)(2,1)S(1)}, u32[]{:S(2)}) %copy-start.8) | copy-done | bytes 262168
  36.9 0.0 copy-start
  36.9 2.7 %all-to-all-start.2 = ((bf16[32,3,2,1024]{3,2,1,0:T(2,128)(2,1)}), bf16[32,3,2,1024]{3,2,1,0:T(2,128)(2,1)S(1)}, u32[]{:S(2)}, u32[]{:S(2)}) async-start(bf16[32,3,2,1024]{3,2,1,0:T(2,128)(2,1)} %get-tuple-element.38), calls=%async_computation.2 | async-start | bytes 786432 | tf_op jit(solution)/shard_map/all_to_all | solution.py:291
  39.7 0.0 copy-start.1
  39.7 1.6 %copy-done.1 = bf16[1024,1024]{1,0:T(8,128)(2,1)S(1)} copy-done((bf16[1024,1024]{1,0:T(8,128)(2,1)S(1)}, bf16[1024,1024]{1,0:T(8,128)(2,1)}, u32[]{:S(2)}) %copy-start.1) | copy-done | bytes 2097176
  41.3 0.0 copy-start.9
  41.3 0.9 %copy-done.9 = bf16[128,1024]{1,0:T(8,128)(2,1)S(1)} copy-done((bf16[128,1024]{1,0:T(8,128)(2,1)S(1)}, bf16[128,1024]{1,0:T(8,128)(2,1)}, u32[]{:S(2)}) %copy-start.9) | copy-done | bytes 262168
  42.2 0.0 copy-start.13
  42.2 0.8 %copy-done.13 = bf16[128,128]{1,0:T(8,128)(2,1)S(1)} copy-done((bf16[128,128]{1,0:T(8,128)(2,1)S(1)}, bf16[128,128]{1,0:T(8,128)(2,1)}, u32[]{:S(2)}) %copy-start.13) | copy-done | bytes 32792
  43.0 0.0 copy-start.15
  43.0 0.8 %copy-done.15 = bf16[128,128]{1,0:T(8,128)(2,1)S(1)} copy-done((bf16[128,128]{1,0:T(8,128)(2,1)S(1)}, bf16[128,128]{1,0:T(8,128)(2,1)}, u32[]{:S(2)}) %copy-start.15) | copy-done | bytes 32792
  43.7 0.6 own_two.1
  44.4 8.7 %all-to-all-done.2.answer_ref = bf16[32,3,2,1024]{3,2,1,0:T(2,128)(2,1)S(1)} async-done(((bf16[32,3,2,1024]{3,2,1,0:T(2,128)(2,1)}), bf16[32,3,2,1024]{3,2,1,0:T(2,128)(2,1)S(1)}, u32[]{:S(2)}, u32[]{:S(2)}) %all-to-all-start.2) | async-done | bytes 393248 | tf_op jit(solution)/shard_map/all_to_all | solution.py:291
  53.1 0.0 copy-done
  53.1 0.0 copy-start.7
  53.1 0.9 %copy-done.7 = f32[2,128,128]{2,1,0:T(8,128)S(1)} copy-done((f32[2,128,128]{2,1,0:T(8,128)S(1)}, f32[2,128,128]{2,1,0:T(8,128)}, u32[]{:S(2)}) %copy-start.7) | copy-done | bytes 131096
  54.0 0.0 copy-start.11
  54.0 0.8 %copy-done.11 = bf16[128,192]{1,0:T(8,128)(2,1)S(1)} copy-done((bf16[128,192]{1,0:T(8,128)(2,1)S(1)}, bf16[128,192]{1,0:T(8,128)(2,1)}, u32[]{:S(2)}) %copy-start.11) | copy-done | bytes 49176
  54.8 0.6 layer_two.1
  55.4 0.1 collective-permute-start
  55.5 0.3 collective-permute-start.1
  55.8 3.5 %collective-permute-start.2 = (bf16[32,1024]{1,0:T(8,128)(2,1)S(1)}, bf16[32,1024]{1,0:T(8,128)(2,1)S(1)}, u32[]{:S(2)}, u32[]{:S(2)}) collective-permute-start(bf16[32,1024]{1,0:T(8,128)(2,1)S(1)} %get-tuple-element.48), channel_id=1, source_target_pairs={{0,6},{1,7},{2,0},{3,1},{4,2},{5,3},{6,4},{7,5},{8,14},{9,15},{10,... | collective-permute-start | bytes 196616 | tf_op jit(solution)/shard_map/ppermute | solution.py:308
  59.3 0.5 place.1.place_ref
  59.8 2.4 %collective-permute-done.refs_1_ = bf16[32,1024]{1,0:T(8,128)(2,1)S(1)} collective-permute-done((bf16[32,1024]{1,0:T(8,128)(2,1)S(1)}, bf16[32,1024]{1,0:T(8,128)(2,1)S(1)}, u32[]{:S(2)}, u32[]{:S(2)}) %collective-permute-start) | collective-permute-done | bytes 65568 | tf_op jit(solution)/shard_map/ppermute | solution.py:308
  62.3 1.8 %collective-permute-done.1.refs_2_ = bf16[32,1024]{1,0:T(8,128)(2,1)S(1)} collective-permute-done((bf16[32,1024]{1,0:T(8,128)(2,1)S(1)}, bf16[32,1024]{1,0:T(8,128)(2,1)S(1)}, u32[]{:S(2)}, u32[]{:S(2)}) %collective-permute-start.1) | collective-permute-done | bytes 65568 | tf_op jit(solution)/shard_map/ppermute | solution.py:308
  64.1 0.0 collective-permute-done.2.refs_3_
  64.1 0.9 %scatter.1 = bf16[128,1024]{1,0:T(8,128)(2,1)} custom-call(bf16[128,128]{1,0:T(8,128)(2,1)S(1)} %place.1.place_ref, bf16[32,1024]{1,0:T(8,128)(2,1)S(1)} %get-tuple-element.45.refs_0_, bf16[32,1024]{1,0:T(8,128)(2,1)S(1)} %collective-permute-done.refs_1_, bf16[32,1024]{1,0:T(8,128)(2,1)S(1)} %collective-permute-done.1.refs_2_, ...), custom_call_target="tpu_custom_call" | custom-call | flops 33554432 | bytes 524288 | tf_op jit(solution)/shard_map/scatter/pallas_call | solution.py:309
Async XLA Ops:
  0.0 18.2 %copy-start.5 = (bf16[128,768]{1,0:T(8,128)(2,1)S(1)}, bf16[128,768]{1,0:T(8,128)(2,1)}, u32[]{:S(2)}) copy-start(bf16[128,768]{1,0:T(8,128)(2,1)} %source_ref.1) | copy-start | bytes 589828
  1.7 0.7 %copy-start.16 = (s32[128]{0:T(128)S(1)}, s32[128]{0:T(128)}, u32[]{:S(2)}) copy-start(s32[128]{0:T(128)} %param.11) | copy-start | bytes 1540
  3.7 14.5 %all-to-all-start = ((s32[32,1,128]{2,1,0:T(1,128)}), s32[32,1,128]{2,1,0:T(1,128)S(1)}, u32[]{:S(2)}, u32[]{:S(2)}) async-start(s32[32,1,128]{2,1,0:T(1,128)} %get-tuple-element.27), calls=%async_computation | async-start | bytes 32768 | tf_op jit(solution)/shard_map/all_to_all | solution.py:248
  11.0 1.4 %copy-start.2 = (bf16[768,1024]{1,0:T(8,128)(2,1)S(1)}, bf16[768,1024]{1,0:T(8,128)(2,1)}, u32[]{:S(2)}) copy-start(bf16[768,1024]{1,0:T(8,128)(2,1)} %weight_ref.4) | copy-start | bytes 4718596
  12.4 0.9 %copy-start.4 = (bf16[128,768]{1,0:T(8,128)(2,1)S(1)}, bf16[128,768]{1,0:T(8,128)(2,1)}, u32[]{:S(2)}) copy-start(bf16[128,768]{1,0:T(8,128)(2,1)} %source_ref.1) | copy-start | bytes 589828
  13.3 0.7 %copy-start.17 = (s32[128]{0:T(128)S(1)}, s32[128]{0:T(128)}, u32[]{:S(2)}) copy-start(s32[128]{0:T(128)} %param.11) | copy-start | bytes 1540
  14.0 20.7 %copy-start.3 = (bf16[768,1024]{1,0:T(8,128)(2,1)S(1)}, bf16[768,1024]{1,0:T(8,128)(2,1)}, u32[]{:S(2)}) copy-start(bf16[768,1024]{1,0:T(8,128)(2,1)} %weight_ref.5) | copy-start | bytes 4718596
  15.3 0.6 copy-start.10
  15.9 0.6 copy-start.12
  16.5 0.6 copy-start.14
  17.1 17.6 %copy-start.6 = (f32[2,128,128]{2,1,0:T(8,128)}, f32[2,128,128]{2,1,0:T(8,128)S(1)}, u32[]{:S(2)}) copy-start(f32[2,128,128]{2,1,0:T(8,128)S(1)} %get-tuple-element.36.count_ref) | copy-start | bytes 393220
  36.2 0.7 %copy-start.8 = (bf16[128,1024]{1,0:T(8,128)(2,1)}, bf16[128,1024]{1,0:T(8,128)(2,1)S(1)}, u32[]{:S(2)}) copy-start(bf16[128,1024]{1,0:T(8,128)(2,1)S(1)} %get-tuple-element.40.hidden_ref) | copy-start | bytes 786436
  36.9 16.2 %copy-start = (bf16[1024,1024]{1,0:T(8,128)(2,1)S(1)}, bf16[1024,1024]{1,0:T(8,128)(2,1)}, u32[]{:S(2)}) copy-start(bf16[1024,1024]{1,0:T(8,128)(2,1)} %weight_ref.7) | copy-start | bytes 6291460
  36.9 16.2 %all-to-all-start.2 = ((bf16[32,3,2,1024]{3,2,1,0:T(2,128)(2,1)}), bf16[32,3,2,1024]{3,2,1,0:T(2,128)(2,1)S(1)}, u32[]{:S(2)}, u32[]{:S(2)}) async-start(bf16[32,3,2,1024]{3,2,1,0:T(2,128)(2,1)} %get-tuple-element.38), calls=%async_computation.2 | async-start | bytes 786432 | tf_op jit(solution)/shard_map/all_to_all | solution.py:291
  39.7 1.6 %copy-start.1 = (bf16[1024,1024]{1,0:T(8,128)(2,1)S(1)}, bf16[1024,1024]{1,0:T(8,128)(2,1)}, u32[]{:S(2)}) copy-start(bf16[1024,1024]{1,0:T(8,128)(2,1)} %weight_ref.6) | copy-start | bytes 6291460
  41.3 0.9 %copy-start.9 = (bf16[128,1024]{1,0:T(8,128)(2,1)S(1)}, bf16[128,1024]{1,0:T(8,128)(2,1)}, u32[]{:S(2)}) copy-start(bf16[128,1024]{1,0:T(8,128)(2,1)} %copy-done.8) | copy-start | bytes 786436
  42.2 0.8 %copy-start.13 = (bf16[128,128]{1,0:T(8,128)(2,1)S(1)}, bf16[128,128]{1,0:T(8,128)(2,1)}, u32[]{:S(2)}) copy-start(bf16[128,128]{1,0:T(8,128)(2,1)} %copy-done.12) | copy-start | bytes 98308
  43.0 0.8 %copy-start.15 = (bf16[128,128]{1,0:T(8,128)(2,1)S(1)}, bf16[128,128]{1,0:T(8,128)(2,1)}, u32[]{:S(2)}) copy-start(bf16[128,128]{1,0:T(8,128)(2,1)} %copy-done.14) | copy-start | bytes 98308
  53.1 0.9 %copy-start.7 = (f32[2,128,128]{2,1,0:T(8,128)S(1)}, f32[2,128,128]{2,1,0:T(8,128)}, u32[]{:S(2)}) copy-start(f32[2,128,128]{2,1,0:T(8,128)} %copy-done.6) | copy-start | bytes 393220
  54.0 0.8 %copy-start.11 = (bf16[128,192]{1,0:T(8,128)(2,1)S(1)}, bf16[128,192]{1,0:T(8,128)(2,1)}, u32[]{:S(2)}) copy-start(bf16[128,192]{1,0:T(8,128)(2,1)} %copy-done.10) | copy-start | bytes 147460
  55.4 6.9 %collective-permute-start = (bf16[32,1024]{1,0:T(8,128)(2,1)S(1)}, bf16[32,1024]{1,0:T(8,128)(2,1)S(1)}, u32[]{:S(2)}, u32[]{:S(2)}) collective-permute-start(bf16[32,1024]{1,0:T(8,128)(2,1)S(1)} %get-tuple-element.46), channel_id=1, source_target_pairs={{0,2},{1,3},{2,4},{3,5},{4,6},{5,7},{6,0},{7,1},{8,10},{9,11},{10,... | collective-permute-start | bytes 196616 | tf_op jit(solution)/shard_map/ppermute | solution.py:308
  55.5 8.6 %collective-permute-start.1 = (bf16[32,1024]{1,0:T(8,128)(2,1)S(1)}, bf16[32,1024]{1,0:T(8,128)(2,1)S(1)}, u32[]{:S(2)}, u32[]{:S(2)}) collective-permute-start(bf16[32,1024]{1,0:T(8,128)(2,1)S(1)} %get-tuple-element.47), channel_id=1, source_target_pairs={{0,4},{1,5},{2,6},{3,7},{4,0},{5,1},{6,2},{7,3},{8,12},{9,13},{10,... | collective-permute-start | bytes 196616 | tf_op jit(solution)/shard_map/ppermute | solution.py:308
  55.8 8.3 %collective-permute-start.2 = (bf16[32,1024]{1,0:T(8,128)(2,1)S(1)}, bf16[32,1024]{1,0:T(8,128)(2,1)S(1)}, u32[]{:S(2)}, u32[]{:S(2)}) collective-permute-start(bf16[32,1024]{1,0:T(8,128)(2,1)S(1)} %get-tuple-element.48), channel_id=1, source_target_pairs={{0,6},{1,7},{2,0},{3,1},{4,2},{5,3},{6,4},{7,5},{8,14},{9,15},{10,... | collective-permute-start | bytes 196616 | tf_op jit(solution)/shard_map/ppermute | solution.py:308

commit v2 on v1

v2 whole, which is shorter than its diff:
```python
import functools

import jax
import jax.numpy as jnp
from jax import lax
from jax.experimental import pallas as pl
from jax.experimental.pallas import tpu as pltpu
from jax.sharding import PartitionSpec as P

CAP = 6
BOTH = ("grp", "dev")
F32 = jnp.float32
BF16 = jnp.bfloat16
I32 = jnp.int32


def divide(values, by):
    if by & (by - 1) == 0:
        return values >> (by.bit_length() - 1)
    return (values * (-(-(1 << 16) // by))) >> 16


def iota(shape, dim):
    return lax.broadcasted_iota(I32, shape, dim)


def bits(condition):
    return jnp.where(condition, 1.0, 0.0)


def earlier(count):
    return bits(iota((count, count), 0) < iota((count, count), 1)).astype(BF16)


def dot(left, right):
    return jnp.dot(left, right, preferred_element_type=F32)


def dot_lanes(left, right):
    return lax.dot_general(left, right, (((1,), (1,)), ((), ())), preferred_element_type=F32)


def near_by(n):
    return [pl.BlockSpec(memory_space=pltpu.VMEM)] * n


def far_off(n):
    return [pl.BlockSpec(memory_space=pltpu.HBM)] * n


def call(kernel, outs, remote, operands, scratch, flops, name, limit=24 << 20):
    single = not isinstance(outs, tuple)
    leaves = (outs,) if single else outs
    moved = sum(a.size * a.dtype.itemsize for a in (*remote, *operands, *leaves))
    return pl.pallas_call(
        kernel,
        out_shape=outs,
        in_specs=far_off(len(remote)) + near_by(len(operands)),
        out_specs=near_by(1)[0] if single else near_by(len(leaves)),
        scratch_shapes=scratch,
        compiler_params=pltpu.CompilerParams(vmem_limit_bytes=limit),
        cost_estimate=pl.CostEstimate(flops=flops, bytes_accessed=moved, transcendentals=0),
        name=name,
    )(*(pltpu.with_memory_space_constraint(a, pltpu.HBM) for a in remote), *operands)


def fetches(weight_ref, held, sems):
    pieces = sems.shape[0]
    depth = weight_ref.shape[0] // pieces
    return [
        pltpu.make_async_copy(
            weight_ref.at[pl.ds(i * depth, depth)], held.at[pl.ds(i * depth, depth)], sems.at[i]
        )
        for i in range(pieces)
    ]


def dot_fetched(left, held, copies):
    depth = held.shape[0] // len(copies)
    result = None
    for i, copy in enumerate(copies):
        copy.wait()
        part = dot(left[:, i * depth : (i + 1) * depth], held[i * depth : (i + 1) * depth])
        result = part if result is None else result + part
    return result


def ask_kernel(members, peers, ids_hbm, mask_hbm, pos_hbm, ask_ref, key_ref, local_ref, span_ref, pos_ref, ids, mask, sems):
    degree, rows = ids.shape
    copies = [
        pltpu.make_async_copy(ids_hbm, ids, sems.at[0]),
        pltpu.make_async_copy(mask_hbm, mask, sems.at[1]),
        pltpu.make_async_copy(pos_hbm, pos_ref, sems.at[2]),
    ]
    for copy in copies:
        copy.start()
    own = lax.axis_index("grp") * members + lax.axis_index("dev")
    peer = iota((peers, rows), 0)
    prefix = earlier(rows)
    for copy in copies:
        copy.wait()
    slots = jnp.where(mask[...] > 0, ids[...], -1)
    owner = divide(jnp.maximum(slots, 0), rows)
    row = slots - owner * rows
    live = slots >= 0
    here = owner == own
    key = jnp.where(live & jnp.logical_not(here), owner, -1)
    total = jnp.zeros((peers, rows), I32)
    for s in range(degree):
        total += jnp.where(key[s : s + 1] == peer, 1, 0)
    before = dot(total.astype(F32).astype(BF16), prefix).astype(I32)
    width = (rows - 1).bit_length()
    per_word = max(1, min(CAP, 24 // width))
    words = -(-CAP // per_word)
    packed = [jnp.zeros((peers, rows), I32) for _ in range(words)]
    running = before
    for s in range(degree):
        hit = key[s : s + 1] == peer
        for w in range(words):
            shift = running - w * per_word
            fits = hit & (shift >= 0) & (shift < per_word)
            packed[w] += jnp.where(fits, row[s : s + 1] << (jnp.clip(shift, 0, per_word - 1) * width), 0)
        running += jnp.where(hit, 1, 0)
    lane = iota((peers, rows), 1)
    wanted = jnp.zeros((peers, rows), I32)
    for w in range(words):
        word = jnp.sum(packed[w].astype(F32), axis=1, keepdims=True).astype(I32)
        slot = lane - w * per_word
        mine = (slot >= 0) & (slot < per_word) & (lane < CAP)
        word = jnp.broadcast_to(word, (peers, rows))
        wanted += jnp.where(mine, (word >> (jnp.clip(slot, 0, per_word - 1) * width)) & ((1 << width) - 1), 0)
    pos = pos_ref[...]
    place = jnp.where(divide(pos, rows) == peer, pos - divide(pos, rows) * rows + 1, 0)
    ask_ref[...] = (place + wanted * (2 * rows)).reshape(peers, 1, rows)
    key_ref[...] = key
    local_ref[...] = jnp.where(live & here, row, -1)
    span_ref[0] = before
    span_ref[1] = total


def plan_kernel(
    peers, degree, weight_hbm, key_ref, local_ref, span_ref, features_ref,
    near_ref, far_ref, order_ref, count_ref, sum_ref, own_ref, held, sems,
):
    copies = fetches(weight_hbm, held, sems)
    for copy in copies:
        copy.start()
    rows = features_ref.shape[0]
    local = local_ref[...]
    node = iota((rows, rows), 0)
    near = jnp.zeros((rows, rows), F32)
    for s in range(degree):
        near += bits(local[s : s + 1] == node)
    near = near.T.astype(BF16)
    near_ref[...] = near
    before, total = span_ref[0], span_ref[1]
    far = [bits((before <= k) & (k < before + total)).astype(BF16) for k in range(CAP)]
    far = jnp.concatenate(far, axis=0)
    size = peers * CAP
    line = iota((size, size), 0)
    peer = divide(line, CAP)
    order = bits(iota((size, size), 1) == (line - peer * CAP) * peers + peer).astype(BF16)
    order_ref[...] = order
    far_ref[...] = dot(order, far).T.astype(BF16)
    live = bits((local >= 0) | (key_ref[...] >= 0))
    count_ref[...] = jnp.broadcast_to(jnp.sum(live, axis=0, keepdims=True), (rows, rows)).T
    features = features_ref[...]
    sum_ref[...] = dot(near, features)
    own_ref[...] = dot_fetched(features, held, copies)


def store_rows(reply_ref, rows):
    peers, pairs, two, width = reply_ref.shape
    reply_ref[...] = rows.reshape(peers, pairs, two, width)


def load_rows(answer_ref):
    peers, pairs, two, width = answer_ref.shape
    return answer_ref[...].reshape(peers * pairs * two, width)


def serve_kernel(asked_ref, order_ref, source_ref, reply_ref, pick_ref):
    peers, _, rows = asked_ref.shape
    asked = asked_ref[...].reshape(peers, rows)
    wanted = divide(asked, 2 * rows)
    lane = iota((peers, rows), 1)
    picks = [bits(wanted[:, k : k + 1] == lane).astype(BF16) for k in range(CAP)]
    pick = dot(order_ref[...], jnp.concatenate(picks, axis=0)).astype(BF16)
    pick_ref[...] = pick
    store_rows(reply_ref, dot(pick, source_ref[...]).astype(BF16))


def layer_one_kernel(weight_hbm, answer_ref, far_ref, sum_ref, own_ref, count_ref, pick_ref, hidden_ref, reply_ref, held, sems):
    copies = fetches(weight_hbm, held, sems)
    for copy in copies:
        copy.start()
    summed = sum_ref[...] + dot(far_ref[...], load_rows(answer_ref))
    mean = (summed / count_ref[:, :1]).astype(BF16)
    hidden = jnp.maximum(own_ref[...] + dot_fetched(mean, held, copies), 0.0).astype(BF16)
    hidden_ref[...] = hidden
    store_rows(reply_ref, dot(pick_ref[...], hidden).astype(BF16))


def own_two_kernel(
    members, weight_hbm, hidden_ref, near_ref, far_ref, count_ref, pos_ref, asked_ref,
    sum_ref, own_ref, far_moved_ref, count_moved_ref, place_ref, held, sems,
):
    copies = fetches(weight_hbm, held, sems)
    for copy in copies:
        copy.start()
    rows = hidden_ref.shape[0]
    capacity = 2 * rows // members
    me = lax.axis_index("dev")
    first = lax.axis_index("grp") * members
    line = iota((rows, rows), 0)
    step = divide(line, capacity)
    rank = line - step * capacity
    target = me + 2 * step
    target = jnp.where(target >= members, target - members, target)
    goes = target == divide(pos_ref[...], rows) - first
    prefix = earlier(rows)
    before = dot(bits(goes).astype(BF16), prefix).astype(I32)
    move = bits(goes & (before == rank)).astype(BF16)
    hidden = hidden_ref[...]
    sum_ref[...] = dot(dot(move, near_ref[...]).astype(BF16), hidden)
    far_moved_ref[...] = dot(move, far_ref[...]).astype(BF16)
    count_moved_ref[...] = dot(move, count_ref[...].astype(BF16))
    own_ref[...] = dot_fetched(dot(move, hidden).astype(BF16), held, copies)
    place = jnp.zeros((rows, rows), F32)
    for q in range(members // 2):
        source = me - 2 * q
        source = first + jnp.where(source < 0, source + members, source)
        sent = asked_ref[source] & (2 * rows - 1)
        valid = jnp.broadcast_to(sent > 0, (rows, rows))
        before = dot(bits(valid).astype(BF16), prefix).astype(I32)
        lands = bits(sent - 1 == line).astype(BF16)
        comes = bits(valid & (step == q) & (before == rank)).astype(BF16)
        place += dot_lanes(lands, comes)
    place_ref[...] = place.astype(BF16)


def layer_two_kernel(weight_hbm, answer_ref, far_ref, sum_ref, own_ref, count_ref, *refs):
    final_refs, held, sems = refs[:-2], refs[-2], refs[-1]
    copies = fetches(weight_hbm, held, sems)
    for copy in copies:
        copy.start()
    summed = sum_ref[...] + dot(far_ref[...], load_rows(answer_ref))
    mean = (summed / count_ref[:, :1]).astype(BF16)
    final = (own_ref[...] + dot_fetched(mean, held, copies)).astype(BF16)
    capacity = final_refs[0].shape[0]
    for q, ref in enumerate(final_refs):
        ref[...] = final[q * capacity : (q + 1) * capacity]


def scatter_kernel(place_ref, *refs):
    out_ref = refs[-1]
    arrived = jnp.concatenate([ref[...] for ref in refs[:-1]], axis=0)
    out_ref[...] = dot(place_ref[...], arrived).astype(BF16)


def body(features, neighbours, neighbour_mask, layer2_position, self_weight1, neigh_weight1, self_weight2, neigh_weight2):
    rows, degree = neighbours.shape
    members = lax.axis_size("dev")
    peers = lax.axis_size("grp") * members
    width_in, width = self_weight1.shape
    steps = members // 2
    capacity = rows // steps
    size = peers * CAP
    shape = jax.ShapeDtypeStruct
    copies = pltpu.SemaphoreType.DMA

    ask, key, local, span, pos = call(
        functools.partial(ask_kernel, members, peers),
        (
            shape((peers, 1, rows), I32),
            shape((degree, rows), I32),
            shape((degree, rows), I32),
            shape((2, peers, rows), I32),
            shape((1, rows), I32),
        ),
        (neighbours.T, neighbour_mask.T, layer2_position.reshape(1, rows)),
        (),
        [pltpu.VMEM((degree, rows), I32), pltpu.VMEM((degree, rows), I32), copies((3,))],
        2 * peers * rows * rows,
        "ask",
    )
    asked = lax.all_to_all(ask, BOTH, 0, 0, tiled=True)
    near, far, order, count, sum_one, own_one = call(
        functools.partial(plan_kernel, peers, degree),
        (
            shape((rows, rows), BF16),
            shape((rows, size), BF16),
            shape((size, size), BF16),
            shape((rows, rows), F32),
            shape((rows, width_in), F32),
            shape((rows, width), F32),
        ),
        (self_weight1,),
        (key, local, span, features),
        [pltpu.VMEM((width_in, width), BF16), copies((1,))],
        2 * rows * width_in * (rows + width),
        "plan",
        limit=40 << 20,
    )
    reply, pick = call(
        serve_kernel,
        (shape((peers, CAP // 2, 2, width_in), BF16), shape((size, rows), BF16)),
        (),
        (asked, order, features),
        [],
        2 * size * rows * width_in,
        "serve",
    )
    answer = lax.all_to_all(reply, BOTH, 0, 0, tiled=True)
    hidden, reply_two = call(
        layer_one_kernel,
        (shape((rows, width), BF16), shape((peers, CAP // 2, 2, width), BF16)),
        (neigh_weight1,),
        (answer, far, sum_one, own_one, count, pick),
        [pltpu.VMEM((width_in, width), BF16), copies((3,))],
        2 * rows * width_in * (size + width) + 2 * size * rows * width,
        "layer_one",
    )
    answer_two = lax.all_to_all(reply_two, BOTH, 0, 0, tiled=True)
    sum_two, own_two, far_moved, count_moved, place = call(
        functools.partial(own_two_kernel, members),
        (
            shape((rows, width), F32),
            shape((rows, width), F32),
            shape((rows, size), BF16),
            shape((rows, rows), F32),
            shape((rows, rows), BF16),
        ),
        (self_weight2,),
        (hidden, near, far, count, pos, asked),
        [pltpu.VMEM((width, width), BF16), copies((1,))],
        2 * rows * width * (2 * rows + width),
        "own_two",
    )
    finals = call(
        layer_two_kernel,
        tuple(shape((capacity, width), BF16) for _ in range(steps)),
        (neigh_weight2,),
        (answer_two, far_moved, sum_two, own_two, count_moved),
        [pltpu.VMEM((width, width), BF16), copies((4,))],
        2 * rows * width * (size + width),
        "layer_two",
    )
    arrived = [finals[0]]
    for q in range(1, steps):
        arrived.append(lax.ppermute(finals[q], "dev", [(i, (i + 2 * q) % members) for i in range(members)]))
    return call(
        scatter_kernel,
        shape((rows, width), BF16),
        (),
        (place, *arrived),
        [],
        2 * rows * rows * width,
        "scatter",
    )


def solution(mesh):
    return jax.shard_map(
        body,
        mesh=mesh,
        in_specs=(
            P(BOTH, None),
            P(BOTH, None),
            P(BOTH, None),
            P(BOTH),
            P(),
            P(),
            P(),
            P(),
        ),
        out_specs=P(BOTH, None),
        check_vma=False,
    )
```

time: 65.6 us -> 61.8 us (0.942)
  local copies, waits for them, and re-layouts: 13.7 us -> 1.85 us
  waiting for transfers between devices: 14 us -> 19.6 us
  Pallas kernels: 7.38 us -> 12.9 us
  blocking collectives: 15.9 us -> 13 us
    unnamed x38 -> x4, local copies, waits for them, and re-layouts: 13.7 us -> 1.85 us
    pallas_call x8 -> x7, Pallas kernels: 7.38 us -> 12.9 us  [call(): pl.pallas_call(kernel, out_shape=outs, in_specs=far_off(len(remote)) + ne...]
    all_to_all x1, waiting for transfers between devices: 1.04 us -> 4.12 us  [body(): asked = lax.all_to_all(ask, BOTH, 0, 0, tiled=True)]
    all_to_all x1, blocking collectives: 15.9 us -> 13 us  [body(): answer = lax.all_to_all(reply, BOTH, 0, 0, tiled=True)]
    all_to_all x1, waiting for transfers between devices: 8.72 us -> 10.7 us  [body(): answer_two = lax.all_to_all(reply_two, BOTH, 0, 0, tiled=True)]
  transfers between devices with their start and end apart: 5 -> 5, of which waited for: 4 -> 4; matrix products, arithmetic and copies ran while one was open for 0% -> 0% of each run, Pallas kernels for 4% -> 8%
where the time goes in v2:
time: 61.8 us; the launch traced here: 61.4 us
  waiting for transfers between devices  19.6 us (32%)
  starting transfers between devices  13.8 us (22%)
  blocking collectives  13 us (21%)
  Pallas kernels  12.9 us (21%)
  local copies, waits for them, and re-layouts  1.85 us (3%)
    all_to_all x1, blocking collectives, body(): answer = lax.all_to_all(reply, BOTH, 0, 0, tiled=True)  13 us
    pallas_call x7, Pallas kernels, call(): pl.pallas_call(kernel, out_shape=outs, in_specs=far_off(len(remote)) + ne...  12.9 us
    all_to_all x1, waiting for transfers between devices, body(): answer_two = lax.all_to_all(reply_two, BOTH, 0, 0, tiled=True)  10.7 us
    all_to_all x1, starting transfers between devices, body(): asked = lax.all_to_all(ask, BOTH, 0, 0, tiled=True)  7.33 us
    ppermute x3, waiting for transfers between devices, body(): lax.ppermute(finals[q], 'dev', [(i, (i + 2 * q) % members) for i in range...  4.79 us
    all_to_all x1, waiting for transfers between devices, body(): asked = lax.all_to_all(ask, BOTH, 0, 0, tiled=True)  4.12 us
    ppermute x3, starting transfers between devices, body(): lax.ppermute(finals[q], 'dev', [(i, (i + 2 * q) % members) for i in range...  3.87 us
    all_to_all x1, starting transfers between devices, body(): answer_two = lax.all_to_all(reply_two, BOTH, 0, 0, tiled=True)  2.61 us
  transfers between devices with their start and end apart: 5, of which 4 were waited for; matrix products, arithmetic and copies ran while one was open for 0% of the time, Pallas kernels for 8%

profile of v2, /device:TPU:0, one launch (start us, length us, event | category | flops | bytes accessed | tf_op | source)
XLA Modules:
  0.0 61.4 jit_solution(8052879062691207383)
XLA Ops:
  0.0 2.0 %ask.1 = (s32[32,1,128]{2,1,0:T(1,128)}, s32[25,128]{1,0:T(8,128)S(1)}, s32[25,128]{1,0:T(8,128)S(1)}, s32[2,32,128]{2,1,0:T(8,128)S(1)}, s32[1,128]{1,0:T(1,128)S(1)}) custom-call(s32[25,128]{1,0:T(8,128)} %bitcast.3, s32[25,128]{1,0:T(8,128)} %bitcast.4, s32[1,128]{1,0:T(1,128)} %bitcast.5), custom_call_target="tpu_custom_call" | custom-call | flops 1048576 | bytes 101376 | tf_op jit(solution)/shard_map/ask/pallas_call | solution.py:55
  2.0 7.3 %all-to-all-start = ((s32[32,1,128]{2,1,0:T(1,128)}), s32[32,1,128]{2,1,0:T(1,128)S(1)}, u32[]{:S(2)}, u32[]{:S(2)}) async-start(s32[32,1,128]{2,1,0:T(1,128)} %get-tuple-element.29), calls=%async_computation | async-start | bytes 32768 | tf_op jit(solution)/shard_map/all_to_all | solution.py:287
  9.4 0.0 copy-start
  9.4 0.9 %copy-done = bf16[128,768]{1,0:T(8,128)(2,1)S(1)} copy-done((bf16[128,768]{1,0:T(8,128)(2,1)S(1)}, bf16[128,768]{1,0:T(8,128)(2,1)}, u32[]{:S(2)}) %copy-start) | copy-done | bytes 196632
  10.3 2.0 %plan.1 = (bf16[128,128]{1,0:T(8,128)(2,1)S(1)}, bf16[128,192]{1,0:T(8,128)(2,1)S(1)}, bf16[192,192]{1,0:T(8,128)(2,1)S(1)}, f32[128,128]{1,0:T(8,128)S(1)}, f32...) custom-call(bf16[768,1024]{1,0:T(8,128)(2,1)} %weight_hbm.4, s32[25,128]{1,0:T(8,128)S(1)} %get-tuple-element.30.key_ref, ...), custom_call_target="tpu_custom_call" | custom-call | flops 226492416 | bytes 2966528 | tf_op jit(solution)/shard_map/plan/pallas_call | solution.py:55
  12.3 4.1 %all-to-all-done.asked_ref = s32[32,1,128]{2,1,0:T(1,128)S(1)} async-done(((s32[32,1,128]{2,1,0:T(1,128)}), s32[32,1,128]{2,1,0:T(1,128)S(1)}, u32[]{:S(2)}, u32[]{:S(2)}) %all-to-all-start) | async-done | bytes 16416 | tf_op jit(solution)/shard_map/all_to_all | solution.py:287
  16.5 0.0 copy-start.1
  16.5 0.9 %copy-done.1 = bf16[128,768]{1,0:T(8,128)(2,1)S(1)} copy-done((bf16[128,768]{1,0:T(8,128)(2,1)S(1)}, bf16[128,768]{1,0:T(8,128)(2,1)}, u32[]{:S(2)}) %copy-start.1) | copy-done | bytes 196632
  17.4 0.6 %serve.1 = (bf16[32,3,2,768]{3,2,1,0:T(2,128)(2,1)S(1)}, bf16[192,128]{1,0:T(8,128)(2,1)S(1)}) custom-call(s32[32,1,128]{2,1,0:T(1,128)S(1)} %all-to-all-done.asked_ref, bf16[192,192]{1,0:T(8,128)(2,1)S(1)} %get-tuple-element.33.order_ref, bf16[128,768]{1,0:T(8,128)(2,1)S(1)} %copy-done.1), custom_call_target="tpu_custom_call" | custom-call | flops 37748736 | bytes 630784 | tf_op jit(solution)/shard_map/serve/pallas_call | solution.py:55
  18.0 13.0 %all_to_all.15.answer_ref = bf16[32,3,2,768]{3,2,1,0:T(2,128)(2,1)S(1)} all-to-all(bf16[32,3,2,768]{3,2,1,0:T(2,128)(2,1)S(1)} %get-tuple-element.34), channel_id=1, replica_groups=mesh['grp'=4,'dev'=8] {'grp','dev'}, dimensions={0} | all-to-all | bytes 589824 | tf_op jit(solution)/shard_map/all_to_all | solution.py:314
  31.1 2.8 %layer_one.1 = (bf16[128,1024]{1,0:T(8,128)(2,1)S(1)}, bf16[32,3,2,1024]{3,2,1,0:T(2,128)(2,1)}) custom-call(bf16[768,1024]{1,0:T(8,128)(2,1)} %weight_hbm.5, bf16[32,3,2,768]{3,2,1,0:T(2,128)(2,1)S(1)} %all_to_all.15.answer_ref, bf16[128,192]{1,0:T(8,128)(2,1)S(1)} %get-tuple-element.35.far_ref, f32[128,768]{1,0:T(8,128)S(1)} %get-tuple-element.36.sum_ref, ...), custom_call_target="tpu_custom_call" | custom-call | flops 289406976 | bytes 3604480 | tf_op jit(solution)/shard_map/layer_one/pallas_call | solution.py:55
  33.9 2.6 %all-to-all-start.2 = ((bf16[32,3,2,1024]{3,2,1,0:T(2,128)(2,1)}), bf16[32,3,2,1024]{3,2,1,0:T(2,128)(2,1)S(1)}, u32[]{:S(2)}, u32[]{:S(2)}) async-start(bf16[32,3,2,1024]{3,2,1,0:T(2,128)(2,1)} %get-tuple-element.44), calls=%async_computation.2 | async-start | bytes 786432 | tf_op jit(solution)/shard_map/all_to_all | solution.py:324
  36.5 2.7 %own_two.1 = (f32[128,1024]{1,0:T(8,128)S(1)}, f32[128,1024]{1,0:T(8,128)S(1)}, bf16[128,192]{1,0:T(8,128)(2,1)S(1)}, f32[128,128]{1,0:T(8,128)S(1)}, bf16[128,128]{1,0:T(8,128)(2,1)S(1)}) custom-call(bf16[1024,1024]{1,0:T(8,128)(2,1)} %weight_hbm.6, bf16[128,1024]{1,0:T(8,128)(2,1)S(1)} %get-tuple-element.40.hidden_ref, ...), custom_call_target="tpu_custom_call" | custom-call | flops 335544320 | bytes 3719680 | tf_op jit(solution)/shard_map/own_two/pallas_call | solution.py:55
  39.2 10.7 %all-to-all-done.2.answer_ref = bf16[32,3,2,1024]{3,2,1,0:T(2,128)(2,1)S(1)} async-done(((bf16[32,3,2,1024]{3,2,1,0:T(2,128)(2,1)}), bf16[32,3,2,1024]{3,2,1,0:T(2,128)(2,1)S(1)}, u32[]{:S(2)}, u32[]{:S(2)}) %all-to-all-start.2) | async-done | bytes 393248 | tf_op jit(solution)/shard_map/all_to_all | solution.py:324
  49.9 1.9 %layer_two.1 = (bf16[32,1024]{1,0:T(8,128)(2,1)S(1)}, bf16[32,1024]{1,0:T(8,128)(2,1)S(1)}, bf16[32,1024]{1,0:T(8,128)(2,1)S(1)}, bf16[32,1024]{1,0:T(8,128)(2,1)S(1)}) custom-call(bf16[1024,1024]{1,0:T(8,128)(2,1)} %weight_hbm.7, bf16[32,3,2,1024]{3,2,1,0:T(2,128)(2,1)S(1)} %all-to-all-done.2.answer_ref, bf16[128,192]{1,0:T(8,128)(2,1)S(1)} %get-tuple-element.45.far_ref, ...), custom_call_target="tpu_custom_call" | custom-call | flops 318767104 | bytes 3915776 | tf_op jit(solution)/shard_map/layer_two/pallas_call | solution.py:55
  51.8 0.1 collective-permute-start
  51.8 0.3 collective-permute-start.1
  52.1 3.5 %collective-permute-start.2 = (bf16[32,1024]{1,0:T(8,128)(2,1)S(1)}, bf16[32,1024]{1,0:T(8,128)(2,1)S(1)}, u32[]{:S(2)}, u32[]{:S(2)}) collective-permute-start(bf16[32,1024]{1,0:T(8,128)(2,1)S(1)} %get-tuple-element.52), channel_id=1, source_target_pairs={{0,6},{1,7},{2,0},{3,1},{4,2},{5,3},{6,4},{7,5},{8,14},{9,15},{10,... | collective-permute-start | bytes 196616 | tf_op jit(solution)/shard_map/ppermute | solution.py:351
  55.7 3.0 %collective-permute-done.refs_1_ = bf16[32,1024]{1,0:T(8,128)(2,1)S(1)} collective-permute-done((bf16[32,1024]{1,0:T(8,128)(2,1)S(1)}, bf16[32,1024]{1,0:T(8,128)(2,1)S(1)}, u32[]{:S(2)}, u32[]{:S(2)}) %collective-permute-start) | collective-permute-done | bytes 65568 | tf_op jit(solution)/shard_map/ppermute | solution.py:351
  58.6 1.8 %collective-permute-done.1.refs_2_ = bf16[32,1024]{1,0:T(8,128)(2,1)S(1)} collective-permute-done((bf16[32,1024]{1,0:T(8,128)(2,1)S(1)}, bf16[32,1024]{1,0:T(8,128)(2,1)S(1)}, u32[]{:S(2)}, u32[]{:S(2)}) %collective-permute-start.1) | collective-permute-done | bytes 65568 | tf_op jit(solution)/shard_map/ppermute | solution.py:351
  60.5 0.0 collective-permute-done.2.refs_3_
  60.5 0.9 %scatter.1 = bf16[128,1024]{1,0:T(8,128)(2,1)} custom-call(bf16[128,128]{1,0:T(8,128)(2,1)S(1)} %get-tuple-element.43.place_ref, bf16[32,1024]{1,0:T(8,128)(2,1)S(1)} %get-tuple-element.49.refs_0_, bf16[32,1024]{1,0:T(8,128)(2,1)S(1)} %collective-permute-done.refs_1_, bf16[32,1024]{1,0:T(8,128)(2,1)S(1)} %collective-permute-done.1.refs_2_, ...), custom_call_target="tpu_custom_call" | custom-call | flops 33554432 | bytes 557056 | tf_op jit(solution)/shard_map/scatter/pallas_call | solution.py:55
Async XLA Ops:
  2.0 14.4 %all-to-all-start = ((s32[32,1,128]{2,1,0:T(1,128)}), s32[32,1,128]{2,1,0:T(1,128)S(1)}, u32[]{:S(2)}, u32[]{:S(2)}) async-start(s32[32,1,128]{2,1,0:T(1,128)} %get-tuple-element.29), calls=%async_computation | async-start | bytes 32768 | tf_op jit(solution)/shard_map/all_to_all | solution.py:287
  9.4 0.9 %copy-start = (bf16[128,768]{1,0:T(8,128)(2,1)S(1)}, bf16[128,768]{1,0:T(8,128)(2,1)}, u32[]{:S(2)}) copy-start(bf16[128,768]{1,0:T(8,128)(2,1)} %source_ref.1) | copy-start | bytes 589828
  16.5 0.9 %copy-start.1 = (bf16[128,768]{1,0:T(8,128)(2,1)S(1)}, bf16[128,768]{1,0:T(8,128)(2,1)}, u32[]{:S(2)}) copy-start(bf16[128,768]{1,0:T(8,128)(2,1)} %source_ref.1) | copy-start | bytes 589828
  33.9 16.0 %all-to-all-start.2 = ((bf16[32,3,2,1024]{3,2,1,0:T(2,128)(2,1)}), bf16[32,3,2,1024]{3,2,1,0:T(2,128)(2,1)S(1)}, u32[]{:S(2)}, u32[]{:S(2)}) async-start(bf16[32,3,2,1024]{3,2,1,0:T(2,128)(2,1)} %get-tuple-element.44), calls=%async_computation.2 | async-start | bytes 786432 | tf_op jit(solution)/shard_map/all_to_all | solution.py:324
  51.8 6.9 %collective-permute-start = (bf16[32,1024]{1,0:T(8,128)(2,1)S(1)}, bf16[32,1024]{1,0:T(8,128)(2,1)S(1)}, u32[]{:S(2)}, u32[]{:S(2)}) collective-permute-start(bf16[32,1024]{1,0:T(8,128)(2,1)S(1)} %get-tuple-element.50), channel_id=1, source_target_pairs={{0,2},{1,3},{2,4},{3,5},{4,6},{5,7},{6,0},{7,1},{8,10},{9,11},{10,... | collective-permute-start | bytes 196616 | tf_op jit(solution)/shard_map/ppermute | solution.py:351
  51.8 8.6 %collective-permute-start.1 = (bf16[32,1024]{1,0:T(8,128)(2,1)S(1)}, bf16[32,1024]{1,0:T(8,128)(2,1)S(1)}, u32[]{:S(2)}, u32[]{:S(2)}) collective-permute-start(bf16[32,1024]{1,0:T(8,128)(2,1)S(1)} %get-tuple-element.51), channel_id=1, source_target_pairs={{0,4},{1,5},{2,6},{3,7},{4,0},{5,1},{6,2},{7,3},{8,12},{9,13},{10,... | collective-permute-start | bytes 196616 | tf_op jit(solution)/shard_map/ppermute | solution.py:351
  52.1 8.3 %collective-permute-start.2 = (bf16[32,1024]{1,0:T(8,128)(2,1)S(1)}, bf16[32,1024]{1,0:T(8,128)(2,1)S(1)}, u32[]{:S(2)}, u32[]{:S(2)}) collective-permute-start(bf16[32,1024]{1,0:T(8,128)(2,1)S(1)} %get-tuple-element.52), channel_id=1, source_target_pairs={{0,6},{1,7},{2,0},{3,1},{4,2},{5,3},{6,4},{7,5},{8,14},{9,15},{10,... | collective-permute-start | bytes 196616 | tf_op jit(solution)/shard_map/ppermute | solution.py:351

commit v3 on v2

--- a/solution.py
+++ b/solution.py
@@ -85,7 +85,7 @@
     return result
 
 
-def ask_kernel(members, peers, ids_hbm, mask_hbm, pos_hbm, ask_ref, key_ref, local_ref, span_ref, pos_ref, ids, mask, sems):
+def ask_kernel(members, peers, ids_hbm, mask_hbm, pos_hbm, ask_ref, key_ref, local_ref, span_ref, ids, mask, pos_ref, sems):
     degree, rows = ids.shape
     copies = [
         pltpu.make_async_copy(ids_hbm, ids, sems.at[0]),
@@ -105,30 +105,31 @@
     live = slots >= 0
     here = owner == own
     key = jnp.where(live & jnp.logical_not(here), owner, -1)
+    half = CAP // 2
+    width = (rows - 1).bit_length()
+    top = width * (half - 1)
+    low = jnp.zeros((peers, rows), I32)
+    high = jnp.zeros((peers, rows), I32)
     total = jnp.zeros((peers, rows), I32)
     for s in range(degree):
-        total += jnp.where(key[s : s + 1] == peer, 1, 0)
+        hit = key[s : s + 1] == peer
+        high = jnp.where(hit, (high << width) | (low >> top), high)
+        low = jnp.where(hit, ((low & ((1 << top) - 1)) << width) | row[s : s + 1], low)
+        total += jnp.where(hit, 1, 0)
     before = dot(total.astype(F32).astype(BF16), prefix).astype(I32)
-    width = (rows - 1).bit_length()
-    per_word = max(1, min(CAP, 24 // width))
-    words = -(-CAP // per_word)
-    packed = [jnp.zeros((peers, rows), I32) for _ in range(words)]
-    running = before
-    for s in range(degree):
-        hit = key[s : s + 1] == peer
-        for w in range(words):
-            shift = running - w * per_word
-            fits = hit & (shift >= 0) & (shift < per_word)
-            packed[w] += jnp.where(fits, row[s : s + 1] << (jnp.clip(shift, 0, per_word - 1) * width), 0)
-        running += jnp.where(hit, 1, 0)
+    packed = [jnp.where(before == 0, low, 0), jnp.where(before == 0, high, jnp.where(before == half, low, 0))]
+    for k in range(1, half):
+        shift, rest = width * k, width * (half - k)
+        inside = before == k
+        packed[0] = jnp.where(inside, (low & ((1 << rest) - 1)) << shift, packed[0])
+        packed[1] = jnp.where(inside, (high << shift) | (low >> rest), packed[1])
+        packed[1] = jnp.where(before == half + k, low << shift, packed[1])
     lane = iota((peers, rows), 1)
     wanted = jnp.zeros((peers, rows), I32)
-    for w in range(words):
-        word = jnp.sum(packed[w].astype(F32), axis=1, keepdims=True).astype(I32)
-        slot = lane - w * per_word
-        mine = (slot >= 0) & (slot < per_word) & (lane < CAP)
-        word = jnp.broadcast_to(word, (peers, rows))
-        wanted += jnp.where(mine, (word >> (jnp.clip(slot, 0, per_word - 1) * width)) & ((1 << width) - 1), 0)
+    for w, word in enumerate(packed):
+        word = jnp.broadcast_to(jnp.sum(word.astype(F32), axis=1, keepdims=True).astype(I32), (peers, rows))
+        for k in range(half):
+            wanted = jnp.where(lane == w * half + k, (word >> (width * k)) & ((1 << width) - 1), wanted)
     pos = pos_ref[...]
     place = jnp.where(divide(pos, rows) == peer, pos - divide(pos, rows) * rows + 1, 0)
     ask_ref[...] = (place + wanted * (2 * rows)).reshape(peers, 1, rows)
@@ -139,11 +140,13 @@
 
 
 def plan_kernel(
-    peers, degree, weight_hbm, key_ref, local_ref, span_ref, features_ref,
-    near_ref, far_ref, order_ref, count_ref, sum_ref, own_ref, held, sems,
+    peers, degree, features_hbm, weight_hbm, later_hbm, key_ref, local_ref, span_ref,
+    near_ref, far_ref, order_ref, count_ref, sum_ref, own_ref, features_ref, later_ref, held, sems,
 ):
-    copies = fetches(weight_hbm, held, sems)
-    for copy in copies:
+    taken = pltpu.make_async_copy(features_hbm, features_ref, sems.at[1])
+    later = pltpu.make_async_copy(later_hbm.at[pl.ds(0, later_ref.shape[0])], later_ref, sems.at[2])
+    copies = fetches(weight_hbm, held, sems.at[pl.ds(0, 1)])
+    for copy in (taken, *copies, later):
         copy.start()
     rows = features_ref.shape[0]
     local = local_ref[...]
@@ -163,10 +166,12 @@
     order_ref[...] = order
     far_ref[...] = dot(order, far).T.astype(BF16)
     live = bits((local >= 0) | (key_ref[...] >= 0))
-    count_ref[...] = jnp.broadcast_to(jnp.sum(live, axis=0, keepdims=True), (rows, rows)).T
+    count_ref[...] = jnp.broadcast_to(jnp.sum(live, axis=0, keepdims=True), (rows, rows)).T.astype(BF16)
+    taken.wait()
     features = features_ref[...]
     sum_ref[...] = dot(near, features)
     own_ref[...] = dot_fetched(features, held, copies)
+    later.wait()
 
 
 def store_rows(reply_ref, rows):
@@ -190,23 +195,34 @@
     store_rows(reply_ref, dot(pick, source_ref[...]).astype(BF16))
 
 
-def layer_one_kernel(weight_hbm, answer_ref, far_ref, sum_ref, own_ref, count_ref, pick_ref, hidden_ref, reply_ref, held, sems):
-    copies = fetches(weight_hbm, held, sems)
-    for copy in copies:
-        copy.start()
+def mean_product(weight_hbm, weight_ref, held, sems, answer_ref, far_ref, sum_ref, own_ref, count_ref):
+    ready = weight_ref.shape[0]
+    rest = pltpu.make_async_copy(weight_hbm.at[pl.ds(ready, held.shape[0])], held, sems.at[0])
+    rest.start()
     summed = sum_ref[...] + dot(far_ref[...], load_rows(answer_ref))
-    mean = (summed / count_ref[:, :1]).astype(BF16)
-    hidden = jnp.maximum(own_ref[...] + dot_fetched(mean, held, copies), 0.0).astype(BF16)
+    mean = (summed / count_ref[:, :1].astype(F32)).astype(BF16)
+    result = own_ref[...] + dot(mean[:, :ready], weight_ref[...])
+    rest.wait()
+    return result + dot(mean[:, ready:], held[...])
+
+
+def layer_one_kernel(
+    weight_hbm, weight_ref, answer_ref, far_ref, sum_ref, own_ref, count_ref, pick_ref, hidden_ref, reply_ref, held, sems
+):
+    hidden = mean_product(weight_hbm, weight_ref, held, sems, answer_ref, far_ref, sum_ref, own_ref, count_ref)
+    hidden = jnp.maximum(hidden, 0.0).astype(BF16)
     hidden_ref[...] = hidden
     store_rows(reply_ref, dot(pick_ref[...], hidden).astype(BF16))
 
 
 def own_two_kernel(
-    members, weight_hbm, hidden_ref, near_ref, far_ref, count_ref, pos_ref, asked_ref,
-    sum_ref, own_ref, far_moved_ref, count_moved_ref, place_ref, held, sems,
+    members, weight_hbm, later_hbm, pos_hbm, hidden_ref, near_ref, far_ref, count_ref, asked_ref,
+    sum_ref, own_ref, far_moved_ref, count_moved_ref, place_ref, later_ref, held, pos_ref, sems,
 ):
-    copies = fetches(weight_hbm, held, sems)
-    for copy in copies:
+    copies = fetches(weight_hbm, held, sems.at[pl.ds(0, 1)])
+    later = pltpu.make_async_copy(later_hbm.at[pl.ds(0, later_ref.shape[0])], later_ref, sems.at[1])
+    taken = pltpu.make_async_copy(pos_hbm, pos_ref, sems.at[2])
+    for copy in (taken, *copies, later):
         copy.start()
     rows = hidden_ref.shape[0]
     capacity = 2 * rows // members
@@ -217,6 +233,7 @@
     rank = line - step * capacity
     target = me + 2 * step
     target = jnp.where(target >= members, target - members, target)
+    taken.wait()
     goes = target == divide(pos_ref[...], rows) - first
     prefix = earlier(rows)
     before = dot(bits(goes).astype(BF16), prefix).astype(I32)
@@ -224,7 +241,7 @@
     hidden = hidden_ref[...]
     sum_ref[...] = dot(dot(move, near_ref[...]).astype(BF16), hidden)
     far_moved_ref[...] = dot(move, far_ref[...]).astype(BF16)
-    count_moved_ref[...] = dot(move, count_ref[...].astype(BF16))
+    count_moved_ref[...] = dot(move, count_ref[...]).astype(BF16)
     own_ref[...] = dot_fetched(dot(move, hidden).astype(BF16), held, copies)
     place = jnp.zeros((rows, rows), F32)
     for q in range(members // 2):
@@ -237,16 +254,13 @@
         comes = bits(valid & (step == q) & (before == rank)).astype(BF16)
         place += dot_lanes(lands, comes)
     place_ref[...] = place.astype(BF16)
-
-
-def layer_two_kernel(weight_hbm, answer_ref, far_ref, sum_ref, own_ref, count_ref, *refs):
+    later.wait()
+
+
+def layer_two_kernel(weight_hbm, weight_ref, answer_ref, far_ref, sum_ref, own_ref, count_ref, *refs):
     final_refs, held, sems = refs[:-2], refs[-2], refs[-1]
-    copies = fetches(weight_hbm, held, sems)
-    for copy in copies:
-        copy.start()
-    summed = sum_ref[...] + dot(far_ref[...], load_rows(answer_ref))
-    mean = (summed / count_ref[:, :1]).astype(BF16)
-    final = (own_ref[...] + dot_fetched(mean, held, copies)).astype(BF16)
+    final = mean_product(weight_hbm, weight_ref, held, sems, answer_ref, far_ref, sum_ref, own_ref, count_ref)
+    final = final.astype(BF16)
     capacity = final_refs[0].shape[0]
     for q, ref in enumerate(final_refs):
         ref[...] = final[q * capacity : (q + 1) * capacity]
@@ -266,38 +280,41 @@
     steps = members // 2
     capacity = rows // steps
     size = peers * CAP
+    ready, ready_two = width_in * 2 // 3, width * 3 // 4
     shape = jax.ShapeDtypeStruct
     copies = pltpu.SemaphoreType.DMA
 
-    ask, key, local, span, pos = call(
+    pos = layer2_position.reshape(1, rows)
+    ask, key, local, span = call(
         functools.partial(ask_kernel, members, peers),
         (
             shape((peers, 1, rows), I32),
             shape((degree, rows), I32),
             shape((degree, rows), I32),
             shape((2, peers, rows), I32),
-            shape((1, rows), I32),
         ),
-        (neighbours.T, neighbour_mask.T, layer2_position.reshape(1, rows)),
+        (neighbours.T, neighbour_mask.T, pos),
         (),
-        [pltpu.VMEM((degree, rows), I32), pltpu.VMEM((degree, rows), I32), copies((3,))],
+        [pltpu.VMEM((degree, rows), I32), pltpu.VMEM((degree, rows), I32), pltpu.VMEM((1, rows), I32), copies((3,))],
         2 * peers * rows * rows,
         "ask",
     )
     asked = lax.all_to_all(ask, BOTH, 0, 0, tiled=True)
-    near, far, order, count, sum_one, own_one = call(
+    near, far, order, count, sum_one, own_one, features, weight = call(
         functools.partial(plan_kernel, peers, degree),
         (
             shape((rows, rows), BF16),
             shape((rows, size), BF16),
             shape((size, size), BF16),
-            shape((rows, rows), F32),
+            shape((rows, rows), BF16),
             shape((rows, width_in), F32),
             shape((rows, width), F32),
+            shape((rows, width_in), BF16),
+            shape((ready, width), BF16),
         ),
-        (self_weight1,),
-        (key, local, span, features),
-        [pltpu.VMEM((width_in, width), BF16), copies((1,))],
+        (features, self_weight1, neigh_weight1),
+        (key, local, span),
+        [pltpu.VMEM((width_in, width), BF16), copies((3,))],
         2 * rows * width_in * (rows + width),
         "plan",
         limit=40 << 20,
@@ -316,24 +333,25 @@
         layer_one_kernel,
         (shape((rows, width), BF16), shape((peers, CAP // 2, 2, width), BF16)),
         (neigh_weight1,),
-        (answer, far, sum_one, own_one, count, pick),
-        [pltpu.VMEM((width_in, width), BF16), copies((3,))],
+        (weight, answer, far, sum_one, own_one, count, pick),
+        [pltpu.VMEM((width_in - ready, width), BF16), copies((1,))],
         2 * rows * width_in * (size + width) + 2 * size * rows * width,
         "layer_one",
     )
     answer_two = lax.all_to_all(reply_two, BOTH, 0, 0, tiled=True)
-    sum_two, own_two, far_moved, count_moved, place = call(
+    sum_two, own_two, far_moved, count_moved, place, weight = call(
         functools.partial(own_two_kernel, members),
         (
             shape((rows, width), F32),
             shape((rows, width), F32),
             shape((rows, size), BF16),
-            shape((rows, rows), F32),
             shape((rows, rows), BF16),
+            shape((rows, rows), BF16),
+            shape((ready_two, width), BF16),
         ),
-        (self_weight2,),
-        (hidden, near, far, count, pos, asked),
-        [pltpu.VMEM((width, width), BF16), copies((1,))],
+        (self_weight2, neigh_weight2, pos),
+        (hidden, near, far, count, asked),
+        [pltpu.VMEM((width, width), BF16), pltpu.VMEM((1, rows), I32), copies((3,))],
         2 * rows * width * (2 * rows + width),
         "own_two",
     )
@@ -341,8 +359,8 @@
         layer_two_kernel,
         tuple(shape((capacity, width), BF16) for _ in range(steps)),
         (neigh_weight2,),
-        (answer_two, far_moved, sum_two, own_two, count_moved),
-        [pltpu.VMEM((width, width), BF16), copies((4,))],
+        (weight, answer_two, far_moved, sum_two, own_two, count_moved),
+        [pltpu.VMEM((width - ready_two, width), BF16), copies((1,))],
         2 * rows * width * (size + width),
         "layer_two",
     )

time: 61.8 us -> 59.5 us (0.963)
  local copies, waits for them, and re-layouts: 1.85 us -> 0 us
  Pallas kernels: 12.9 us -> 11.3 us
  waiting for transfers between devices: 19.6 us -> 20.9 us
    unnamed x4 -> x0, local copies, waits for them, and re-layouts: 1.85 us -> none
    pallas_call x7, Pallas kernels: 12.9 us -> 11.3 us  [call(): pl.pallas_call(kernel, out_shape=outs, in_specs=far_off(len(remote)) + ne...]
    all_to_all x1, waiting for transfers between devices: 4.12 us -> 5.08 us  [body(): asked = lax.all_to_all(ask, BOTH, 0, 0, tiled=True)]
  transfers between devices with their start and end apart: 5 -> 5, of which waited for: 4 -> 4; matrix products, arithmetic and copies ran while one was open for 0% -> 0% of each run, Pallas kernels for 8% -> 7%
where the time goes in v3:
time: 59.5 us; the launch traced here: 59.1 us
  waiting for transfers between devices  20.9 us (35%)
  starting transfers between devices  13.8 us (23%)
  blocking collectives  13 us (22%)
  Pallas kernels  11.3 us (19%)
    all_to_all x1, blocking collectives, body(): answer = lax.all_to_all(reply, BOTH, 0, 0, tiled=True)  13 us
    pallas_call x7, Pallas kernels, call(): pl.pallas_call(kernel, out_shape=outs, in_specs=far_off(len(remote)) + ne...  11.3 us
    all_to_all x1, waiting for transfers between devices, body(): answer_two = lax.all_to_all(reply_two, BOTH, 0, 0, tiled=True)  11 us
    all_to_all x1, starting transfers between devices, body(): asked = lax.all_to_all(ask, BOTH, 0, 0, tiled=True)  7.33 us
    all_to_all x1, waiting for transfers between devices, body(): asked = lax.all_to_all(ask, BOTH, 0, 0, tiled=True)  5.08 us
    ppermute x3, waiting for transfers between devices, body(): lax.ppermute(finals[q], 'dev', [(i, (i + 2 * q) % members) for i in range...  4.8 us
    ppermute x3, starting transfers between devices, body(): lax.ppermute(finals[q], 'dev', [(i, (i + 2 * q) % members) for i in range...  3.87 us
    all_to_all x1, starting transfers between devices, body(): answer_two = lax.all_to_all(reply_two, BOTH, 0, 0, tiled=True)  2.61 us
  transfers between devices with their start and end apart: 5, of which 4 were waited for; matrix products, arithmetic and copies ran while one was open for 0% of the time, Pallas kernels for 7%

profile of v3, /device:TPU:0, one launch (start us, length us, event | category | flops | bytes accessed | tf_op | source)
XLA Modules:
  0.0 59.1 jit_solution(429233015908567915)
XLA Ops:
  0.0 1.7 %ask.1 = (s32[32,1,128]{2,1,0:T(1,128)}, s32[25,128]{1,0:T(8,128)S(1)}, s32[25,128]{1,0:T(8,128)S(1)}, s32[2,32,128]{2,1,0:T(8,128)S(1)}) custom-call(s32[25,128]{1,0:T(8,128)} %bitcast.3, s32[25,128]{1,0:T(8,128)} %bitcast.4, s32[1,128]{1,0:T(1,128)} %bitcast.5), custom_call_target="tpu_custom_call" | custom-call | flops 1048576 | bytes 100864 | tf_op jit(solution)/shard_map/ask/pallas_call | solution.py:55
  1.7 7.3 %all-to-all-start = ((s32[32,1,128]{2,1,0:T(1,128)}), s32[32,1,128]{2,1,0:T(1,128)S(1)}, u32[]{:S(2)}, u32[]{:S(2)}) async-start(s32[32,1,128]{2,1,0:T(1,128)} %get-tuple-element.35), calls=%async_computation | async-start | bytes 32768 | tf_op jit(solution)/shard_map/all_to_all | solution.py:302
  9.1 2.0 %plan.1 = (bf16[128,128]{1,0:T(8,128)(2,1)S(1)}, bf16[128,192]{1,0:T(8,128)(2,1)S(1)}, bf16[192,192]{1,0:T(8,128)(2,1)S(1)}, bf16[128,128]{1,0:T(8,128)(2,1)S(1)...) custom-call(bf16[128,768]{1,0:T(8,128)(2,1)} %features_hbm.1, ...), custom_call_target="tpu_custom_call" | custom-call | flops 226492416 | bytes 5751808 | tf_op jit(solution)/shard_map/plan/pallas_call | solution.py:55
  11.1 5.1 %all-to-all-done.asked_ref = s32[32,1,128]{2,1,0:T(1,128)S(1)} async-done(((s32[32,1,128]{2,1,0:T(1,128)}), s32[32,1,128]{2,1,0:T(1,128)S(1)}, u32[]{:S(2)}, u32[]{:S(2)}) %all-to-all-start) | async-done | bytes 16416 | tf_op jit(solution)/shard_map/all_to_all | solution.py:302
  16.2 0.6 %serve.1 = (bf16[32,3,2,768]{3,2,1,0:T(2,128)(2,1)S(1)}, bf16[192,128]{1,0:T(8,128)(2,1)S(1)}) custom-call(s32[32,1,128]{2,1,0:T(1,128)S(1)} %all-to-all-done.asked_ref, bf16[192,192]{1,0:T(8,128)(2,1)S(1)} %get-tuple-element.36.order_ref, bf16[128,768]{1,0:T(8,128)(2,1)S(1)} %get-tuple-element.37.source_ref), custom_call_target="tpu_custom_call" | custom-call | flops 37748736 | bytes 630784 | tf_op jit(solution)/shard_map/serve/pallas_call | solution.py:55
  16.8 13.0 %all_to_all.15.answer_ref = bf16[32,3,2,768]{3,2,1,0:T(2,128)(2,1)S(1)} all-to-all(bf16[32,3,2,768]{3,2,1,0:T(2,128)(2,1)S(1)} %get-tuple-element.38), channel_id=1, replica_groups=mesh['grp'=4,'dev'=8] {'grp','dev'}, dimensions={0} | all-to-all | bytes 589824 | tf_op jit(solution)/shard_map/all_to_all | solution.py:331
  29.9 2.3 %layer_one.1 = (bf16[128,1024]{1,0:T(8,128)(2,1)S(1)}, bf16[32,3,2,1024]{3,2,1,0:T(2,128)(2,1)}) custom-call(bf16[768,1024]{1,0:T(8,128)(2,1)} %weight_hbm.5, bf16[512,1024]{1,0:T(8,128)(2,1)S(1)} %get-tuple-element.34.weight_ref, bf16[32,3,2,768]{3,2,1,0:T(2,128)(2,1)S(1)} %all_to_all.15.answer_ref, bf16[128,192]{1,0:T(8,128)(2,1)S(1)} %get-tuple-element.39.far_ref, ...), custom_call_target="tpu_custom_call" | custom-call | flops 289406976 | bytes 4620288 | tf_op jit(solution)/shard_map/layer_one/pallas_call | solution.py:55
  32.2 2.6 %all-to-all-start.2 = ((bf16[32,3,2,1024]{3,2,1,0:T(2,128)(2,1)}), bf16[32,3,2,1024]{3,2,1,0:T(2,128)(2,1)S(1)}, u32[]{:S(2)}, u32[]{:S(2)}) async-start(bf16[32,3,2,1024]{3,2,1,0:T(2,128)(2,1)} %get-tuple-element.48), calls=%async_computation.2 | async-start | bytes 786432 | tf_op jit(solution)/shard_map/all_to_all | solution.py:341
  34.8 2.4 %own_two.1 = (f32[128,1024]{1,0:T(8,128)S(1)}, f32[128,1024]{1,0:T(8,128)S(1)}, bf16[128,192]{1,0:T(8,128)(2,1)S(1)}, bf16[128,128]{1,0:T(8,128)(2,1)S(1)}, bf16...) custom-call(bf16[1024,1024]{1,0:T(8,128)(2,1)} %weight_hbm.6, bf16[1024,1024]{1,0:T(8,128)(2,1)} %weight_hbm.7, ...), custom_call_target="tpu_custom_call" | custom-call | flops 335544320 | bytes 7324160 | tf_op jit(solution)/shard_map/own_two/pallas_call | solution.py:55
  37.2 11.0 %all-to-all-done.2.answer_ref = bf16[32,3,2,1024]{3,2,1,0:T(2,128)(2,1)S(1)} async-done(((bf16[32,3,2,1024]{3,2,1,0:T(2,128)(2,1)}), bf16[32,3,2,1024]{3,2,1,0:T(2,128)(2,1)S(1)}, u32[]{:S(2)}, u32[]{:S(2)}) %all-to-all-start.2) | async-done | bytes 393248 | tf_op jit(solution)/shard_map/all_to_all | solution.py:341
  48.2 1.3 %layer_two.1 = (bf16[32,1024]{1,0:T(8,128)(2,1)S(1)}, bf16[32,1024]{1,0:T(8,128)(2,1)S(1)}, bf16[32,1024]{1,0:T(8,128)(2,1)S(1)}, bf16[32,1024]{1,0:T(8,128)(2,1)S(1)}) custom-call(bf16[1024,1024]{1,0:T(8,128)(2,1)} %weight_hbm.7, bf16[768,1024]{1,0:T(8,128)(2,1)S(1)} %get-tuple-element.47.weight_ref, ...), custom_call_target="tpu_custom_call" | custom-call | flops 318767104 | bytes 5455872 | tf_op jit(solution)/shard_map/layer_two/pallas_call | solution.py:55
  49.5 0.1 collective-permute-start
  49.6 0.3 collective-permute-start.1
  49.9 3.5 %collective-permute-start.2 = (bf16[32,1024]{1,0:T(8,128)(2,1)S(1)}, bf16[32,1024]{1,0:T(8,128)(2,1)S(1)}, u32[]{:S(2)}, u32[]{:S(2)}) collective-permute-start(bf16[32,1024]{1,0:T(8,128)(2,1)S(1)} %get-tuple-element.56), channel_id=1, source_target_pairs={{0,6},{1,7},{2,0},{3,1},{4,2},{5,3},{6,4},{7,5},{8,14},{9,15},{10,... | collective-permute-start | bytes 196616 | tf_op jit(solution)/shard_map/ppermute | solution.py:369
  53.4 3.0 %collective-permute-done.refs_1_ = bf16[32,1024]{1,0:T(8,128)(2,1)S(1)} collective-permute-done((bf16[32,1024]{1,0:T(8,128)(2,1)S(1)}, bf16[32,1024]{1,0:T(8,128)(2,1)S(1)}, u32[]{:S(2)}, u32[]{:S(2)}) %collective-permute-start) | collective-permute-done | bytes 65568 | tf_op jit(solution)/shard_map/ppermute | solution.py:369
  56.4 1.8 %collective-permute-done.1.refs_2_ = bf16[32,1024]{1,0:T(8,128)(2,1)S(1)} collective-permute-done((bf16[32,1024]{1,0:T(8,128)(2,1)S(1)}, bf16[32,1024]{1,0:T(8,128)(2,1)S(1)}, u32[]{:S(2)}, u32[]{:S(2)}) %collective-permute-start.1) | collective-permute-done | bytes 65568 | tf_op jit(solution)/shard_map/ppermute | solution.py:369
  58.2 0.0 collective-permute-done.2.refs_3_
  58.2 0.9 %scatter.1 = bf16[128,1024]{1,0:T(8,128)(2,1)} custom-call(bf16[128,128]{1,0:T(8,128)(2,1)S(1)} %get-tuple-element.46.place_ref, bf16[32,1024]{1,0:T(8,128)(2,1)S(1)} %get-tuple-element.53.refs_0_, bf16[32,1024]{1,0:T(8,128)(2,1)S(1)} %collective-permute-done.refs_1_, bf16[32,1024]{1,0:T(8,128)(2,1)S(1)} %collective-permute-done.1.refs_2_, ...), custom_call_target="tpu_custom_call" | custom-call | flops 33554432 | bytes 557056 | tf_op jit(solution)/shard_map/scatter/pallas_call | solution.py:55
Async XLA Ops:
  1.7 14.4 %all-to-all-start = ((s32[32,1,128]{2,1,0:T(1,128)}), s32[32,1,128]{2,1,0:T(1,128)S(1)}, u32[]{:S(2)}, u32[]{:S(2)}) async-start(s32[32,1,128]{2,1,0:T(1,128)} %get-tuple-element.35), calls=%async_computation | async-start | bytes 32768 | tf_op jit(solution)/shard_map/all_to_all | solution.py:302
  32.2 16.0 %all-to-all-start.2 = ((bf16[32,3,2,1024]{3,2,1,0:T(2,128)(2,1)}), bf16[32,3,2,1024]{3,2,1,0:T(2,128)(2,1)S(1)}, u32[]{:S(2)}, u32[]{:S(2)}) async-start(bf16[32,3,2,1024]{3,2,1,0:T(2,128)(2,1)} %get-tuple-element.48), calls=%async_computation.2 | async-start | bytes 786432 | tf_op jit(solution)/shard_map/all_to_all | solution.py:341
  49.5 6.9 %collective-permute-start = (bf16[32,1024]{1,0:T(8,128)(2,1)S(1)}, bf16[32,1024]{1,0:T(8,128)(2,1)S(1)}, u32[]{:S(2)}, u32[]{:S(2)}) collective-permute-start(bf16[32,1024]{1,0:T(8,128)(2,1)S(1)} %get-tuple-element.54), channel_id=1, source_target_pairs={{0,2},{1,3},{2,4},{3,5},{4,6},{5,7},{6,0},{7,1},{8,10},{9,11},{10,... | collective-permute-start | bytes 196616 | tf_op jit(solution)/shard_map/ppermute | solution.py:369
  49.6 8.6 %collective-permute-start.1 = (bf16[32,1024]{1,0:T(8,128)(2,1)S(1)}, bf16[32,1024]{1,0:T(8,128)(2,1)S(1)}, u32[]{:S(2)}, u32[]{:S(2)}) collective-permute-start(bf16[32,1024]{1,0:T(8,128)(2,1)S(1)} %get-tuple-element.55), channel_id=1, source_target_pairs={{0,4},{1,5},{2,6},{3,7},{4,0},{5,1},{6,2},{7,3},{8,12},{9,13},{10,... | collective-permute-start | bytes 196616 | tf_op jit(solution)/shard_map/ppermute | solution.py:369
  49.9 8.3 %collective-permute-start.2 = (bf16[32,1024]{1,0:T(8,128)(2,1)S(1)}, bf16[32,1024]{1,0:T(8,128)(2,1)S(1)}, u32[]{:S(2)}, u32[]{:S(2)}) collective-permute-start(bf16[32,1024]{1,0:T(8,128)(2,1)S(1)} %get-tuple-element.56), channel_id=1, source_target_pairs={{0,6},{1,7},{2,0},{3,1},{4,2},{5,3},{6,4},{7,5},{8,14},{9,15},{10,... | collective-permute-start | bytes 196616 | tf_op jit(solution)/shard_map/ppermute | solution.py:369

commit v4 on v3

--- a/solution.py
+++ b/solution.py
@@ -141,7 +141,7 @@
 
 def plan_kernel(
     peers, degree, features_hbm, weight_hbm, later_hbm, key_ref, local_ref, span_ref,
-    near_ref, far_ref, order_ref, count_ref, sum_ref, own_ref, features_ref, later_ref, held, sems,
+    near_ref, far_ref, order_ref, own_ref, features_ref, later_ref, held, sems,
 ):
     taken = pltpu.make_async_copy(features_hbm, features_ref, sems.at[1])
     later = pltpu.make_async_copy(later_hbm.at[pl.ds(0, later_ref.shape[0])], later_ref, sems.at[2])
@@ -164,13 +164,12 @@
     peer = divide(line, CAP)
     order = bits(iota((size, size), 1) == (line - peer * CAP) * peers + peer).astype(BF16)
     order_ref[...] = order
-    far_ref[...] = dot(order, far).T.astype(BF16)
+    far_ref[:, :size] = dot(order, far).T.astype(BF16)
     live = bits((local >= 0) | (key_ref[...] >= 0))
-    count_ref[...] = jnp.broadcast_to(jnp.sum(live, axis=0, keepdims=True), (rows, rows)).T.astype(BF16)
+    count = jnp.broadcast_to(jnp.sum(live, axis=0, keepdims=True), (rows, rows)).T.astype(BF16)
+    far_ref[:, size:] = count[:, : far_ref.shape[1] - size]
     taken.wait()
-    features = features_ref[...]
-    sum_ref[...] = dot(near, features)
-    own_ref[...] = dot_fetched(features, held, copies)
+    own_ref[...] = dot_fetched(features_ref[...], held, copies)
     later.wait()
 
 
@@ -195,29 +194,26 @@
     store_rows(reply_ref, dot(pick, source_ref[...]).astype(BF16))
 
 
-def mean_product(weight_hbm, weight_ref, held, sems, answer_ref, far_ref, sum_ref, own_ref, count_ref):
-    ready = weight_ref.shape[0]
-    rest = pltpu.make_async_copy(weight_hbm.at[pl.ds(ready, held.shape[0])], held, sems.at[0])
-    rest.start()
-    summed = sum_ref[...] + dot(far_ref[...], load_rows(answer_ref))
-    mean = (summed / count_ref[:, :1].astype(F32)).astype(BF16)
-    result = own_ref[...] + dot(mean[:, :ready], weight_ref[...])
-    rest.wait()
-    return result + dot(mean[:, ready:], held[...])
+def mean_product(weight_ref, table_ref, near_ref, answer_ref, far_ref, own_ref):
+    answer = load_rows(answer_ref)
+    size = answer.shape[0]
+    summed = dot(near_ref[...], table_ref[...]) + dot(far_ref[:, :size], answer)
+    mean = (summed / far_ref[:, size : size + 1].astype(F32)).astype(BF16)
+    return own_ref[...] + dot(mean, weight_ref[...])
 
 
 def layer_one_kernel(
-    weight_hbm, weight_ref, answer_ref, far_ref, sum_ref, own_ref, count_ref, pick_ref, hidden_ref, reply_ref, held, sems
+    weight_ref, features_ref, near_ref, answer_ref, far_ref, own_ref, pick_ref, hidden_ref, reply_ref
 ):
-    hidden = mean_product(weight_hbm, weight_ref, held, sems, answer_ref, far_ref, sum_ref, own_ref, count_ref)
+    hidden = mean_product(weight_ref, features_ref, near_ref, answer_ref, far_ref, own_ref)
     hidden = jnp.maximum(hidden, 0.0).astype(BF16)
     hidden_ref[...] = hidden
     store_rows(reply_ref, dot(pick_ref[...], hidden).astype(BF16))
 
 
 def own_two_kernel(
-    members, weight_hbm, later_hbm, pos_hbm, hidden_ref, near_ref, far_ref, count_ref, asked_ref,
-    sum_ref, own_ref, far_moved_ref, count_moved_ref, place_ref, later_ref, held, pos_ref, sems,
+    members, weight_hbm, later_hbm, pos_hbm, hidden_ref, near_ref, far_ref, asked_ref,
+    own_ref, near_moved_ref, far_moved_ref, place_ref, later_ref, held, pos_ref, sems,
 ):
     copies = fetches(weight_hbm, held, sems.at[pl.ds(0, 1)])
     later = pltpu.make_async_copy(later_hbm.at[pl.ds(0, later_ref.shape[0])], later_ref, sems.at[1])
@@ -239,9 +235,8 @@
     before = dot(bits(goes).astype(BF16), prefix).astype(I32)
     move = bits(goes & (before == rank)).astype(BF16)
     hidden = hidden_ref[...]
-    sum_ref[...] = dot(dot(move, near_ref[...]).astype(BF16), hidden)
+    near_moved_ref[...] = dot(move, near_ref[...]).astype(BF16)
     far_moved_ref[...] = dot(move, far_ref[...]).astype(BF16)
-    count_moved_ref[...] = dot(move, count_ref[...]).astype(BF16)
     own_ref[...] = dot_fetched(dot(move, hidden).astype(BF16), held, copies)
     place = jnp.zeros((rows, rows), F32)
     for q in range(members // 2):
@@ -257,10 +252,8 @@
     later.wait()
 
 
-def layer_two_kernel(weight_hbm, weight_ref, answer_ref, far_ref, sum_ref, own_ref, count_ref, *refs):
-    final_refs, held, sems = refs[:-2], refs[-2], refs[-1]
-    final = mean_product(weight_hbm, weight_ref, held, sems, answer_ref, far_ref, sum_ref, own_ref, count_ref)
-    final = final.astype(BF16)
+def layer_two_kernel(weight_ref, hidden_ref, near_ref, answer_ref, far_ref, own_ref, *final_refs):
+    final = mean_product(weight_ref, hidden_ref, near_ref, answer_ref, far_ref, own_ref).astype(BF16)
     capacity = final_refs[0].shape[0]
     for q, ref in enumerate(final_refs):
         ref[...] = final[q * capacity : (q + 1) * capacity]
@@ -280,7 +273,6 @@
     steps = members // 2
     capacity = rows // steps
     size = peers * CAP
-    ready, ready_two = width_in * 2 // 3, width * 3 // 4
     shape = jax.ShapeDtypeStruct
     copies = pltpu.SemaphoreType.DMA
 
@@ -300,17 +292,15 @@
         "ask",
     )
     asked = lax.all_to_all(ask, BOTH, 0, 0, tiled=True)
-    near, far, order, count, sum_one, own_one, features, weight = call(
+    near, far, order, own_one, features, weight = call(
         functools.partial(plan_kernel, peers, degree),
         (
             shape((rows, rows), BF16),
-            shape((rows, size), BF16),
+            shape((rows, size + 8), BF16),
             shape((size, size), BF16),
-            shape((rows, rows), BF16),
-            shape((rows, width_in), F32),
             shape((rows, width), F32),
             shape((rows, width_in), BF16),
-            shape((ready, width), BF16),
+            shape((width_in, width), BF16),
         ),
         (features, self_weight1, neigh_weight1),
         (key, local, span),
@@ -332,25 +322,24 @@
     hidden, reply_two = call(
         layer_one_kernel,
         (shape((rows, width), BF16), shape((peers, CAP // 2, 2, width), BF16)),
-        (neigh_weight1,),
-        (weight, answer, far, sum_one, own_one, count, pick),
-        [pltpu.VMEM((width_in - ready, width), BF16), copies((1,))],
+        (),
+        (weight, features, near, answer, far, own_one, pick),
+        [],
         2 * rows * width_in * (size + width) + 2 * size * rows * width,
         "layer_one",
     )
     answer_two = lax.all_to_all(reply_two, BOTH, 0, 0, tiled=True)
-    sum_two, own_two, far_moved, count_moved, place, weight = call(
+    own_two, near_moved, far_moved, place, weight = call(
         functools.partial(own_two_kernel, members),
         (
             shape((rows, width), F32),
-            shape((rows, width), F32),
-            shape((rows, size), BF16),
             shape((rows, rows), BF16),
+            shape((rows, size + 8), BF16),
             shape((rows, rows), BF16),
-            shape((ready_two, width), BF16),
+            shape((width, width), BF16),
         ),
         (self_weight2, neigh_weight2, pos),
-        (hidden, near, far, count, asked),
+        (hidden, near, far, asked),
         [pltpu.VMEM((width, width), BF16), pltpu.VMEM((1, rows), I32), copies((3,))],
         2 * rows * width * (2 * rows + width),
         "own_two",
@@ -358,9 +347,9 @@
     finals = call(
         layer_two_kernel,
         tuple(shape((capacity, width), BF16) for _ in range(steps)),
-        (neigh_weight2,),
-        (weight, answer_two, far_moved, sum_two, own_two, count_moved),
-        [pltpu.VMEM((width - ready_two, width), BF16), copies((1,))],
+        (),
+        (weight, hidden, near_moved, answer_two, far_moved, own_two),
+        [],
         2 * rows * width * (size + width),
         "layer_two",
     )

time: 59.5 us -> 58 us (0.975)
  Pallas kernels: 11.3 us -> 9.88 us
    pallas_call x7, Pallas kernels: 11.3 us -> 9.88 us  [call(): pl.pallas_call(kernel, out_shape=outs, in_specs=far_off(len(remote)) + ne...]
  transfers between devices with their start and end apart: 5 -> 5, of which waited for: 4 -> 4; matrix products, arithmetic and copies ran while one was open for 0% -> 0% of each run, Pallas kernels for 7% -> 8%
where the time goes in v4:
time: 58 us; the launch traced here: 57.7 us
  waiting for transfers between devices  20.9 us (36%)
  starting transfers between devices  13.8 us (24%)
  blocking collectives  13 us (22%)
  Pallas kernels  9.88 us (17%)
    all_to_all x1, blocking collectives, body(): answer = lax.all_to_all(reply, BOTH, 0, 0, tiled=True)  13 us
    all_to_all x1, waiting for transfers between devices, body(): answer_two = lax.all_to_all(reply_two, BOTH, 0, 0, tiled=True)  11 us
    pallas_call x7, Pallas kernels, call(): pl.pallas_call(kernel, out_shape=outs, in_specs=far_off(len(remote)) + ne...  9.88 us
    all_to_all x1, starting transfers between devices, body(): asked = lax.all_to_all(ask, BOTH, 0, 0, tiled=True)  7.33 us
    all_to_all x1, waiting for transfers between devices, body(): asked = lax.all_to_all(ask, BOTH, 0, 0, tiled=True)  5.06 us
    ppermute x3, waiting for transfers between devices, body(): lax.ppermute(finals[q], 'dev', [(i, (i + 2 * q) % members) for i in range...  4.8 us
    ppermute x3, starting transfers between devices, body(): lax.ppermute(finals[q], 'dev', [(i, (i + 2 * q) % members) for i in range...  3.87 us
    all_to_all x1, starting transfers between devices, body(): answer_two = lax.all_to_all(reply_two, BOTH, 0, 0, tiled=True)  2.59 us
  transfers between devices with their start and end apart: 5, of which 4 were waited for; matrix products, arithmetic and copies ran while one was open for 0% of the time, Pallas kernels for 8%

profile of v4, /device:TPU:0, one launch (start us, length us, event | category | flops | bytes accessed | tf_op | source)
XLA Modules:
  0.0 57.7 jit_solution(7656876621583671418)
XLA Ops:
  0.0 1.7 %ask.1 = (s32[32,1,128]{2,1,0:T(1,128)}, s32[25,128]{1,0:T(8,128)S(1)}, s32[25,128]{1,0:T(8,128)S(1)}, s32[2,32,128]{2,1,0:T(8,128)S(1)}) custom-call(s32[25,128]{1,0:T(8,128)} %bitcast.3, s32[25,128]{1,0:T(8,128)} %bitcast.4, s32[1,128]{1,0:T(1,128)} %bitcast.5), custom_call_target="tpu_custom_call" | custom-call | flops 1048576 | bytes 100864 | tf_op jit(solution)/shard_map/ask/pallas_call | solution.py:55
  1.7 7.3 %all-to-all-start = ((s32[32,1,128]{2,1,0:T(1,128)}), s32[32,1,128]{2,1,0:T(1,128)S(1)}, u32[]{:S(2)}, u32[]{:S(2)}) async-start(s32[32,1,128]{2,1,0:T(1,128)} %get-tuple-element.34), calls=%async_computation | async-start | bytes 32768 | tf_op jit(solution)/shard_map/all_to_all | solution.py:294
  9.1 2.0 %plan.1 = (bf16[128,128]{1,0:T(8,128)(2,1)S(1)}, bf16[128,200]{1,0:T(8,128)(2,1)S(1)}, bf16[192,192]{1,0:T(8,128)(2,1)S(1)}, f32[128,1024]{1,0:T(8,128)S(1)}, bf...) custom-call(bf16[128,768]{1,0:T(8,128)(2,1)} %features_hbm.1, bf16[768,1024]{1,0:T(8,128)(2,1)} %weight_hbm.2, ...), custom_call_target="tpu_custom_call" | custom-call | flops 226492416 | bytes 5852160 | tf_op jit(solution)/shard_map/plan/pallas_call | solution.py:55
  11.1 5.1 %all-to-all-done.asked_ref = s32[32,1,128]{2,1,0:T(1,128)S(1)} async-done(((s32[32,1,128]{2,1,0:T(1,128)}), s32[32,1,128]{2,1,0:T(1,128)S(1)}, u32[]{:S(2)}, u32[]{:S(2)}) %all-to-all-start) | async-done | bytes 16416 | tf_op jit(solution)/shard_map/all_to_all | solution.py:294
  16.2 0.6 %serve.1 = (bf16[32,3,2,768]{3,2,1,0:T(2,128)(2,1)S(1)}, bf16[192,128]{1,0:T(8,128)(2,1)S(1)}) custom-call(s32[32,1,128]{2,1,0:T(1,128)S(1)} %all-to-all-done.asked_ref, bf16[192,192]{1,0:T(8,128)(2,1)S(1)} %get-tuple-element.35.order_ref, bf16[128,768]{1,0:T(8,128)(2,1)S(1)} %get-tuple-element.32.source_ref.features_ref), custom_call_target="tpu_custom_call" | custom-call | flops 37748736 | bytes 630784 | tf_op jit(solution)/shard_map/serve/pallas_call | solution.py:55
  16.8 13.0 %all_to_all.15.answer_ref = bf16[32,3,2,768]{3,2,1,0:T(2,128)(2,1)S(1)} all-to-all(bf16[32,3,2,768]{3,2,1,0:T(2,128)(2,1)S(1)} %get-tuple-element.36), channel_id=1, replica_groups=mesh['grp'=4,'dev'=8] {'grp','dev'}, dimensions={0} | all-to-all | bytes 589824 | tf_op jit(solution)/shard_map/all_to_all | solution.py:321
  29.9 1.5 %layer_one.1 = (bf16[128,1024]{1,0:T(8,128)(2,1)S(1)}, bf16[32,3,2,1024]{3,2,1,0:T(2,128)(2,1)}) custom-call(bf16[768,1024]{1,0:T(8,128)(2,1)S(1)} %get-tuple-element.31.weight_ref, bf16[128,768]{1,0:T(8,128)(2,1)S(1)} %get-tuple-element.32.source_ref.features_ref, bf16[128,128]{1,0:T(8,128)(2,1)S(1)} %get-tuple-element.33.near_ref, ...), custom_call_target="tpu_custom_call" | custom-call | flops 289406976 | bytes 3377152 | tf_op jit(solution)/shard_map/layer_one/pallas_call | solution.py:55
  31.4 2.6 %all-to-all-start.2 = ((bf16[32,3,2,1024]{3,2,1,0:T(2,128)(2,1)}), bf16[32,3,2,1024]{3,2,1,0:T(2,128)(2,1)S(1)}, u32[]{:S(2)}, u32[]{:S(2)}) async-start(bf16[32,3,2,1024]{3,2,1,0:T(2,128)(2,1)} %get-tuple-element.44), calls=%async_computation.2 | async-start | bytes 786432 | tf_op jit(solution)/shard_map/all_to_all | solution.py:331
  34.0 2.4 %own_two.1 = (f32[128,1024]{1,0:T(8,128)S(1)}, bf16[128,128]{1,0:T(8,128)(2,1)S(1)}, bf16[128,200]{1,0:T(8,128)(2,1)S(1)}, bf16[128,128]{1,0:T(8,128)(2,1)S(1)}, bf16[1024,1024]{1,0:T(8,128)(2,1)S(1)}) custom-call(bf16[1024,1024]{1,0:T(8,128)(2,1)} %weight_hbm.3, bf16[1024,1024]{1,0:T(8,128)(2,1)} %later_hbm.3, s32[1,128]{1,0:T(1,128)} %bitcast.6, ...), custom_call_target="tpu_custom_call" | custom-call | flops 335544320 | bytes 7295488 | tf_op jit(solution)/shard_map/own_two/pallas_call | solution.py:55
  36.4 11.0 %all-to-all-done.2.answer_ref = bf16[32,3,2,1024]{3,2,1,0:T(2,128)(2,1)S(1)} async-done(((bf16[32,3,2,1024]{3,2,1,0:T(2,128)(2,1)}), bf16[32,3,2,1024]{3,2,1,0:T(2,128)(2,1)S(1)}, u32[]{:S(2)}, u32[]{:S(2)}) %all-to-all-start.2) | async-done | bytes 393248 | tf_op jit(solution)/shard_map/all_to_all | solution.py:331
  47.4 0.7 %layer_two.1 = (bf16[32,1024]{1,0:T(8,128)(2,1)S(1)}, bf16[32,1024]{1,0:T(8,128)(2,1)S(1)}, bf16[32,1024]{1,0:T(8,128)(2,1)S(1)}, bf16[32,1024]{1,0:T(8,128)(2,1)S(1)}) custom-call(bf16[1024,1024]{1,0:T(8,128)(2,1)S(1)} %get-tuple-element.42.weight_ref, bf16[128,1024]{1,0:T(8,128)(2,1)S(1)} %get-tuple-element.40.hidden_ref, ...), custom_call_target="tpu_custom_call" | custom-call | flops 318767104 | bytes 3622912 | tf_op jit(solution)/shard_map/layer_two/pallas_call | solution.py:55
  48.1 0.1 collective-permute-start
  48.1 0.3 collective-permute-start.1
  48.4 3.5 %collective-permute-start.2 = (bf16[32,1024]{1,0:T(8,128)(2,1)S(1)}, bf16[32,1024]{1,0:T(8,128)(2,1)S(1)}, u32[]{:S(2)}, u32[]{:S(2)}) collective-permute-start(bf16[32,1024]{1,0:T(8,128)(2,1)S(1)} %get-tuple-element.50), channel_id=1, source_target_pairs={{0,6},{1,7},{2,0},{3,1},{4,2},{5,3},{6,4},{7,5},{8,14},{9,15},{10,... | collective-permute-start | bytes 196616 | tf_op jit(solution)/shard_map/ppermute | solution.py:358
  52.0 3.0 %collective-permute-done.refs_1_ = bf16[32,1024]{1,0:T(8,128)(2,1)S(1)} collective-permute-done((bf16[32,1024]{1,0:T(8,128)(2,1)S(1)}, bf16[32,1024]{1,0:T(8,128)(2,1)S(1)}, u32[]{:S(2)}, u32[]{:S(2)}) %collective-permute-start) | collective-permute-done | bytes 65568 | tf_op jit(solution)/shard_map/ppermute | solution.py:358
  54.9 1.8 %collective-permute-done.1.refs_2_ = bf16[32,1024]{1,0:T(8,128)(2,1)S(1)} collective-permute-done((bf16[32,1024]{1,0:T(8,128)(2,1)S(1)}, bf16[32,1024]{1,0:T(8,128)(2,1)S(1)}, u32[]{:S(2)}, u32[]{:S(2)}) %collective-permute-start.1) | collective-permute-done | bytes 65568 | tf_op jit(solution)/shard_map/ppermute | solution.py:358
  56.8 0.0 collective-permute-done.2.refs_3_
  56.8 0.9 %scatter.1 = bf16[128,1024]{1,0:T(8,128)(2,1)} custom-call(bf16[128,128]{1,0:T(8,128)(2,1)S(1)} %get-tuple-element.41.place_ref, bf16[32,1024]{1,0:T(8,128)(2,1)S(1)} %get-tuple-element.47.refs_0_, bf16[32,1024]{1,0:T(8,128)(2,1)S(1)} %collective-permute-done.refs_1_, bf16[32,1024]{1,0:T(8,128)(2,1)S(1)} %collective-permute-done.1.refs_2_, ...), custom_call_target="tpu_custom_call" | custom-call | flops 33554432 | bytes 557056 | tf_op jit(solution)/shard_map/scatter/pallas_call | solution.py:55
Async XLA Ops:
  1.7 14.4 %all-to-all-start = ((s32[32,1,128]{2,1,0:T(1,128)}), s32[32,1,128]{2,1,0:T(1,128)S(1)}, u32[]{:S(2)}, u32[]{:S(2)}) async-start(s32[32,1,128]{2,1,0:T(1,128)} %get-tuple-element.34), calls=%async_computation | async-start | bytes 32768 | tf_op jit(solution)/shard_map/all_to_all | solution.py:294
  31.4 16.0 %all-to-all-start.2 = ((bf16[32,3,2,1024]{3,2,1,0:T(2,128)(2,1)}), bf16[32,3,2,1024]{3,2,1,0:T(2,128)(2,1)S(1)}, u32[]{:S(2)}, u32[]{:S(2)}) async-start(bf16[32,3,2,1024]{3,2,1,0:T(2,128)(2,1)} %get-tuple-element.44), calls=%async_computation.2 | async-start | bytes 786432 | tf_op jit(solution)/shard_map/all_to_all | solution.py:331
  48.1 6.9 %collective-permute-start = (bf16[32,1024]{1,0:T(8,128)(2,1)S(1)}, bf16[32,1024]{1,0:T(8,128)(2,1)S(1)}, u32[]{:S(2)}, u32[]{:S(2)}) collective-permute-start(bf16[32,1024]{1,0:T(8,128)(2,1)S(1)} %get-tuple-element.48), channel_id=1, source_target_pairs={{0,2},{1,3},{2,4},{3,5},{4,6},{5,7},{6,0},{7,1},{8,10},{9,11},{10,... | collective-permute-start | bytes 196616 | tf_op jit(solution)/shard_map/ppermute | solution.py:358
  48.1 8.6 %collective-permute-start.1 = (bf16[32,1024]{1,0:T(8,128)(2,1)S(1)}, bf16[32,1024]{1,0:T(8,128)(2,1)S(1)}, u32[]{:S(2)}, u32[]{:S(2)}) collective-permute-start(bf16[32,1024]{1,0:T(8,128)(2,1)S(1)} %get-tuple-element.49), channel_id=1, source_target_pairs={{0,4},{1,5},{2,6},{3,7},{4,0},{5,1},{6,2},{7,3},{8,12},{9,13},{10,... | collective-permute-start | bytes 196616 | tf_op jit(solution)/shard_map/ppermute | solution.py:358
  48.4 8.3 %collective-permute-start.2 = (bf16[32,1024]{1,0:T(8,128)(2,1)S(1)}, bf16[32,1024]{1,0:T(8,128)(2,1)S(1)}, u32[]{:S(2)}, u32[]{:S(2)}) collective-permute-start(bf16[32,1024]{1,0:T(8,128)(2,1)S(1)} %get-tuple-element.50), channel_id=1, source_target_pairs={{0,6},{1,7},{2,0},{3,1},{4,2},{5,3},{6,4},{7,5},{8,14},{9,15},{10,... | collective-permute-start | bytes 196616 | tf_op jit(solution)/shard_map/ppermute | solution.py:358

commit v5 on v4

--- a/solution.py
+++ b/solution.py
@@ -48,15 +48,15 @@
     return [pl.BlockSpec(memory_space=pltpu.HBM)] * n
 
 
-def call(kernel, outs, remote, operands, scratch, flops, name, limit=24 << 20):
+def call(kernel, outs, remote, operands, scratch, flops, name, limit=24 << 20, away=0):
     single = not isinstance(outs, tuple)
     leaves = (outs,) if single else outs
     moved = sum(a.size * a.dtype.itemsize for a in (*remote, *operands, *leaves))
     return pl.pallas_call(
         kernel,
-        out_shape=outs,
+        out_shape=outs if single else (*(pltpu.HBM(a.shape, a.dtype) for a in leaves[:away]), *leaves[away:]),
         in_specs=far_off(len(remote)) + near_by(len(operands)),
-        out_specs=near_by(1)[0] if single else near_by(len(leaves)),
+        out_specs=near_by(1)[0] if single else far_off(away) + near_by(len(leaves) - away),
         scratch_shapes=scratch,
         compiler_params=pltpu.CompilerParams(vmem_limit_bytes=limit),
         cost_estimate=pl.CostEstimate(flops=flops, bytes_accessed=moved, transcendentals=0),
@@ -140,14 +140,10 @@
 
 
 def plan_kernel(
-    peers, degree, features_hbm, weight_hbm, later_hbm, key_ref, local_ref, span_ref,
-    near_ref, far_ref, order_ref, own_ref, features_ref, later_ref, held, sems,
+    peers, degree, features_hbm, key_ref, local_ref, span_ref, near_ref, far_ref, order_ref, features_ref, sems
 ):
-    taken = pltpu.make_async_copy(features_hbm, features_ref, sems.at[1])
-    later = pltpu.make_async_copy(later_hbm.at[pl.ds(0, later_ref.shape[0])], later_ref, sems.at[2])
-    copies = fetches(weight_hbm, held, sems.at[pl.ds(0, 1)])
-    for copy in (taken, *copies, later):
-        copy.start()
+    taken = pltpu.make_async_copy(features_hbm, features_ref, sems.at[0])
+    taken.start()
     rows = features_ref.shape[0]
     local = local_ref[...]
     node = iota((rows, rows), 0)
@@ -169,8 +165,6 @@
     count = jnp.broadcast_to(jnp.sum(live, axis=0, keepdims=True), (rows, rows)).T.astype(BF16)
     far_ref[:, size:] = count[:, : far_ref.shape[1] - size]
     taken.wait()
-    own_ref[...] = dot_fetched(features_ref[...], held, copies)
-    later.wait()
 
 
 def store_rows(reply_ref, rows):
@@ -194,33 +188,47 @@
     store_rows(reply_ref, dot(pick, source_ref[...]).astype(BF16))
 
 
-def mean_product(weight_ref, table_ref, near_ref, answer_ref, far_ref, own_ref):
-    answer = load_rows(answer_ref)
-    size = answer.shape[0]
-    summed = dot(near_ref[...], table_ref[...]) + dot(far_ref[:, :size], answer)
-    mean = (summed / far_ref[:, size : size + 1].astype(F32)).astype(BF16)
-    return own_ref[...] + dot(mean, weight_ref[...])
+def mean_of(near_ref, own, far_ref, other):
+    size = other.shape[0]
+    summed = dot(near_ref[...], own) + dot(far_ref[:, :size], other)
+    return (summed / far_ref[:, size : size + 1].astype(F32)).astype(BF16)
 
 
 def layer_one_kernel(
-    weight_ref, features_ref, near_ref, answer_ref, far_ref, own_ref, pick_ref, hidden_ref, reply_ref
+    features_ref, near_ref, answer_ref, far_ref, pick_ref, answer_hbm, mean_hbm, reply_ref, mean_ref, sems
 ):
-    hidden = mean_product(weight_ref, features_ref, near_ref, answer_ref, far_ref, own_ref)
-    hidden = jnp.maximum(hidden, 0.0).astype(BF16)
-    hidden_ref[...] = hidden
-    store_rows(reply_ref, dot(pick_ref[...], hidden).astype(BF16))
-
-
-def own_two_kernel(
-    members, weight_hbm, later_hbm, pos_hbm, hidden_ref, near_ref, far_ref, asked_ref,
-    own_ref, near_moved_ref, far_moved_ref, place_ref, later_ref, held, pos_ref, sems,
+    kept = pltpu.make_async_copy(answer_ref, answer_hbm, sems.at[0])
+    kept.start()
+    mean = mean_of(near_ref, features_ref[...], far_ref, load_rows(answer_ref))
+    mean_ref[...] = mean
+    saved = pltpu.make_async_copy(mean_ref, mean_hbm, sems.at[1])
+    saved.start()
+    store_rows(reply_ref, dot(pick_ref[...], mean).astype(BF16))
+    kept.wait()
+    saved.wait()
+
+
+def between_kernel(
+    members, self_one_hbm, neigh_one_hbm, self_two_hbm, neigh_two_hbm, pos_hbm, features_hbm, answer_hbm, mean_hbm,
+    near_ref, far_ref, asked_ref,
+    final_hbm, hidden_ref, base_ref, near_moved_ref, far_moved_ref, place_ref, neigh_one_ref, later_ref,
+    held_one, held_two, features_ref, answer_ref, mean_ref, final_ref, pos_ref, sems,
 ):
-    copies = fetches(weight_hbm, held, sems.at[pl.ds(0, 1)])
-    later = pltpu.make_async_copy(later_hbm.at[pl.ds(0, later_ref.shape[0])], later_ref, sems.at[1])
-    taken = pltpu.make_async_copy(pos_hbm, pos_ref, sems.at[2])
-    for copy in (taken, *copies, later):
+    copies = [
+        pltpu.make_async_copy(pos_hbm, pos_ref, sems.at[0]),
+        pltpu.make_async_copy(self_one_hbm, held_one, sems.at[1]),
+        pltpu.make_async_copy(neigh_one_hbm, neigh_one_ref, sems.at[2]),
+        pltpu.make_async_copy(self_two_hbm, held_two, sems.at[3]),
+        pltpu.make_async_copy(neigh_two_hbm.at[pl.ds(0, later_ref.shape[0])], later_ref, sems.at[4]),
+    ]
+    inputs = [
+        pltpu.make_async_copy(features_hbm, features_ref, sems.at[6]),
+        pltpu.make_async_copy(answer_hbm, answer_ref, sems.at[7]),
+        pltpu.make_async_copy(mean_hbm, mean_ref, sems.at[8]),
+    ]
+    for copy in (*inputs, *copies):
         copy.start()
-    rows = hidden_ref.shape[0]
+    rows = features_ref.shape[0]
     capacity = 2 * rows // members
     me = lax.axis_index("dev")
     first = lax.axis_index("grp") * members
@@ -229,15 +237,13 @@
     rank = line - step * capacity
     target = me + 2 * step
     target = jnp.where(target >= members, target - members, target)
-    taken.wait()
+    prefix = earlier(rows)
+    copies[0].wait()
     goes = target == divide(pos_ref[...], rows) - first
-    prefix = earlier(rows)
     before = dot(bits(goes).astype(BF16), prefix).astype(I32)
     move = bits(goes & (before == rank)).astype(BF16)
-    hidden = hidden_ref[...]
     near_moved_ref[...] = dot(move, near_ref[...]).astype(BF16)
     far_moved_ref[...] = dot(move, far_ref[...]).astype(BF16)
-    own_ref[...] = dot_fetched(dot(move, hidden).astype(BF16), held, copies)
     place = jnp.zeros((rows, rows), F32)
     for q in range(members // 2):
         source = me - 2 * q
@@ -249,13 +255,38 @@
         comes = bits(valid & (step == q) & (before == rank)).astype(BF16)
         place += dot_lanes(lands, comes)
     place_ref[...] = place.astype(BF16)
-    later.wait()
-
-
-def layer_two_kernel(weight_ref, hidden_ref, near_ref, answer_ref, far_ref, own_ref, *final_refs):
-    final = mean_product(weight_ref, hidden_ref, near_ref, answer_ref, far_ref, own_ref).astype(BF16)
-    capacity = final_refs[0].shape[0]
-    for q, ref in enumerate(final_refs):
+    for copy in (*inputs, copies[1]):
+        copy.wait()
+    own = dot(features_ref[...], held_one[...])
+    base_ref[...] = dot(load_rows(answer_ref), held_one[...]).astype(BF16)
+    copies[2].wait()
+    hidden = jnp.maximum(own + dot(mean_ref[...], neigh_one_ref[...]), 0.0).astype(BF16)
+    hidden_ref[...] = hidden
+    moved = dot(move, hidden).astype(BF16)
+    copies[3].wait()
+    final_ref[...] = dot(moved, held_two[...])
+    away = pltpu.make_async_copy(final_ref, final_hbm, sems.at[5])
+    away.start()
+    copies[4].wait()
+    away.wait()
+
+
+def layer_two_kernel(
+    neigh_two_hbm, final_hbm, neigh_one_ref, ready_ref, base_ref, hidden_ref, near_ref, answer_ref, far_ref, *refs
+):
+    outs, held, final_ref, sems = refs[:-3], refs[-3], refs[-2], refs[-1]
+    ready = ready_ref.shape[0]
+    copies = fetches(neigh_two_hbm.at[pl.ds(ready, held.shape[0])], held, sems.at[pl.ds(0, sems.shape[0] - 1)])
+    last = pltpu.make_async_copy(final_hbm, final_ref, sems.at[sems.shape[0] - 1])
+    for copy in (*copies, last):
+        copy.start()
+    other = jnp.maximum(base_ref[...].astype(F32) + dot(load_rows(answer_ref), neigh_one_ref[...]), 0.0).astype(BF16)
+    mean = mean_of(near_ref, hidden_ref[...], far_ref, other)
+    final = dot(mean[:, :ready], ready_ref[...]) + dot_fetched(mean[:, ready:], held, copies)
+    last.wait()
+    final = (final + final_ref[...]).astype(BF16)
+    capacity = outs[0].shape[0]
+    for q, ref in enumerate(outs):
         ref[...] = final[q * capacity : (q + 1) * capacity]
 
 
@@ -273,6 +304,7 @@
     steps = members // 2
     capacity = rows // steps
     size = peers * CAP
+    early = width // 4
     shape = jax.ShapeDtypeStruct
     copies = pltpu.SemaphoreType.DMA
 
@@ -292,20 +324,18 @@
         "ask",
     )
     asked = lax.all_to_all(ask, BOTH, 0, 0, tiled=True)
-    near, far, order, own_one, features, weight = call(
+    near, far, order, table = call(
         functools.partial(plan_kernel, peers, degree),
         (
             shape((rows, rows), BF16),
             shape((rows, size + 8), BF16),
             shape((size, size), BF16),
-            shape((rows, width), F32),
             shape((rows, width_in), BF16),
-            shape((width_in, width), BF16),
         ),
-        (features, self_weight1, neigh_weight1),
+        (features,),
         (key, local, span),
-        [pltpu.VMEM((width_in, width), BF16), copies((3,))],
-        2 * rows * width_in * (rows + width),
+        [copies((1,))],
+        2 * size * size * rows,
         "plan",
         limit=40 << 20,
     )
@@ -313,45 +343,65 @@
         serve_kernel,
         (shape((peers, CAP // 2, 2, width_in), BF16), shape((size, rows), BF16)),
         (),
-        (asked, order, features),
+        (asked, order, table),
         [],
         2 * size * rows * width_in,
         "serve",
     )
     answer = lax.all_to_all(reply, BOTH, 0, 0, tiled=True)
-    hidden, reply_two = call(
+    kept, mean, reply_two = call(
         layer_one_kernel,
-        (shape((rows, width), BF16), shape((peers, CAP // 2, 2, width), BF16)),
+        (
+            shape((peers, CAP // 2, 2, width_in), BF16),
+            shape((rows, width_in), BF16),
+            shape((peers, CAP // 2, 2, width_in), BF16),
+        ),
         (),
-        (weight, features, near, answer, far, own_one, pick),
-        [],
-        2 * rows * width_in * (size + width) + 2 * size * rows * width,
+        (table, near, answer, far, pick),
+        [pltpu.VMEM((rows, width_in), BF16), copies((2,))],
+        2 * rows * width_in * (size + rows) + 2 * size * rows * width_in,
         "layer_one",
+        away=2,
     )
     answer_two = lax.all_to_all(reply_two, BOTH, 0, 0, tiled=True)
-    own_two, near_moved, far_moved, place, weight = call(
-        functools.partial(own_two_kernel, members),
+    final, hidden, base, near_moved, far_moved, place, weight, ready = call(
+        functools.partial(between_kernel, members),
         (
             shape((rows, width), F32),
+            shape((rows, width), BF16),
+            shape((size, width), BF16),
             shape((rows, rows), BF16),
             shape((rows, size + 8), BF16),
             shape((rows, rows), BF16),
-            shape((width, width), BF16),
+            shape((width_in, width), BF16),
+            shape((early, width), BF16),
         ),
-        (self_weight2, neigh_weight2, pos),
-        (hidden, near, far, asked),
-        [pltpu.VMEM((width, width), BF16), pltpu.VMEM((1, rows), I32), copies((3,))],
-        2 * rows * width * (2 * rows + width),
-        "own_two",
+        (self_weight1, neigh_weight1, self_weight2, neigh_weight2, pos, features, kept, mean),
+        (near, far, asked),
+        [
+            pltpu.VMEM((width_in, width), BF16),
+            pltpu.VMEM((width, width), BF16),
+            pltpu.VMEM((rows, width_in), BF16),
+            pltpu.VMEM((peers, CAP // 2, 2, width_in), BF16),
+            pltpu.VMEM((rows, width_in), BF16),
+            pltpu.VMEM((rows, width), F32),
+            pltpu.VMEM((1, rows), I32),
+            copies((9,)),
+        ],
+        2 * width * (rows * (2 * width_in + rows + width) + size * width_in),
+        "between",
+        limit=48 << 20,
+        away=1,
     )
     finals = call(
         layer_two_kernel,
         tuple(shape((capacity, width), BF16) for _ in range(steps)),
-        (),
-        (weight, hidden, near_moved, answer_two, far_moved, own_two),
-        [],
-        2 * rows * width * (size + width),
+        (neigh_weight2, final),
+        (weight, ready, base, hidden, near_moved, answer_two, far_moved),
+        [pltpu.VMEM((width - early, width), BF16), pltpu.VMEM((rows, width), F32), copies((3,))],
+        2 * width * (size * width_in + rows * (size + rows + width)),
         "layer_two",
+        limit=48 << 20,
     )
     arrived = [finals[0]]
     for q in range(1, steps):

time: 58 us -> 57.9 us (level)
  waiting for transfers between devices: 20.9 us -> 17.9 us
  Pallas kernels: 9.88 us -> 12.8 us
    all_to_all x1, waiting for transfers between devices: 11 us -> 7 us  [body(): answer_two = lax.all_to_all(reply_two, BOTH, 0, 0, tiled=True)]
    pallas_call x7, Pallas kernels: 9.88 us -> 12.8 us  [call(): pl.pallas_call(kernel, out_shape=outs if single else (*(pltpu.HBM(a.shape...]
    all_to_all x1, waiting for transfers between devices: 5.06 us -> 6.09 us  [body(): asked = lax.all_to_all(ask, BOTH, 0, 0, tiled=True)]
  transfers between devices with their start and end apart: 5 -> 5, of which waited for: 4 -> 4; matrix products, arithmetic and copies ran while one was open for 0% -> 0% of each run, Pallas kernels for 8% -> 9%
where the time goes in v5:
time: 57.9 us; the launch traced here: 57.6 us
  waiting for transfers between devices  17.9 us (31%)
  starting transfers between devices  13.8 us (24%)
  blocking collectives  13 us (22%)
  Pallas kernels  12.8 us (22%)
    all_to_all x1, blocking collectives, body(): answer = lax.all_to_all(reply, BOTH, 0, 0, tiled=True)  13 us
    pallas_call x7, Pallas kernels, call(): pl.pallas_call(kernel, out_shape=outs if single else (*(pltpu.HBM(a.shape...  12.8 us
    all_to_all x1, starting transfers between devices, body(): asked = lax.all_to_all(ask, BOTH, 0, 0, tiled=True)  7.33 us
    all_to_all x1, waiting for transfers between devices, body(): answer_two = lax.all_to_all(reply_two, BOTH, 0, 0, tiled=True)  7 us
    all_to_all x1, waiting for transfers between devices, body(): asked = lax.all_to_all(ask, BOTH, 0, 0, tiled=True)  6.09 us
    ppermute x3, waiting for transfers between devices, body(): lax.ppermute(finals[q], 'dev', [(i, (i + 2 * q) % members) for i in range...  4.8 us
    ppermute x3, starting transfers between devices, body(): lax.ppermute(finals[q], 'dev', [(i, (i + 2 * q) % members) for i in range...  3.87 us
    all_to_all x1, starting transfers between devices, body(): answer_two = lax.all_to_all(reply_two, BOTH, 0, 0, tiled=True)  2.6 us
  transfers between devices with their start and end apart: 5, of which 4 were waited for; matrix products, arithmetic and copies ran while one was open for 0% of the time, Pallas kernels for 9%

profile of v5, /device:TPU:0, one launch (start us, length us, event | category | flops | bytes accessed | tf_op | source)
XLA Modules:
  0.0 57.6 jit_solution(1960698693568347863)
XLA Ops:
  0.0 1.7 %ask.1 = (s32[32,1,128]{2,1,0:T(1,128)}, s32[25,128]{1,0:T(8,128)S(1)}, s32[25,128]{1,0:T(8,128)S(1)}, s32[2,32,128]{2,1,0:T(8,128)S(1)}) custom-call(s32[25,128]{1,0:T(8,128)} %bitcast.3, s32[25,128]{1,0:T(8,128)} %bitcast.4, s32[1,128]{1,0:T(1,128)} %bitcast.5), custom_call_target="tpu_custom_call" | custom-call | flops 1048576 | bytes 100864 | tf_op jit(solution)/shard_map/ask/pallas_call | solution.py:55
  1.7 7.3 %all-to-all-start = ((s32[32,1,128]{2,1,0:T(1,128)}), s32[32,1,128]{2,1,0:T(1,128)S(1)}, u32[]{:S(2)}, u32[]{:S(2)}) async-start(s32[32,1,128]{2,1,0:T(1,128)} %get-tuple-element.35), calls=%async_computation | async-start | bytes 32768 | tf_op jit(solution)/shard_map/all_to_all | solution.py:326
  9.1 1.0 %plan.1 = (bf16[128,128]{1,0:T(8,128)(2,1)S(1)}, bf16[128,200]{1,0:T(8,128)(2,1)S(1)}, bf16[192,192]{1,0:T(8,128)(2,1)S(1)}, bf16[128,768]{1,0:T(8,128)(2,1)S(1)}) custom-call(bf16[128,768]{1,0:T(8,128)(2,1)} %features_hbm.3, s32[25,128]{1,0:T(8,128)S(1)} %get-tuple-element.30.key_ref, s32[25,128]{1,0:T(8,128)S(1)} %get-tuple-element.31.local_ref, ...), custom_call_target="tpu_custom_call" | custom-call | flops 9437184 | bytes 609280 | tf_op jit(solution)/shard_map/plan/pallas_call | solution.py:55
  10.1 6.1 %all-to-all-done.asked_ref = s32[32,1,128]{2,1,0:T(1,128)S(1)} async-done(((s32[32,1,128]{2,1,0:T(1,128)}), s32[32,1,128]{2,1,0:T(1,128)S(1)}, u32[]{:S(2)}, u32[]{:S(2)}) %all-to-all-start) | async-done | bytes 16416 | tf_op jit(solution)/shard_map/all_to_all | solution.py:326
  16.2 0.6 %serve.1 = (bf16[32,3,2,768]{3,2,1,0:T(2,128)(2,1)S(1)}, bf16[192,128]{1,0:T(8,128)(2,1)S(1)}) custom-call(s32[32,1,128]{2,1,0:T(1,128)S(1)} %all-to-all-done.asked_ref, bf16[192,192]{1,0:T(8,128)(2,1)S(1)} %get-tuple-element.36.order_ref, bf16[128,768]{1,0:T(8,128)(2,1)S(1)} %get-tuple-element.33.source_ref.features_ref), custom_call_target="tpu_custom_call" | custom-call | flops 37748736 | bytes 630784 | tf_op jit(solution)/shard_map/serve/pallas_call | solution.py:55
  16.8 13.0 %all_to_all.15.answer_ref = bf16[32,3,2,768]{3,2,1,0:T(2,128)(2,1)S(1)} all-to-all(bf16[32,3,2,768]{3,2,1,0:T(2,128)(2,1)S(1)} %get-tuple-element.37), channel_id=1, replica_groups=mesh['grp'=4,'dev'=8] {'grp','dev'}, dimensions={0} | all-to-all | bytes 589824 | tf_op jit(solution)/shard_map/all_to_all | solution.py:351
  29.9 1.7 %layer_one.1 = (bf16[32,3,2,768]{3,2,1,0:T(2,128)(2,1)}, bf16[128,768]{1,0:T(8,128)(2,1)}, bf16[32,3,2,768]{3,2,1,0:T(2,128)(2,1)}) custom-call(bf16[128,768]{1,0:T(8,128)(2,1)S(1)} %get-tuple-element.33.source_ref.features_ref, bf16[128,128]{1,0:T(8,128)(2,1)S(1)} %get-tuple-element.34.near_ref, bf16[32,3,2,768]{3,2,1,0:T(2,128)(2,1)S(1)} %all_to_all.15.answer_ref, ...), custom_call_target="tpu_custom_call" | custom-call | flops 100663296 | bytes 1411072 | tf_op jit(solution)/shard_map/layer_one/pallas_call | solution.py:55
  31.6 2.6 %all-to-all-start.2 = ((bf16[32,3,2,768]{3,2,1,0:T(2,128)(2,1)}), bf16[32,3,2,768]{3,2,1,0:T(2,128)(2,1)S(1)}, u32[]{:S(2)}, u32[]{:S(2)}) async-start(bf16[32,3,2,768]{3,2,1,0:T(2,128)(2,1)} %get-tuple-element.49), calls=%async_computation.2 | async-start | bytes 589824 | tf_op jit(solution)/shard_map/all_to_all | solution.py:366
  34.2 4.3 %between.1 = (f32[128,1024]{1,0:T(8,128)}, bf16[128,1024]{1,0:T(8,128)(2,1)S(1)}, bf16[192,1024]{1,0:T(8,128)(2,1)S(1)}, bf16[128,128]{1,0:T(8,128)(2,1)S(1)}, b...) custom-call(bf16[768,1024]{1,0:T(8,128)(2,1)} %self_one_hbm.1, ...), custom_call_target="tpu_custom_call" | custom-call | flops 1006632960 | bytes 11522560 | tf_op jit(solution)/shard_map/between/pallas_call | solution.py:55
  38.5 7.0 %all-to-all-done.2.answer_ref = bf16[32,3,2,768]{3,2,1,0:T(2,128)(2,1)S(1)} async-done(((bf16[32,3,2,768]{3,2,1,0:T(2,128)(2,1)}), bf16[32,3,2,768]{3,2,1,0:T(2,128)(2,1)S(1)}, u32[]{:S(2)}, u32[]{:S(2)}) %all-to-all-start.2) | async-done | bytes 294944 | tf_op jit(solution)/shard_map/all_to_all | solution.py:366
  45.5 2.5 %layer_two.1 = (bf16[32,1024]{1,0:T(8,128)(2,1)S(1)}, bf16[32,1024]{1,0:T(8,128)(2,1)S(1)}, bf16[32,1024]{1,0:T(8,128)(2,1)S(1)}, bf16[32,1024]{1,0:T(8,128)(2,1)S(1)}) custom-call(bf16[1024,1024]{1,0:T(8,128)(2,1)} %neigh_two_hbm.3, f32[128,1024]{1,0:T(8,128)} %get-tuple-element.43.final_hbm, bf16[768,1024]{1,0:T(8,128)(2,1)S(1)} %get-tuple-element.44.neigh_one_ref, ...), custom_call_target="tpu_custom_call" | custom-call | flops 654311424 | bytes 6014976 | tf_op jit(solution)/shard_map/layer_two/pallas_call | solution.py:55
  48.0 0.1 collective-permute-start
  48.1 0.3 collective-permute-start.1
  48.3 3.6 %collective-permute-start.2 = (bf16[32,1024]{1,0:T(8,128)(2,1)S(1)}, bf16[32,1024]{1,0:T(8,128)(2,1)S(1)}, u32[]{:S(2)}, u32[]{:S(2)}) collective-permute-start(bf16[32,1024]{1,0:T(8,128)(2,1)S(1)} %get-tuple-element.54), channel_id=1, source_target_pairs={{0,6},{1,7},{2,0},{3,1},{4,2},{5,3},{6,4},{7,5},{8,14},{9,15},{10,... | collective-permute-start | bytes 196616 | tf_op jit(solution)/shard_map/ppermute | solution.py:408
  51.9 3.0 %collective-permute-done.refs_1_ = bf16[32,1024]{1,0:T(8,128)(2,1)S(1)} collective-permute-done((bf16[32,1024]{1,0:T(8,128)(2,1)S(1)}, bf16[32,1024]{1,0:T(8,128)(2,1)S(1)}, u32[]{:S(2)}, u32[]{:S(2)}) %collective-permute-start) | collective-permute-done | bytes 65568 | tf_op jit(solution)/shard_map/ppermute | solution.py:408
  54.9 1.8 %collective-permute-done.1.refs_2_ = bf16[32,1024]{1,0:T(8,128)(2,1)S(1)} collective-permute-done((bf16[32,1024]{1,0:T(8,128)(2,1)S(1)}, bf16[32,1024]{1,0:T(8,128)(2,1)S(1)}, u32[]{:S(2)}, u32[]{:S(2)}) %collective-permute-start.1) | collective-permute-done | bytes 65568 | tf_op jit(solution)/shard_map/ppermute | solution.py:408
  56.7 0.0 collective-permute-done.2.refs_3_
  56.7 0.9 %scatter.1 = bf16[128,1024]{1,0:T(8,128)(2,1)} custom-call(bf16[128,128]{1,0:T(8,128)(2,1)S(1)} %get-tuple-element.42.place_ref, bf16[32,1024]{1,0:T(8,128)(2,1)S(1)} %get-tuple-element.51.refs_0_, bf16[32,1024]{1,0:T(8,128)(2,1)S(1)} %collective-permute-done.refs_1_, bf16[32,1024]{1,0:T(8,128)(2,1)S(1)} %collective-permute-done.1.refs_2_, ...), custom_call_target="tpu_custom_call" | custom-call | flops 33554432 | bytes 557056 | tf_op jit(solution)/shard_map/scatter/pallas_call | solution.py:55
Async XLA Ops:
  1.7 14.4 %all-to-all-start = ((s32[32,1,128]{2,1,0:T(1,128)}), s32[32,1,128]{2,1,0:T(1,128)S(1)}, u32[]{:S(2)}, u32[]{:S(2)}) async-start(s32[32,1,128]{2,1,0:T(1,128)} %get-tuple-element.35), calls=%async_computation | async-start | bytes 32768 | tf_op jit(solution)/shard_map/all_to_all | solution.py:326
  31.6 13.9 %all-to-all-start.2 = ((bf16[32,3,2,768]{3,2,1,0:T(2,128)(2,1)}), bf16[32,3,2,768]{3,2,1,0:T(2,128)(2,1)S(1)}, u32[]{:S(2)}, u32[]{:S(2)}) async-start(bf16[32,3,2,768]{3,2,1,0:T(2,128)(2,1)} %get-tuple-element.49), calls=%async_computation.2 | async-start | bytes 589824 | tf_op jit(solution)/shard_map/all_to_all | solution.py:366
  48.0 6.9 %collective-permute-start = (bf16[32,1024]{1,0:T(8,128)(2,1)S(1)}, bf16[32,1024]{1,0:T(8,128)(2,1)S(1)}, u32[]{:S(2)}, u32[]{:S(2)}) collective-permute-start(bf16[32,1024]{1,0:T(8,128)(2,1)S(1)} %get-tuple-element.52), channel_id=1, source_target_pairs={{0,2},{1,3},{2,4},{3,5},{4,6},{5,7},{6,0},{7,1},{8,10},{9,11},{10,... | collective-permute-start | bytes 196616 | tf_op jit(solution)/shard_map/ppermute | solution.py:408
  48.1 8.6 %collective-permute-start.1 = (bf16[32,1024]{1,0:T(8,128)(2,1)S(1)}, bf16[32,1024]{1,0:T(8,128)(2,1)S(1)}, u32[]{:S(2)}, u32[]{:S(2)}) collective-permute-start(bf16[32,1024]{1,0:T(8,128)(2,1)S(1)} %get-tuple-element.53), channel_id=1, source_target_pairs={{0,4},{1,5},{2,6},{3,7},{4,0},{5,1},{6,2},{7,3},{8,12},{9,13},{10,... | collective-permute-start | bytes 196616 | tf_op jit(solution)/shard_map/ppermute | solution.py:408
  48.3 8.4 %collective-permute-start.2 = (bf16[32,1024]{1,0:T(8,128)(2,1)S(1)}, bf16[32,1024]{1,0:T(8,128)(2,1)S(1)}, u32[]{:S(2)}, u32[]{:S(2)}) collective-permute-start(bf16[32,1024]{1,0:T(8,128)(2,1)S(1)} %get-tuple-element.54), channel_id=1, source_target_pairs={{0,6},{1,7},{2,0},{3,1},{4,2},{5,3},{6,4},{7,5},{8,14},{9,15},{10,... | collective-permute-start | bytes 196616 | tf_op jit(solution)/shard_map/ppermute | solution.py:408

commit v6 on v5

--- a/solution.py
+++ b/solution.py
@@ -188,10 +188,9 @@
     store_rows(reply_ref, dot(pick, source_ref[...]).astype(BF16))
 
 
-def mean_of(near_ref, own, far_ref, other):
-    size = other.shape[0]
-    summed = dot(near_ref[...], own) + dot(far_ref[:, :size], other)
-    return (summed / far_ref[:, size : size + 1].astype(F32)).astype(BF16)
+def over_count(summed, far):
+    size = far.shape[1] - 8
+    return (summed / far[:, size : size + 1].astype(F32)).astype(BF16)
 
 
 def layer_one_kernel(
@@ -199,7 +198,9 @@
 ):
     kept = pltpu.make_async_copy(answer_ref, answer_hbm, sems.at[0])
     kept.start()
-    mean = mean_of(near_ref, features_ref[...], far_ref, load_rows(answer_ref))
+    answer = load_rows(answer_ref)
+    far = far_ref[...]
+    mean = over_count(dot(near_ref[...], features_ref[...]) + dot(far[:, : answer.shape[0]], answer), far)
     mean_ref[...] = mean
     saved = pltpu.make_async_copy(mean_ref, mean_hbm, sems.at[1])
     saved.start()
@@ -211,15 +212,17 @@
 def between_kernel(
     members, self_one_hbm, neigh_one_hbm, self_two_hbm, neigh_two_hbm, pos_hbm, features_hbm, answer_hbm, mean_hbm,
     near_ref, far_ref, asked_ref,
-    final_hbm, hidden_ref, base_ref, near_moved_ref, far_moved_ref, place_ref, neigh_one_ref, later_ref,
-    held_one, held_two, features_ref, answer_ref, mean_ref, final_ref, pos_ref, sems,
+    final_hbm, place_hbm, base_ref, far_moved_ref, neigh_one_ref, ready_ref,
+    held_one, held_two, rest, features_ref, answer_ref, mean_ref, final_ref, place_ref, pos_ref, sems,
 ):
+    ready = ready_ref.shape[0]
     copies = [
         pltpu.make_async_copy(pos_hbm, pos_ref, sems.at[0]),
         pltpu.make_async_copy(self_one_hbm, held_one, sems.at[1]),
         pltpu.make_async_copy(neigh_one_hbm, neigh_one_ref, sems.at[2]),
         pltpu.make_async_copy(self_two_hbm, held_two, sems.at[3]),
-        pltpu.make_async_copy(neigh_two_hbm.at[pl.ds(0, later_ref.shape[0])], later_ref, sems.at[4]),
+        pltpu.make_async_copy(neigh_two_hbm.at[pl.ds(0, ready)], ready_ref, sems.at[4]),
+        pltpu.make_async_copy(neigh_two_hbm.at[pl.ds(ready, rest.shape[0])], rest, sems.at[5]),
     ]
     inputs = [
         pltpu.make_async_copy(features_hbm, features_ref, sems.at[6]),
@@ -242,8 +245,9 @@
     goes = target == divide(pos_ref[...], rows) - first
     before = dot(bits(goes).astype(BF16), prefix).astype(I32)
     move = bits(goes & (before == rank)).astype(BF16)
-    near_moved_ref[...] = dot(move, near_ref[...]).astype(BF16)
-    far_moved_ref[...] = dot(move, far_ref[...]).astype(BF16)
+    near = dot(move, near_ref[...]).astype(BF16)
+    far = dot(move, far_ref[...]).astype(BF16)
+    far_moved_ref[...] = far
     place = jnp.zeros((rows, rows), F32)
     for q in range(members // 2):
         source = me - 2 * q
@@ -255,33 +259,39 @@
         comes = bits(valid & (step == q) & (before == rank)).astype(BF16)
         place += dot_lanes(lands, comes)
     place_ref[...] = place.astype(BF16)
+    placed = pltpu.make_async_copy(place_ref, place_hbm, sems.at[9])
+    placed.start()
     for copy in (*inputs, copies[1]):
         copy.wait()
     own = dot(features_ref[...], held_one[...])
     base_ref[...] = dot(load_rows(answer_ref), held_one[...]).astype(BF16)
     copies[2].wait()
     hidden = jnp.maximum(own + dot(mean_ref[...], neigh_one_ref[...]), 0.0).astype(BF16)
-    hidden_ref[...] = hidden
+    mean = over_count(dot(near, hidden), far)
     moved = dot(move, hidden).astype(BF16)
     copies[3].wait()
-    final_ref[...] = dot(moved, held_two[...])
-    away = pltpu.make_async_copy(final_ref, final_hbm, sems.at[5])
+    final = dot(moved, held_two[...])
+    copies[4].wait()
+    final += dot(mean[:, :ready], ready_ref[...])
+    copies[5].wait()
+    final_ref[...] = final + dot(mean[:, ready:], rest[...])
+    away = pltpu.make_async_copy(final_ref, final_hbm, sems.at[10])
     away.start()
-    copies[4].wait()
     away.wait()
-
-
-def layer_two_kernel(
-    neigh_two_hbm, final_hbm, neigh_one_ref, ready_ref, base_ref, hidden_ref, near_ref, answer_ref, far_ref, *refs
-):
+    placed.wait()
+
+
+def layer_two_kernel(neigh_two_hbm, final_hbm, neigh_one_ref, ready_ref, base_ref, answer_ref, far_ref, *refs):
     outs, held, final_ref, sems = refs[:-3], refs[-3], refs[-2], refs[-1]
     ready = ready_ref.shape[0]
-    copies = fetches(neigh_two_hbm.at[pl.ds(ready, held.shape[0])], held, sems.at[pl.ds(0, sems.shape[0] - 1)])
-    last = pltpu.make_async_copy(final_hbm, final_ref, sems.at[sems.shape[0] - 1])
+    pieces = sems.shape[0] - 1
+    copies = fetches(neigh_two_hbm.at[pl.ds(ready, held.shape[0])], held, sems.at[pl.ds(0, pieces)])
+    last = pltpu.make_async_copy(final_hbm, final_ref, sems.at[pieces])
     for copy in (*copies, last):
         copy.start()
+    far = far_ref[...]
     other = jnp.maximum(base_ref[...].astype(F32) + dot(load_rows(answer_ref), neigh_one_ref[...]), 0.0).astype(BF16)
-    mean = mean_of(near_ref, hidden_ref[...], far_ref, other)
+    mean = over_count(dot(far[:, : other.shape[0]], other), far)
     final = dot(mean[:, :ready], ready_ref[...]) + dot_fetched(mean[:, ready:], held, copies)
     last.wait()
     final = (final + final_ref[...]).astype(BF16)
@@ -304,7 +314,7 @@
     steps = members // 2
     capacity = rows // steps
     size = peers * CAP
-    early = width // 4
+    early = width // 2
     shape = jax.ShapeDtypeStruct
     copies = pltpu.SemaphoreType.DMA
 
@@ -364,15 +374,13 @@
         away=2,
     )
     answer_two = lax.all_to_all(reply_two, BOTH, 0, 0, tiled=True)
-    final, hidden, base, near_moved, far_moved, place, weight, ready = call(
+    final, place, base, far_moved, weight, ready = call(
         functools.partial(between_kernel, members),
         (
             shape((rows, width), F32),
-            shape((rows, width), BF16),
+            shape((rows, rows), BF16),
             shape((size, width), BF16),
-            shape((rows, rows), BF16),
             shape((rows, size + 8), BF16),
-            shape((rows, rows), BF16),
             shape((width_in, width), BF16),
             shape((early, width), BF16),
         ),
@@ -381,25 +389,27 @@
         [
             pltpu.VMEM((width_in, width), BF16),
             pltpu.VMEM((width, width), BF16),
+            pltpu.VMEM((width - early, width), BF16),
             pltpu.VMEM((rows, width_in), BF16),
             pltpu.VMEM((peers, CAP // 2, 2, width_in), BF16),
             pltpu.VMEM((rows, width_in), BF16),
             pltpu.VMEM((rows, width), F32),
+            pltpu.VMEM((rows, rows), BF16),
             pltpu.VMEM((1, rows), I32),
-            copies((9,)),
+            copies((11,)),
         ],
-        2 * width * (rows * (2 * width_in + rows + width) + size * width_in),
+        2 * width * (rows * (2 * width_in + rows + 2 * width) + size * width_in),
         "between",
         limit=48 << 20,
-        away=1,
+        away=2,
     )
     finals = call(
         layer_two_kernel,
         tuple(shape((capacity, width), BF16) for _ in range(steps)),
         (neigh_weight2, final),
-        (weight, ready, base, hidden, near_moved, answer_two, far_moved),
+        (weight, ready, base, answer_two, far_moved),
         [pltpu.VMEM((width - early, width), BF16), pltpu.VMEM((rows, width), F32), copies((3,))],
-        2 * width * (size * width_in + rows * (size + rows + width)),
+        2 * width * (size * width_in + rows * (size + width)),
         "layer_two",
         limit=48 << 20,
     )

time: 57.9 us -> 57.7 us (level)
  waiting for transfers between devices: 17.9 us -> 17.3 us
  transfers between devices with their start and end apart: 5 -> 5, of which waited for: 4 -> 4; matrix products, arithmetic and copies ran while one was open for 0% -> 0% of each run, Pallas kernels for 9% -> 10%
where the time goes in v6:
time: 57.7 us; the launch traced here: 57.3 us
  waiting for transfers between devices  17.3 us (30%)
  starting transfers between devices  13.8 us (24%)
  Pallas kernels  13.1 us (23%)
  blocking collectives  13 us (23%)
    pallas_call x7, Pallas kernels, call(): pl.pallas_call(kernel, out_shape=outs if single else (*(pltpu.HBM(a.shape...  13.1 us
    all_to_all x1, blocking collectives, body(): answer = lax.all_to_all(reply, BOTH, 0, 0, tiled=True)  13 us
    all_to_all x1, starting transfers between devices, body(): asked = lax.all_to_all(ask, BOTH, 0, 0, tiled=True)  7.33 us
    all_to_all x1, waiting for transfers between devices, body(): answer_two = lax.all_to_all(reply_two, BOTH, 0, 0, tiled=True)  6.42 us
    all_to_all x1, waiting for transfers between devices, body(): asked = lax.all_to_all(ask, BOTH, 0, 0, tiled=True)  6.09 us
    ppermute x3, waiting for transfers between devices, body(): lax.ppermute(finals[q], 'dev', [(i, (i + 2 * q) % members) for i in range...  4.8 us
    ppermute x3, starting transfers between devices, body(): lax.ppermute(finals[q], 'dev', [(i, (i + 2 * q) % members) for i in range...  3.87 us
    all_to_all x1, starting transfers between devices, body(): answer_two = lax.all_to_all(reply_two, BOTH, 0, 0, tiled=True)  2.6 us
  transfers between devices with their start and end apart: 5, of which 4 were waited for; matrix products, arithmetic and copies ran while one was open for 0% of the time, Pallas kernels for 10%

profile of v6, /device:TPU:0, one launch (start us, length us, event | category | flops | bytes accessed | tf_op | source)
XLA Modules:
  0.0 57.3 jit_solution(10022339948897234082)
XLA Ops:
  0.0 1.7 %ask.1 = (s32[32,1,128]{2,1,0:T(1,128)}, s32[25,128]{1,0:T(8,128)S(1)}, s32[25,128]{1,0:T(8,128)S(1)}, s32[2,32,128]{2,1,0:T(8,128)S(1)}) custom-call(s32[25,128]{1,0:T(8,128)} %bitcast.3, s32[25,128]{1,0:T(8,128)} %bitcast.4, s32[1,128]{1,0:T(1,128)} %bitcast.5), custom_call_target="tpu_custom_call" | custom-call | flops 1048576 | bytes 100864 | tf_op jit(solution)/shard_map/ask/pallas_call | solution.py:55
  1.7 7.3 %all-to-all-start = ((s32[32,1,128]{2,1,0:T(1,128)}), s32[32,1,128]{2,1,0:T(1,128)S(1)}, u32[]{:S(2)}, u32[]{:S(2)}) async-start(s32[32,1,128]{2,1,0:T(1,128)} %get-tuple-element.33), calls=%async_computation | async-start | bytes 32768 | tf_op jit(solution)/shard_map/all_to_all | solution.py:336
  9.1 1.0 %plan.1 = (bf16[128,128]{1,0:T(8,128)(2,1)S(1)}, bf16[128,200]{1,0:T(8,128)(2,1)S(1)}, bf16[192,192]{1,0:T(8,128)(2,1)S(1)}, bf16[128,768]{1,0:T(8,128)(2,1)S(1)}) custom-call(bf16[128,768]{1,0:T(8,128)(2,1)} %features_hbm.3, s32[25,128]{1,0:T(8,128)S(1)} %get-tuple-element.28.key_ref, s32[25,128]{1,0:T(8,128)S(1)} %get-tuple-element.29.local_ref, ...), custom_call_target="tpu_custom_call" | custom-call | flops 9437184 | bytes 609280 | tf_op jit(solution)/shard_map/plan/pallas_call | solution.py:55
  10.1 6.1 %all-to-all-done.asked_ref = s32[32,1,128]{2,1,0:T(1,128)S(1)} async-done(((s32[32,1,128]{2,1,0:T(1,128)}), s32[32,1,128]{2,1,0:T(1,128)S(1)}, u32[]{:S(2)}, u32[]{:S(2)}) %all-to-all-start) | async-done | bytes 16416 | tf_op jit(solution)/shard_map/all_to_all | solution.py:336
  16.2 0.6 %serve.1 = (bf16[32,3,2,768]{3,2,1,0:T(2,128)(2,1)S(1)}, bf16[192,128]{1,0:T(8,128)(2,1)S(1)}) custom-call(s32[32,1,128]{2,1,0:T(1,128)S(1)} %all-to-all-done.asked_ref, bf16[192,192]{1,0:T(8,128)(2,1)S(1)} %get-tuple-element.34.order_ref, bf16[128,768]{1,0:T(8,128)(2,1)S(1)} %get-tuple-element.31.source_ref.features_ref), custom_call_target="tpu_custom_call" | custom-call | flops 37748736 | bytes 630784 | tf_op jit(solution)/shard_map/serve/pallas_call | solution.py:55
  16.8 13.0 %all_to_all.15.answer_ref = bf16[32,3,2,768]{3,2,1,0:T(2,128)(2,1)S(1)} all-to-all(bf16[32,3,2,768]{3,2,1,0:T(2,128)(2,1)S(1)} %get-tuple-element.35), channel_id=1, replica_groups=mesh['grp'=4,'dev'=8] {'grp','dev'}, dimensions={0} | all-to-all | bytes 589824 | tf_op jit(solution)/shard_map/all_to_all | solution.py:361
  29.9 1.7 %layer_one.1 = (bf16[32,3,2,768]{3,2,1,0:T(2,128)(2,1)}, bf16[128,768]{1,0:T(8,128)(2,1)}, bf16[32,3,2,768]{3,2,1,0:T(2,128)(2,1)}) custom-call(bf16[128,768]{1,0:T(8,128)(2,1)S(1)} %get-tuple-element.31.source_ref.features_ref, bf16[128,128]{1,0:T(8,128)(2,1)S(1)} %get-tuple-element.32.near_ref, bf16[32,3,2,768]{3,2,1,0:T(2,128)(2,1)S(1)} %all_to_all.15.answer_ref, ...), custom_call_target="tpu_custom_call" | custom-call | flops 100663296 | bytes 1411072 | tf_op jit(solution)/shard_map/layer_one/pallas_call | solution.py:55
  31.6 2.6 %all-to-all-start.2 = ((bf16[32,3,2,768]{3,2,1,0:T(2,128)(2,1)}), bf16[32,3,2,768]{3,2,1,0:T(2,128)(2,1)S(1)}, u32[]{:S(2)}, u32[]{:S(2)}) async-start(bf16[32,3,2,768]{3,2,1,0:T(2,128)(2,1)} %get-tuple-element.45), calls=%async_computation.2 | async-start | bytes 589824 | tf_op jit(solution)/shard_map/all_to_all | solution.py:376
  34.2 4.9 %between.1 = (f32[128,1024]{1,0:T(8,128)}, bf16[128,128]{1,0:T(8,128)(2,1)}, bf16[192,1024]{1,0:T(8,128)(2,1)S(1)}, bf16[128,200]{1,0:T(8,128)(2,1)S(1)}, bf16[7...) custom-call(bf16[768,1024]{1,0:T(8,128)(2,1)} %self_one_hbm.1, bf16[768,1024]{1,0:T(8,128)(2,1)} %neigh_one_hbm.1, ...), custom_call_target="tpu_custom_call" | custom-call | flops 1275068416 | bytes 11751936 | tf_op jit(solution)/shard_map/between/pallas_call | solution.py:55
  39.1 6.4 %all-to-all-done.2.answer_ref = bf16[32,3,2,768]{3,2,1,0:T(2,128)(2,1)S(1)} async-done(((bf16[32,3,2,768]{3,2,1,0:T(2,128)(2,1)}), bf16[32,3,2,768]{3,2,1,0:T(2,128)(2,1)S(1)}, u32[]{:S(2)}, u32[]{:S(2)}) %all-to-all-start.2) | async-done | bytes 294944 | tf_op jit(solution)/shard_map/all_to_all | solution.py:376
  45.5 0.0 copy-start
  45.5 2.2 %layer_two.1 = (bf16[32,1024]{1,0:T(8,128)(2,1)S(1)}, bf16[32,1024]{1,0:T(8,128)(2,1)S(1)}, bf16[32,1024]{1,0:T(8,128)(2,1)S(1)}, bf16[32,1024]{1,0:T(8,128)(2,1)S(1)}) custom-call(bf16[1024,1024]{1,0:T(8,128)(2,1)} %neigh_two_hbm.3, f32[128,1024]{1,0:T(8,128)} %get-tuple-element.41.final_hbm, bf16[768,1024]{1,0:T(8,128)(2,1)S(1)} %get-tuple-element.42.neigh_one_ref, ...), custom_call_target="tpu_custom_call" | custom-call | flops 620756992 | bytes 6244352 | tf_op jit(solution)/shard_map/layer_two/pallas_call | solution.py:55
  47.7 0.1 collective-permute-start
  47.8 0.3 collective-permute-start.1
  48.0 3.6 %collective-permute-start.2 = (bf16[32,1024]{1,0:T(8,128)(2,1)S(1)}, bf16[32,1024]{1,0:T(8,128)(2,1)S(1)}, u32[]{:S(2)}, u32[]{:S(2)}) collective-permute-start(bf16[32,1024]{1,0:T(8,128)(2,1)S(1)} %get-tuple-element.50), channel_id=1, source_target_pairs={{0,6},{1,7},{2,0},{3,1},{4,2},{5,3},{6,4},{7,5},{8,14},{9,15},{10,... | collective-permute-start | bytes 196616 | tf_op jit(solution)/shard_map/ppermute | solution.py:418
  51.6 3.0 %collective-permute-done.refs_1_ = bf16[32,1024]{1,0:T(8,128)(2,1)S(1)} collective-permute-done((bf16[32,1024]{1,0:T(8,128)(2,1)S(1)}, bf16[32,1024]{1,0:T(8,128)(2,1)S(1)}, u32[]{:S(2)}, u32[]{:S(2)}) %collective-permute-start) | collective-permute-done | bytes 65568 | tf_op jit(solution)/shard_map/ppermute | solution.py:418
  54.6 1.8 %collective-permute-done.1.refs_2_ = bf16[32,1024]{1,0:T(8,128)(2,1)S(1)} collective-permute-done((bf16[32,1024]{1,0:T(8,128)(2,1)S(1)}, bf16[32,1024]{1,0:T(8,128)(2,1)S(1)}, u32[]{:S(2)}, u32[]{:S(2)}) %collective-permute-start.1) | collective-permute-done | bytes 65568 | tf_op jit(solution)/shard_map/ppermute | solution.py:418
  56.4 0.0 collective-permute-done.2.refs_3_
  56.4 0.0 copy-done
  56.4 0.9 %scatter.1 = bf16[128,1024]{1,0:T(8,128)(2,1)} custom-call(bf16[128,128]{1,0:T(8,128)(2,1)S(1)} %copy-done, bf16[32,1024]{1,0:T(8,128)(2,1)S(1)} %get-tuple-element.47.refs_0_, bf16[32,1024]{1,0:T(8,128)(2,1)S(1)} %collective-permute-done.refs_1_, bf16[32,1024]{1,0:T(8,128)(2,1)S(1)} %collective-permute-done.1.refs_2_, ...), custom_call_target="tpu_custom_call" | custom-call | flops 33554432 | bytes 557056 | tf_op jit(solution)/shard_map/scatter/pallas_call | solution.py:55
Async XLA Ops:
  1.7 14.4 %all-to-all-start = ((s32[32,1,128]{2,1,0:T(1,128)}), s32[32,1,128]{2,1,0:T(1,128)S(1)}, u32[]{:S(2)}, u32[]{:S(2)}) async-start(s32[32,1,128]{2,1,0:T(1,128)} %get-tuple-element.33), calls=%async_computation | async-start | bytes 32768 | tf_op jit(solution)/shard_map/all_to_all | solution.py:336
  31.6 13.9 %all-to-all-start.2 = ((bf16[32,3,2,768]{3,2,1,0:T(2,128)(2,1)}), bf16[32,3,2,768]{3,2,1,0:T(2,128)(2,1)S(1)}, u32[]{:S(2)}, u32[]{:S(2)}) async-start(bf16[32,3,2,768]{3,2,1,0:T(2,128)(2,1)} %get-tuple-element.45), calls=%async_computation.2 | async-start | bytes 589824 | tf_op jit(solution)/shard_map/all_to_all | solution.py:376
  45.5 10.9 %copy-start = (bf16[128,128]{1,0:T(8,128)(2,1)S(1)}, bf16[128,128]{1,0:T(8,128)(2,1)}, u32[]{:S(2)}) copy-start(bf16[128,128]{1,0:T(8,128)(2,1)} %get-tuple-element.40.place_ref) | copy-start | bytes 98308
  47.7 6.9 %collective-permute-start = (bf16[32,1024]{1,0:T(8,128)(2,1)S(1)}, bf16[32,1024]{1,0:T(8,128)(2,1)S(1)}, u32[]{:S(2)}, u32[]{:S(2)}) collective-permute-start(bf16[32,1024]{1,0:T(8,128)(2,1)S(1)} %get-tuple-element.48), channel_id=1, source_target_pairs={{0,2},{1,3},{2,4},{3,5},{4,6},{5,7},{6,0},{7,1},{8,10},{9,11},{10,... | collective-permute-start | bytes 196616 | tf_op jit(solution)/shard_map/ppermute | solution.py:418
  47.8 8.6 %collective-permute-start.1 = (bf16[32,1024]{1,0:T(8,128)(2,1)S(1)}, bf16[32,1024]{1,0:T(8,128)(2,1)S(1)}, u32[]{:S(2)}, u32[]{:S(2)}) collective-permute-start(bf16[32,1024]{1,0:T(8,128)(2,1)S(1)} %get-tuple-element.49), channel_id=1, source_target_pairs={{0,4},{1,5},{2,6},{3,7},{4,0},{5,1},{6,2},{7,3},{8,12},{9,13},{10,... | collective-permute-start | bytes 196616 | tf_op jit(solution)/shard_map/ppermute | solution.py:418
  48.0 8.3 %collective-permute-start.2 = (bf16[32,1024]{1,0:T(8,128)(2,1)S(1)}, bf16[32,1024]{1,0:T(8,128)(2,1)S(1)}, u32[]{:S(2)}, u32[]{:S(2)}) collective-permute-start(bf16[32,1024]{1,0:T(8,128)(2,1)S(1)} %get-tuple-element.50), channel_id=1, source_target_pairs={{0,6},{1,7},{2,0},{3,1},{4,2},{5,3},{6,4},{7,5},{8,14},{9,15},{10,... | collective-permute-start | bytes 196616 | tf_op jit(solution)/shard_map/ppermute | solution.py:418

commit v7 on v6

--- a/solution.py
+++ b/solution.py
@@ -85,14 +85,17 @@
     return result
 
 
-def ask_kernel(members, peers, ids_hbm, mask_hbm, pos_hbm, ask_ref, key_ref, local_ref, span_ref, ids, mask, pos_ref, sems):
+def ask_kernel(
+    members, peers, ids_hbm, mask_hbm, pos_hbm, features_hbm, ask_ref, near_ref, far_ref, order_ref, features_ref, ids, mask, pos_ref, sems
+):
     degree, rows = ids.shape
     copies = [
         pltpu.make_async_copy(ids_hbm, ids, sems.at[0]),
         pltpu.make_async_copy(mask_hbm, mask, sems.at[1]),
         pltpu.make_async_copy(pos_hbm, pos_ref, sems.at[2]),
     ]
-    for copy in copies:
+    table = pltpu.make_async_copy(features_hbm, features_ref, sems.at[3])
+    for copy in (*copies, table):
         copy.start()
     own = lax.axis_index("grp") * members + lax.axis_index("dev")
     peer = iota((peers, rows), 0)
@@ -133,38 +136,23 @@
     pos = pos_ref[...]
     place = jnp.where(divide(pos, rows) == peer, pos - divide(pos, rows) * rows + 1, 0)
     ask_ref[...] = (place + wanted * (2 * rows)).reshape(peers, 1, rows)
-    key_ref[...] = key
-    local_ref[...] = jnp.where(live & here, row, -1)
-    span_ref[0] = before
-    span_ref[1] = total
-
-
-def plan_kernel(
-    peers, degree, features_hbm, key_ref, local_ref, span_ref, near_ref, far_ref, order_ref, features_ref, sems
-):
-    taken = pltpu.make_async_copy(features_hbm, features_ref, sems.at[0])
-    taken.start()
-    rows = features_ref.shape[0]
-    local = local_ref[...]
+    local = jnp.where(live & here, row, -1)
     node = iota((rows, rows), 0)
     near = jnp.zeros((rows, rows), F32)
     for s in range(degree):
         near += bits(local[s : s + 1] == node)
-    near = near.T.astype(BF16)
-    near_ref[...] = near
-    before, total = span_ref[0], span_ref[1]
+    near_ref[...] = near.T.astype(BF16)
     far = [bits((before <= k) & (k < before + total)).astype(BF16) for k in range(CAP)]
     far = jnp.concatenate(far, axis=0)
     size = peers * CAP
     line = iota((size, size), 0)
-    peer = divide(line, CAP)
-    order = bits(iota((size, size), 1) == (line - peer * CAP) * peers + peer).astype(BF16)
+    device = divide(line, CAP)
+    order = bits(iota((size, size), 1) == (line - device * CAP) * peers + device).astype(BF16)
     order_ref[...] = order
     far_ref[:, :size] = dot(order, far).T.astype(BF16)
-    live = bits((local >= 0) | (key_ref[...] >= 0))
-    count = jnp.broadcast_to(jnp.sum(live, axis=0, keepdims=True), (rows, rows)).T.astype(BF16)
+    count = jnp.broadcast_to(jnp.sum(bits(live), axis=0, keepdims=True), (rows, rows)).T.astype(BF16)
     far_ref[:, size:] = count[:, : far_ref.shape[1] - size]
-    taken.wait()
+    table.wait()
 
 
 def store_rows(reply_ref, rows):
@@ -319,36 +307,23 @@
     copies = pltpu.SemaphoreType.DMA
 
     pos = layer2_position.reshape(1, rows)
-    ask, key, local, span = call(
+    ask, near, far, order, table = call(
         functools.partial(ask_kernel, members, peers),
         (
             shape((peers, 1, rows), I32),
-            shape((degree, rows), I32),
-            shape((degree, rows), I32),
-            shape((2, peers, rows), I32),
-        ),
-        (neighbours.T, neighbour_mask.T, pos),
-        (),
-        [pltpu.VMEM((degree, rows), I32), pltpu.VMEM((degree, rows), I32), pltpu.VMEM((1, rows), I32), copies((3,))],
-        2 * peers * rows * rows,
-        "ask",
-    )
-    asked = lax.all_to_all(ask, BOTH, 0, 0, tiled=True)
-    near, far, order, table = call(
-        functools.partial(plan_kernel, peers, degree),
-        (
             shape((rows, rows), BF16),
             shape((rows, size + 8), BF16),
             shape((size, size), BF16),
             shape((rows, width_in), BF16),
         ),
-        (features,),
-        (key, local, span),
-        [copies((1,))],
+        (neighbours.T, neighbour_mask.T, pos, features),
+        (),
+        [pltpu.VMEM((degree, rows), I32), pltpu.VMEM((degree, rows), I32), pltpu.VMEM((1, rows), I32), copies((4,))],
         2 * size * size * rows,
-        "plan",
+        "ask",
         limit=40 << 20,
     )
+    asked = lax.all_to_all(ask, BOTH, 0, 0, tiled=True)
     reply, pick = call(
         serve_kernel,
         (shape((peers, CAP // 2, 2, width_in), BF16), shape((size, rows), BF16)),

time: 57.7 us -> 57.2 us (level)
  blocking collectives: 13 us -> 27.3 us
  starting transfers between devices: 13.8 us -> 6.48 us
  waiting for transfers between devices: 17.3 us -> 11.2 us
  Pallas kernels: 13.1 us -> 11.8 us
    all_to_all x0 -> x1, blocking collectives: none -> 14.3 us  [body(): asked = lax.all_to_all(ask, BOTH, 0, 0, tiled=True)]
    all_to_all x1 -> x0, starting transfers between devices: 7.33 us -> none  [body(): asked = lax.all_to_all(ask, BOTH, 0, 0, tiled=True)]
    all_to_all x1 -> x0, waiting for transfers between devices: 6.09 us -> none  [body(): asked = lax.all_to_all(ask, BOTH, 0, 0, tiled=True)]
    pallas_call x7 -> x6, Pallas kernels: 13.1 us -> 11.8 us  [call(): pl.pallas_call(kernel, out_shape=outs if single else (*(pltpu.HBM(a.shape...]
  transfers between devices with their start and end apart: 5 -> 4, of which waited for: 4 -> 3; matrix products, arithmetic and copies ran while one was open for 0% -> 0% of each run, Pallas kernels for 10% -> 9%
where the time goes in v7:
time: 57.2 us; the launch traced here: 56.9 us
  blocking collectives  27.3 us (48%)
  Pallas kernels  11.8 us (21%)
  waiting for transfers between devices  11.2 us (20%)
  starting transfers between devices  6.48 us (11%)
    all_to_all x1, blocking collectives, body(): asked = lax.all_to_all(ask, BOTH, 0, 0, tiled=True)  14.3 us
    all_to_all x1, blocking collectives, body(): answer = lax.all_to_all(reply, BOTH, 0, 0, tiled=True)  13 us
    pallas_call x6, Pallas kernels, call(): pl.pallas_call(kernel, out_shape=outs if single else (*(pltpu.HBM(a.shape...  11.8 us
    all_to_all x1, waiting for transfers between devices, body(): answer_two = lax.all_to_all(reply_two, BOTH, 0, 0, tiled=True)  6.42 us
    ppermute x3, waiting for transfers between devices, body(): lax.ppermute(finals[q], 'dev', [(i, (i + 2 * q) % members) for i in range...  4.8 us
    ppermute x3, starting transfers between devices, body(): lax.ppermute(finals[q], 'dev', [(i, (i + 2 * q) % members) for i in range...  3.87 us
    all_to_all x1, starting transfers between devices, body(): answer_two = lax.all_to_all(reply_two, BOTH, 0, 0, tiled=True)  2.6 us
  transfers between devices with their start and end apart: 4, of which 3 were waited for; matrix products, arithmetic and copies ran while one was open for 0% of the time, Pallas kernels for 9%

profile of v7, /device:TPU:0, one launch (start us, length us, event | category | flops | bytes accessed | tf_op | source)
XLA Modules:
  0.0 56.9 jit_solution(14291245089992351653)
XLA Ops:
  0.0 1.5 %ask.1 = (s32[32,1,128]{2,1,0:T(1,128)S(1)}, bf16[128,128]{1,0:T(8,128)(2,1)S(1)}, bf16[128,200]{1,0:T(8,128)(2,1)S(1)}, bf16[192,192]{1,0:T(8,128)(2,1)S(1)}, bf16[128,768]{1,0:T(8,128)(2,1)S(1)}) custom-call(s32[25,128]{1,0:T(8,128)} %bitcast.3, s32[25,128]{1,0:T(8,128)} %bitcast.4, s32[1,128]{1,0:T(1,128)} %bitcast.5, bf16[128,768]{1,0:T(8,128)(2,1)} %features_hbm.3), custom_call_target="tpu_custom_call" | custom-call | flops 9437184 | bytes 593408 | tf_op jit(solution)/shard_map/ask/pallas_call | solution.py:55
  1.5 14.3 %all_to_all.15.asked_ref = s32[32,1,128]{2,1,0:T(1,128)S(1)} all-to-all(s32[32,1,128]{2,1,0:T(1,128)S(1)} %get-tuple-element.27), channel_id=1, replica_groups=mesh['grp'=4,'dev'=8] {'grp','dev'}, dimensions={0} | all-to-all | bytes 32768 | tf_op jit(solution)/shard_map/all_to_all | solution.py:326
  15.8 0.6 %serve.1 = (bf16[32,3,2,768]{3,2,1,0:T(2,128)(2,1)S(1)}, bf16[192,128]{1,0:T(8,128)(2,1)S(1)}) custom-call(s32[32,1,128]{2,1,0:T(1,128)S(1)} %all_to_all.15.asked_ref, bf16[192,192]{1,0:T(8,128)(2,1)S(1)} %get-tuple-element.28.order_ref, bf16[128,768]{1,0:T(8,128)(2,1)S(1)} %get-tuple-element.25.source_ref.features_ref), custom_call_target="tpu_custom_call" | custom-call | flops 37748736 | bytes 630784 | tf_op jit(solution)/shard_map/serve/pallas_call | solution.py:55
  16.4 13.0 %all_to_all.16.answer_ref = bf16[32,3,2,768]{3,2,1,0:T(2,128)(2,1)S(1)} all-to-all(bf16[32,3,2,768]{3,2,1,0:T(2,128)(2,1)S(1)} %get-tuple-element.29), channel_id=1, replica_groups=mesh['grp'=4,'dev'=8] {'grp','dev'}, dimensions={0} | all-to-all | bytes 589824 | tf_op jit(solution)/shard_map/all_to_all | solution.py:336
  29.5 1.7 %layer_one.1 = (bf16[32,3,2,768]{3,2,1,0:T(2,128)(2,1)}, bf16[128,768]{1,0:T(8,128)(2,1)}, bf16[32,3,2,768]{3,2,1,0:T(2,128)(2,1)}) custom-call(bf16[128,768]{1,0:T(8,128)(2,1)S(1)} %get-tuple-element.25.source_ref.features_ref, bf16[128,128]{1,0:T(8,128)(2,1)S(1)} %get-tuple-element.26.near_ref, bf16[32,3,2,768]{3,2,1,0:T(2,128)(2,1)S(1)} %all_to_all.16.answer_ref, ...), custom_call_target="tpu_custom_call" | custom-call | flops 100663296 | bytes 1411072 | tf_op jit(solution)/shard_map/layer_one/pallas_call | solution.py:55
  31.2 2.6 %all-to-all-start.2 = ((bf16[32,3,2,768]{3,2,1,0:T(2,128)(2,1)}), bf16[32,3,2,768]{3,2,1,0:T(2,128)(2,1)S(1)}, u32[]{:S(2)}, u32[]{:S(2)}) async-start(bf16[32,3,2,768]{3,2,1,0:T(2,128)(2,1)} %get-tuple-element.39), calls=%async_computation.2 | async-start | bytes 589824 | tf_op jit(solution)/shard_map/all_to_all | solution.py:351
  33.8 4.9 %between.1 = (f32[128,1024]{1,0:T(8,128)}, bf16[128,128]{1,0:T(8,128)(2,1)}, bf16[192,1024]{1,0:T(8,128)(2,1)S(1)}, bf16[128,200]{1,0:T(8,128)(2,1)S(1)}, bf16[7...) custom-call(bf16[768,1024]{1,0:T(8,128)(2,1)} %self_one_hbm.1, bf16[768,1024]{1,0:T(8,128)(2,1)} %neigh_one_hbm.1, ...), custom_call_target="tpu_custom_call" | custom-call | flops 1275068416 | bytes 11751936 | tf_op jit(solution)/shard_map/between/pallas_call | solution.py:55
  38.7 6.4 %all-to-all-done.2.answer_ref = bf16[32,3,2,768]{3,2,1,0:T(2,128)(2,1)S(1)} async-done(((bf16[32,3,2,768]{3,2,1,0:T(2,128)(2,1)}), bf16[32,3,2,768]{3,2,1,0:T(2,128)(2,1)S(1)}, u32[]{:S(2)}, u32[]{:S(2)}) %all-to-all-start.2) | async-done | bytes 294944 | tf_op jit(solution)/shard_map/all_to_all | solution.py:351
  45.1 0.0 copy-start
  45.1 2.2 %layer_two.1 = (bf16[32,1024]{1,0:T(8,128)(2,1)S(1)}, bf16[32,1024]{1,0:T(8,128)(2,1)S(1)}, bf16[32,1024]{1,0:T(8,128)(2,1)S(1)}, bf16[32,1024]{1,0:T(8,128)(2,1)S(1)}) custom-call(bf16[1024,1024]{1,0:T(8,128)(2,1)} %neigh_two_hbm.3, f32[128,1024]{1,0:T(8,128)} %get-tuple-element.35.final_hbm, bf16[768,1024]{1,0:T(8,128)(2,1)S(1)} %get-tuple-element.36.neigh_one_ref, ...), custom_call_target="tpu_custom_call" | custom-call | flops 620756992 | bytes 6244352 | tf_op jit(solution)/shard_map/layer_two/pallas_call | solution.py:55
  47.3 0.1 collective-permute-start
  47.4 0.2 collective-permute-start.1
  47.6 3.6 %collective-permute-start.2 = (bf16[32,1024]{1,0:T(8,128)(2,1)S(1)}, bf16[32,1024]{1,0:T(8,128)(2,1)S(1)}, u32[]{:S(2)}, u32[]{:S(2)}) collective-permute-start(bf16[32,1024]{1,0:T(8,128)(2,1)S(1)} %get-tuple-element.44), channel_id=1, source_target_pairs={{0,6},{1,7},{2,0},{3,1},{4,2},{5,3},{6,4},{7,5},{8,14},{9,15},{10,... | collective-permute-start | bytes 196616 | tf_op jit(solution)/shard_map/ppermute | solution.py:393
  51.2 3.0 %collective-permute-done.refs_1_ = bf16[32,1024]{1,0:T(8,128)(2,1)S(1)} collective-permute-done((bf16[32,1024]{1,0:T(8,128)(2,1)S(1)}, bf16[32,1024]{1,0:T(8,128)(2,1)S(1)}, u32[]{:S(2)}, u32[]{:S(2)}) %collective-permute-start) | collective-permute-done | bytes 65568 | tf_op jit(solution)/shard_map/ppermute | solution.py:393
  54.2 1.8 %collective-permute-done.1.refs_2_ = bf16[32,1024]{1,0:T(8,128)(2,1)S(1)} collective-permute-done((bf16[32,1024]{1,0:T(8,128)(2,1)S(1)}, bf16[32,1024]{1,0:T(8,128)(2,1)S(1)}, u32[]{:S(2)}, u32[]{:S(2)}) %collective-permute-start.1) | collective-permute-done | bytes 65568 | tf_op jit(solution)/shard_map/ppermute | solution.py:393
  56.0 0.0 collective-permute-done.2.refs_3_
  56.0 0.0 copy-done
  56.0 0.9 %scatter.1 = bf16[128,1024]{1,0:T(8,128)(2,1)} custom-call(bf16[128,128]{1,0:T(8,128)(2,1)S(1)} %copy-done, bf16[32,1024]{1,0:T(8,128)(2,1)S(1)} %get-tuple-element.41.refs_0_, bf16[32,1024]{1,0:T(8,128)(2,1)S(1)} %collective-permute-done.refs_1_, bf16[32,1024]{1,0:T(8,128)(2,1)S(1)} %collective-permute-done.1.refs_2_, ...), custom_call_target="tpu_custom_call" | custom-call | flops 33554432 | bytes 557056 | tf_op jit(solution)/shard_map/scatter/pallas_call | solution.py:55
Async XLA Ops:
  31.2 13.9 %all-to-all-start.2 = ((bf16[32,3,2,768]{3,2,1,0:T(2,128)(2,1)}), bf16[32,3,2,768]{3,2,1,0:T(2,128)(2,1)S(1)}, u32[]{:S(2)}, u32[]{:S(2)}) async-start(bf16[32,3,2,768]{3,2,1,0:T(2,128)(2,1)} %get-tuple-element.39), calls=%async_computation.2 | async-start | bytes 589824 | tf_op jit(solution)/shard_map/all_to_all | solution.py:351
  45.1 10.9 %copy-start = (bf16[128,128]{1,0:T(8,128)(2,1)S(1)}, bf16[128,128]{1,0:T(8,128)(2,1)}, u32[]{:S(2)}) copy-start(bf16[128,128]{1,0:T(8,128)(2,1)} %get-tuple-element.34.place_ref) | copy-start | bytes 98308
  47.3 6.9 %collective-permute-start = (bf16[32,1024]{1,0:T(8,128)(2,1)S(1)}, bf16[32,1024]{1,0:T(8,128)(2,1)S(1)}, u32[]{:S(2)}, u32[]{:S(2)}) collective-permute-start(bf16[32,1024]{1,0:T(8,128)(2,1)S(1)} %get-tuple-element.42), channel_id=1, source_target_pairs={{0,2},{1,3},{2,4},{3,5},{4,6},{5,7},{6,0},{7,1},{8,10},{9,11},{10,... | collective-permute-start | bytes 196616 | tf_op jit(solution)/shard_map/ppermute | solution.py:393
  47.4 8.6 %collective-permute-start.1 = (bf16[32,1024]{1,0:T(8,128)(2,1)S(1)}, bf16[32,1024]{1,0:T(8,128)(2,1)S(1)}, u32[]{:S(2)}, u32[]{:S(2)}) collective-permute-start(bf16[32,1024]{1,0:T(8,128)(2,1)S(1)} %get-tuple-element.43), channel_id=1, source_target_pairs={{0,4},{1,5},{2,6},{3,7},{4,0},{5,1},{6,2},{7,3},{8,12},{9,13},{10,... | collective-permute-start | bytes 196616 | tf_op jit(solution)/shard_map/ppermute | solution.py:393
  47.6 8.4 %collective-permute-start.2 = (bf16[32,1024]{1,0:T(8,128)(2,1)S(1)}, bf16[32,1024]{1,0:T(8,128)(2,1)S(1)}, u32[]{:S(2)}, u32[]{:S(2)}) collective-permute-start(bf16[32,1024]{1,0:T(8,128)(2,1)S(1)} %get-tuple-element.44), channel_id=1, source_target_pairs={{0,6},{1,7},{2,0},{3,1},{4,2},{5,3},{6,4},{7,5},{8,14},{9,15},{10,... | collective-permute-start | bytes 196616 | tf_op jit(solution)/shard_map/ppermute | solution.py:393

commit v8 on v7

--- a/solution.py
+++ b/solution.py
@@ -200,7 +200,7 @@
 def between_kernel(
     members, self_one_hbm, neigh_one_hbm, self_two_hbm, neigh_two_hbm, pos_hbm, features_hbm, answer_hbm, mean_hbm,
     near_ref, far_ref, asked_ref,
-    final_hbm, place_hbm, base_ref, far_moved_ref, neigh_one_ref, ready_ref,
+    final_hbm, place_hbm, base_ref, far_moved_ref, dense_ref, neigh_one_ref, ready_ref,
     held_one, held_two, rest, features_ref, answer_ref, mean_ref, final_ref, place_ref, pos_ref, sems,
 ):
     ready = ready_ref.shape[0]
@@ -235,7 +235,15 @@
     move = bits(goes & (before == rank)).astype(BF16)
     near = dot(move, near_ref[...]).astype(BF16)
     far = dot(move, far_ref[...]).astype(BF16)
-    far_moved_ref[...] = far
+    size = far.shape[1] - 8
+    used = jnp.sum(far_ref[:, :size].astype(F32), axis=0, keepdims=True) > 0.0
+    used = jnp.broadcast_to(used, dense_ref.shape)
+    seats = dot(bits(used).astype(BF16), earlier(size)).astype(I32)
+    dense = bits(used & (seats == iota(used.shape, 0))).astype(BF16)
+    dense_ref[...] = dense
+    held = dense.shape[0]
+    far_moved_ref[:, :held] = dot_lanes(far[:, :size], dense).astype(BF16)
+    far_moved_ref[:, held:] = far[:, size:]
     place = jnp.zeros((rows, rows), F32)
     for q in range(members // 2):
         source = me - 2 * q
@@ -252,7 +260,7 @@
     for copy in (*inputs, copies[1]):
         copy.wait()
     own = dot(features_ref[...], held_one[...])
-    base_ref[...] = dot(load_rows(answer_ref), held_one[...]).astype(BF16)
+    base_ref[...] = dot(dot(dense, load_rows(answer_ref)).astype(BF16), held_one[...]).astype(BF16)
     copies[2].wait()
     hidden = jnp.maximum(own + dot(mean_ref[...], neigh_one_ref[...]), 0.0).astype(BF16)
     mean = over_count(dot(near, hidden), far)
@@ -262,14 +270,14 @@
     copies[4].wait()
     final += dot(mean[:, :ready], ready_ref[...])
     copies[5].wait()
-    final_ref[...] = final + dot(mean[:, ready:], rest[...])
+    final_ref[...] = (final + dot(mean[:, ready:], rest[...])).astype(BF16)
     away = pltpu.make_async_copy(final_ref, final_hbm, sems.at[10])
     away.start()
     away.wait()
     placed.wait()
 
 
-def layer_two_kernel(neigh_two_hbm, final_hbm, neigh_one_ref, ready_ref, base_ref, answer_ref, far_ref, *refs):
+def layer_two_kernel(neigh_two_hbm, final_hbm, neigh_one_ref, ready_ref, base_ref, answer_ref, far_ref, dense_ref, *refs):
     outs, held, final_ref, sems = refs[:-3], refs[-3], refs[-2], refs[-1]
     ready = ready_ref.shape[0]
     pieces = sems.shape[0] - 1
@@ -278,11 +286,12 @@
     for copy in (*copies, last):
         copy.start()
     far = far_ref[...]
-    other = jnp.maximum(base_ref[...].astype(F32) + dot(load_rows(answer_ref), neigh_one_ref[...]), 0.0).astype(BF16)
+    answer = dot(dense_ref[...], load_rows(answer_ref)).astype(BF16)
+    other = jnp.maximum(base_ref[...].astype(F32) + dot(answer, neigh_one_ref[...]), 0.0).astype(BF16)
     mean = over_count(dot(far[:, : other.shape[0]], other), far)
     final = dot(mean[:, :ready], ready_ref[...]) + dot_fetched(mean[:, ready:], held, copies)
     last.wait()
-    final = (final + final_ref[...]).astype(BF16)
+    final = (final + final_ref[...].astype(F32)).astype(BF16)
     capacity = outs[0].shape[0]
     for q, ref in enumerate(outs):
         ref[...] = final[q * capacity : (q + 1) * capacity]
@@ -302,7 +311,8 @@
     steps = members // 2
     capacity = rows // steps
     size = peers * CAP
-    early = width // 2
+    early = width * 9 // 16
+    held = -(-((peers - 1) * CAP // 2) // 16) * 16
     shape = jax.ShapeDtypeStruct
     copies = pltpu.SemaphoreType.DMA
 
@@ -349,13 +359,14 @@
         away=2,
     )
     answer_two = lax.all_to_all(reply_two, BOTH, 0, 0, tiled=True)
-    final, place, base, far_moved, weight, ready = call(
+    final, place, base, far_moved, dense, weight, ready = call(
         functools.partial(between_kernel, members),
         (
-            shape((rows, width), F32),
+            shape((rows, width), BF16),
             shape((rows, rows), BF16),
-            shape((size, width), BF16),
-            shape((rows, size + 8), BF16),
+            shape((held, width), BF16),
+            shape((rows, held + 8), BF16),
+            shape((held, size), BF16),
             shape((width_in, width), BF16),
             shape((early, width), BF16),
         ),
@@ -368,7 +379,7 @@
             pltpu.VMEM((rows, width_in), BF16),
             pltpu.VMEM((peers, CAP // 2, 2, width_in), BF16),
             pltpu.VMEM((rows, width_in), BF16),
-            pltpu.VMEM((rows, width), F32),
+            pltpu.VMEM((rows, width), BF16),
             pltpu.VMEM((rows, rows), BF16),
             pltpu.VMEM((1, rows), I32),
             copies((11,)),
@@ -382,8 +393,8 @@
         layer_two_kernel,
         tuple(shape((capacity, width), BF16) for _ in range(steps)),
         (neigh_weight2, final),
-        (weight, ready, base, answer_two, far_moved),
-        [pltpu.VMEM((width - early, width), BF16), pltpu.VMEM((rows, width), F32), copies((3,))],
+        (weight, ready, base, answer_two, far_moved, dense),
+        [pltpu.VMEM((width - early, width), BF16), pltpu.VMEM((rows, width), BF16), copies((3,))],
         2 * width * (size * width_in + rows * (size + width)),
         "layer_two",
         limit=48 << 20,

time: 57.2 us -> 57.3 us (level)
  no operation moved by 1% of the time
where the time goes in v8:
time: 57.3 us; the launch traced here: 57 us
  blocking collectives  27.3 us (48%)
  Pallas kernels  12 us (21%)
  waiting for transfers between devices  11.1 us (19%)
  starting transfers between devices  6.48 us (11%)
    all_to_all x1, blocking collectives, body(): asked = lax.all_to_all(ask, BOTH, 0, 0, tiled=True)  14.3 us
    all_to_all x1, blocking collectives, body(): answer = lax.all_to_all(reply, BOTH, 0, 0, tiled=True)  13 us
    pallas_call x6, Pallas kernels, call(): pl.pallas_call(kernel, out_shape=outs if single else (*(pltpu.HBM(a.shape...  12 us
    all_to_all x1, waiting for transfers between devices, body(): answer_two = lax.all_to_all(reply_two, BOTH, 0, 0, tiled=True)  6.3 us
    ppermute x3, waiting for transfers between devices, body(): lax.ppermute(finals[q], 'dev', [(i, (i + 2 * q) % members) for i in range...  4.79 us
    ppermute x3, starting transfers between devices, body(): lax.ppermute(finals[q], 'dev', [(i, (i + 2 * q) % members) for i in range...  3.87 us
    all_to_all x1, starting transfers between devices, body(): answer_two = lax.all_to_all(reply_two, BOTH, 0, 0, tiled=True)  2.6 us
  transfers between devices with their start and end apart: 4, of which 3 were waited for; matrix products, arithmetic and copies ran while one was open for 0% of the time, Pallas kernels for 9%

profile of v8, /device:TPU:0, one launch (start us, length us, event | category | flops | bytes accessed | tf_op | source)
XLA Modules:
  0.0 57.0 jit_solution(269467870406120255)
XLA Ops:
  0.0 1.5 %ask.1 = (s32[32,1,128]{2,1,0:T(1,128)S(1)}, bf16[128,128]{1,0:T(8,128)(2,1)S(1)}, bf16[128,200]{1,0:T(8,128)(2,1)S(1)}, bf16[192,192]{1,0:T(8,128)(2,1)S(1)}, bf16[128,768]{1,0:T(8,128)(2,1)S(1)}) custom-call(s32[25,128]{1,0:T(8,128)} %bitcast.3, s32[25,128]{1,0:T(8,128)} %bitcast.4, s32[1,128]{1,0:T(1,128)} %bitcast.5, bf16[128,768]{1,0:T(8,128)(2,1)} %features_hbm.3), custom_call_target="tpu_custom_call" | custom-call | flops 9437184 | bytes 593408 | tf_op jit(solution)/shard_map/ask/pallas_call | solution.py:55
  1.5 14.3 %all_to_all.15.asked_ref = s32[32,1,128]{2,1,0:T(1,128)S(1)} all-to-all(s32[32,1,128]{2,1,0:T(1,128)S(1)} %get-tuple-element.28), channel_id=1, replica_groups=mesh['grp'=4,'dev'=8] {'grp','dev'}, dimensions={0} | all-to-all | bytes 32768 | tf_op jit(solution)/shard_map/all_to_all | solution.py:336
  15.8 0.6 %serve.1 = (bf16[32,3,2,768]{3,2,1,0:T(2,128)(2,1)S(1)}, bf16[192,128]{1,0:T(8,128)(2,1)S(1)}) custom-call(s32[32,1,128]{2,1,0:T(1,128)S(1)} %all_to_all.15.asked_ref, bf16[192,192]{1,0:T(8,128)(2,1)S(1)} %get-tuple-element.29.order_ref, bf16[128,768]{1,0:T(8,128)(2,1)S(1)} %get-tuple-element.26.source_ref.features_ref), custom_call_target="tpu_custom_call" | custom-call | flops 37748736 | bytes 630784 | tf_op jit(solution)/shard_map/serve/pallas_call | solution.py:55
  16.4 13.0 %all_to_all.16.answer_ref = bf16[32,3,2,768]{3,2,1,0:T(2,128)(2,1)S(1)} all-to-all(bf16[32,3,2,768]{3,2,1,0:T(2,128)(2,1)S(1)} %get-tuple-element.30), channel_id=1, replica_groups=mesh['grp'=4,'dev'=8] {'grp','dev'}, dimensions={0} | all-to-all | bytes 589824 | tf_op jit(solution)/shard_map/all_to_all | solution.py:346
  29.5 1.7 %layer_one.1 = (bf16[32,3,2,768]{3,2,1,0:T(2,128)(2,1)}, bf16[128,768]{1,0:T(8,128)(2,1)}, bf16[32,3,2,768]{3,2,1,0:T(2,128)(2,1)}) custom-call(bf16[128,768]{1,0:T(8,128)(2,1)S(1)} %get-tuple-element.26.source_ref.features_ref, bf16[128,128]{1,0:T(8,128)(2,1)S(1)} %get-tuple-element.27.near_ref, bf16[32,3,2,768]{3,2,1,0:T(2,128)(2,1)S(1)} %all_to_all.16.answer_ref, ...), custom_call_target="tpu_custom_call" | custom-call | flops 100663296 | bytes 1411072 | tf_op jit(solution)/shard_map/layer_one/pallas_call | solution.py:55
  31.2 2.6 %all-to-all-start.2 = ((bf16[32,3,2,768]{3,2,1,0:T(2,128)(2,1)}), bf16[32,3,2,768]{3,2,1,0:T(2,128)(2,1)S(1)}, u32[]{:S(2)}, u32[]{:S(2)}) async-start(bf16[32,3,2,768]{3,2,1,0:T(2,128)(2,1)} %get-tuple-element.40), calls=%async_computation.2 | async-start | bytes 589824 | tf_op jit(solution)/shard_map/all_to_all | solution.py:361
  33.8 5.0 %between.1 = (bf16[128,1024]{1,0:T(8,128)(2,1)}, bf16[128,128]{1,0:T(8,128)(2,1)}, bf16[96,1024]{1,0:T(8,128)(2,1)S(1)}, bf16[128,104]{1,0:T(8,128)(2,1)S(1)}, b...) custom-call(bf16[768,1024]{1,0:T(8,128)(2,1)} %self_one_hbm.1, ...), custom_call_target="tpu_custom_call" | custom-call | flops 1275068416 | bytes 11436544 | tf_op jit(solution)/shard_map/between/pallas_call | solution.py:55
  38.8 6.3 %all-to-all-done.2.answer_ref = bf16[32,3,2,768]{3,2,1,0:T(2,128)(2,1)S(1)} async-done(((bf16[32,3,2,768]{3,2,1,0:T(2,128)(2,1)}), bf16[32,3,2,768]{3,2,1,0:T(2,128)(2,1)S(1)}, u32[]{:S(2)}, u32[]{:S(2)}) %all-to-all-start.2) | async-done | bytes 294944 | tf_op jit(solution)/shard_map/all_to_all | solution.py:361
  45.1 0.0 copy-start
  45.1 2.3 %layer_two.1 = (bf16[32,1024]{1,0:T(8,128)(2,1)S(1)}, bf16[32,1024]{1,0:T(8,128)(2,1)S(1)}, bf16[32,1024]{1,0:T(8,128)(2,1)S(1)}, bf16[32,1024]{1,0:T(8,128)(2,1)S(1)}) custom-call(bf16[1024,1024]{1,0:T(8,128)(2,1)} %neigh_two_hbm.3, bf16[128,1024]{1,0:T(8,128)(2,1)} %get-tuple-element.36.final_hbm, bf16[768,1024]{1,0:T(8,128)(2,1)S(1)} %get-tuple-element.37.neigh_one_ref, ...), custom_call_target="tpu_custom_call" | custom-call | flops 620756992 | bytes 5928960 | tf_op jit(solution)/shard_map/layer_two/pallas_call | solution.py:55
  47.4 0.1 collective-permute-start
  47.5 0.2 collective-permute-start.1
  47.7 3.6 %collective-permute-start.2 = (bf16[32,1024]{1,0:T(8,128)(2,1)S(1)}, bf16[32,1024]{1,0:T(8,128)(2,1)S(1)}, u32[]{:S(2)}, u32[]{:S(2)}) collective-permute-start(bf16[32,1024]{1,0:T(8,128)(2,1)S(1)} %get-tuple-element.46), channel_id=1, source_target_pairs={{0,6},{1,7},{2,0},{3,1},{4,2},{5,3},{6,4},{7,5},{8,14},{9,15},{10,... | collective-permute-start | bytes 196616 | tf_op jit(solution)/shard_map/ppermute | solution.py:404
  51.3 3.0 %collective-permute-done.refs_1_ = bf16[32,1024]{1,0:T(8,128)(2,1)S(1)} collective-permute-done((bf16[32,1024]{1,0:T(8,128)(2,1)S(1)}, bf16[32,1024]{1,0:T(8,128)(2,1)S(1)}, u32[]{:S(2)}, u32[]{:S(2)}) %collective-permute-start) | collective-permute-done | bytes 65568 | tf_op jit(solution)/shard_map/ppermute | solution.py:404
  54.3 1.8 %collective-permute-done.1.refs_2_ = bf16[32,1024]{1,0:T(8,128)(2,1)S(1)} collective-permute-done((bf16[32,1024]{1,0:T(8,128)(2,1)S(1)}, bf16[32,1024]{1,0:T(8,128)(2,1)S(1)}, u32[]{:S(2)}, u32[]{:S(2)}) %collective-permute-start.1) | collective-permute-done | bytes 65568 | tf_op jit(solution)/shard_map/ppermute | solution.py:404
  56.1 0.0 collective-permute-done.2.refs_3_
  56.1 0.0 copy-done
  56.1 0.9 %scatter.1 = bf16[128,1024]{1,0:T(8,128)(2,1)} custom-call(bf16[128,128]{1,0:T(8,128)(2,1)S(1)} %copy-done, bf16[32,1024]{1,0:T(8,128)(2,1)S(1)} %get-tuple-element.43.refs_0_, bf16[32,1024]{1,0:T(8,128)(2,1)S(1)} %collective-permute-done.refs_1_, bf16[32,1024]{1,0:T(8,128)(2,1)S(1)} %collective-permute-done.1.refs_2_, ...), custom_call_target="tpu_custom_call" | custom-call | flops 33554432 | bytes 557056 | tf_op jit(solution)/shard_map/scatter/pallas_call | solution.py:55
Async XLA Ops:
  31.2 13.9 %all-to-all-start.2 = ((bf16[32,3,2,768]{3,2,1,0:T(2,128)(2,1)}), bf16[32,3,2,768]{3,2,1,0:T(2,128)(2,1)S(1)}, u32[]{:S(2)}, u32[]{:S(2)}) async-start(bf16[32,3,2,768]{3,2,1,0:T(2,128)(2,1)} %get-tuple-element.40), calls=%async_computation.2 | async-start | bytes 589824 | tf_op jit(solution)/shard_map/all_to_all | solution.py:361
  45.1 11.0 %copy-start = (bf16[128,128]{1,0:T(8,128)(2,1)S(1)}, bf16[128,128]{1,0:T(8,128)(2,1)}, u32[]{:S(2)}) copy-start(bf16[128,128]{1,0:T(8,128)(2,1)} %get-tuple-element.35.place_ref) | copy-start | bytes 98308
  47.4 6.9 %collective-permute-start = (bf16[32,1024]{1,0:T(8,128)(2,1)S(1)}, bf16[32,1024]{1,0:T(8,128)(2,1)S(1)}, u32[]{:S(2)}, u32[]{:S(2)}) collective-permute-start(bf16[32,1024]{1,0:T(8,128)(2,1)S(1)} %get-tuple-element.44), channel_id=1, source_target_pairs={{0,2},{1,3},{2,4},{3,5},{4,6},{5,7},{6,0},{7,1},{8,10},{9,11},{10,... | collective-permute-start | bytes 196616 | tf_op jit(solution)/shard_map/ppermute | solution.py:404
  47.5 8.6 %collective-permute-start.1 = (bf16[32,1024]{1,0:T(8,128)(2,1)S(1)}, bf16[32,1024]{1,0:T(8,128)(2,1)S(1)}, u32[]{:S(2)}, u32[]{:S(2)}) collective-permute-start(bf16[32,1024]{1,0:T(8,128)(2,1)S(1)} %get-tuple-element.45), channel_id=1, source_target_pairs={{0,4},{1,5},{2,6},{3,7},{4,0},{5,1},{6,2},{7,3},{8,12},{9,13},{10,... | collective-permute-start | bytes 196616 | tf_op jit(solution)/shard_map/ppermute | solution.py:404
  47.7 8.4 %collective-permute-start.2 = (bf16[32,1024]{1,0:T(8,128)(2,1)S(1)}, bf16[32,1024]{1,0:T(8,128)(2,1)S(1)}, u32[]{:S(2)}, u32[]{:S(2)}) collective-permute-start(bf16[32,1024]{1,0:T(8,128)(2,1)S(1)} %get-tuple-element.46), channel_id=1, source_target_pairs={{0,6},{1,7},{2,0},{3,1},{4,2},{5,3},{6,4},{7,5},{8,14},{9,15},{10,... | collective-permute-start | bytes 196616 | tf_op jit(solution)/shard_map/ppermute | solution.py:404

commit v9 on v8

--- a/solution.py
+++ b/solution.py
@@ -182,7 +182,7 @@
 
 
 def layer_one_kernel(
-    features_ref, near_ref, answer_ref, far_ref, pick_ref, answer_hbm, mean_hbm, reply_ref, mean_ref, sems
+    features_ref, near_ref, answer_ref, far_ref, pick_ref, answer_hbm, mean_hbm, reply_hbm, mean_ref, reply_ref, sems
 ):
     kept = pltpu.make_async_copy(answer_ref, answer_hbm, sems.at[0])
     kept.start()
@@ -193,8 +193,11 @@
     saved = pltpu.make_async_copy(mean_ref, mean_hbm, sems.at[1])
     saved.start()
     store_rows(reply_ref, dot(pick_ref[...], mean).astype(BF16))
+    sent = pltpu.make_async_copy(reply_ref, reply_hbm, sems.at[2])
+    sent.start()
     kept.wait()
     saved.wait()
+    sent.wait()
 
 
 def between_kernel(
@@ -283,8 +286,18 @@
     pieces = sems.shape[0] - 1
     copies = fetches(neigh_two_hbm.at[pl.ds(ready, held.shape[0])], held, sems.at[pl.ds(0, pieces)])
     last = pltpu.make_async_copy(final_hbm, final_ref, sems.at[pieces])
-    for copy in (*copies, last):
-        copy.start()
+
+    depth = held.shape[0] // pieces
+
+    @pl.loop(0, pieces)
+    def _(i):
+        piece = pl.ds(pl.multiple_of(i * depth, 16), depth)
+        pltpu.make_async_copy(neigh_two_hbm.at[pl.ds(ready, held.shape[0])].at[piece], held.at[piece], sems.at[i]).start()
+
+        @pl.when(i == pieces - 1)
+        def _():
+            last.start()
+
     far = far_ref[...]
     answer = dot(dense_ref[...], load_rows(answer_ref)).astype(BF16)
     other = jnp.maximum(base_ref[...].astype(F32) + dot(answer, neigh_one_ref[...]), 0.0).astype(BF16)
@@ -353,10 +366,10 @@
         ),
         (),
         (table, near, answer, far, pick),
-        [pltpu.VMEM((rows, width_in), BF16), copies((2,))],
+        [pltpu.VMEM((rows, width_in), BF16), pltpu.VMEM((peers, CAP // 2, 2, width_in), BF16), copies((3,))],
         2 * rows * width_in * (size + rows) + 2 * size * rows * width_in,
         "layer_one",
-        away=2,
+        away=3,
     )
     answer_two = lax.all_to_all(reply_two, BOTH, 0, 0, tiled=True)
     final, place, base, far_moved, dense, weight, ready = call(

time: 57.3 us -> 56.4 us (0.984)
  Pallas kernels: 12 us -> 11.1 us
    pallas_call x6, Pallas kernels: 12 us -> 11.1 us  [call(): pl.pallas_call(kernel, out_shape=outs if single else (*(pltpu.HBM(a.shape...]
where the time goes in v9:
time: 56.4 us; the launch traced here: 56 us
  blocking collectives  27.3 us (48%)
  Pallas kernels  11.1 us (20%)
  waiting for transfers between devices  11.1 us (20%)
  starting transfers between devices  6.48 us (11%)
    all_to_all x1, blocking collectives, body(): asked = lax.all_to_all(ask, BOTH, 0, 0, tiled=True)  14.3 us
    all_to_all x1, blocking collectives, body(): answer = lax.all_to_all(reply, BOTH, 0, 0, tiled=True)  13 us
    pallas_call x6, Pallas kernels, call(): pl.pallas_call(kernel, out_shape=outs if single else (*(pltpu.HBM(a.shape...  11.1 us
    all_to_all x1, waiting for transfers between devices, body(): answer_two = lax.all_to_all(reply_two, BOTH, 0, 0, tiled=True)  6.3 us
    ppermute x3, waiting for transfers between devices, body(): lax.ppermute(finals[q], 'dev', [(i, (i + 2 * q) % members) for i in range...  4.79 us
    ppermute x3, starting transfers between devices, body(): lax.ppermute(finals[q], 'dev', [(i, (i + 2 * q) % members) for i in range...  3.87 us
    all_to_all x1, starting transfers between devices, body(): answer_two = lax.all_to_all(reply_two, BOTH, 0, 0, tiled=True)  2.6 us
  transfers between devices with their start and end apart: 4, of which 3 were waited for; matrix products, arithmetic and copies ran while one was open for 0% of the time, Pallas kernels for 9%

profile of v9, /device:TPU:0, one launch (start us, length us, event | category | flops | bytes accessed | tf_op | source)
XLA Modules:
  0.0 56.0 jit_solution(16358861901412659357)
XLA Ops:
  0.0 1.5 %ask.1 = (s32[32,1,128]{2,1,0:T(1,128)S(1)}, bf16[128,128]{1,0:T(8,128)(2,1)S(1)}, bf16[128,200]{1,0:T(8,128)(2,1)S(1)}, bf16[192,192]{1,0:T(8,128)(2,1)S(1)}, bf16[128,768]{1,0:T(8,128)(2,1)S(1)}) custom-call(s32[25,128]{1,0:T(8,128)} %bitcast.3, s32[25,128]{1,0:T(8,128)} %bitcast.4, s32[1,128]{1,0:T(1,128)} %bitcast.5, bf16[128,768]{1,0:T(8,128)(2,1)} %features_hbm.3), custom_call_target="tpu_custom_call" | custom-call | flops 9437184 | bytes 593408 | tf_op jit(solution)/shard_map/ask/pallas_call | solution.py:55
  1.5 14.3 %all_to_all.15.asked_ref = s32[32,1,128]{2,1,0:T(1,128)S(1)} all-to-all(s32[32,1,128]{2,1,0:T(1,128)S(1)} %get-tuple-element.28), channel_id=1, replica_groups=mesh['grp'=4,'dev'=8] {'grp','dev'}, dimensions={0} | all-to-all | bytes 32768 | tf_op jit(solution)/shard_map/all_to_all | solution.py:349
  15.8 0.6 %serve.1 = (bf16[32,3,2,768]{3,2,1,0:T(2,128)(2,1)S(1)}, bf16[192,128]{1,0:T(8,128)(2,1)S(1)}) custom-call(s32[32,1,128]{2,1,0:T(1,128)S(1)} %all_to_all.15.asked_ref, bf16[192,192]{1,0:T(8,128)(2,1)S(1)} %get-tuple-element.29.order_ref, bf16[128,768]{1,0:T(8,128)(2,1)S(1)} %get-tuple-element.26.source_ref.features_ref), custom_call_target="tpu_custom_call" | custom-call | flops 37748736 | bytes 630784 | tf_op jit(solution)/shard_map/serve/pallas_call | solution.py:55
  16.4 13.0 %all_to_all.16.answer_ref = bf16[32,3,2,768]{3,2,1,0:T(2,128)(2,1)S(1)} all-to-all(bf16[32,3,2,768]{3,2,1,0:T(2,128)(2,1)S(1)} %get-tuple-element.30), channel_id=1, replica_groups=mesh['grp'=4,'dev'=8] {'grp','dev'}, dimensions={0} | all-to-all | bytes 589824 | tf_op jit(solution)/shard_map/all_to_all | solution.py:359
  29.5 1.3 %layer_one.1 = (bf16[32,3,2,768]{3,2,1,0:T(2,128)(2,1)}, bf16[128,768]{1,0:T(8,128)(2,1)}, bf16[32,3,2,768]{3,2,1,0:T(2,128)(2,1)}) custom-call(bf16[128,768]{1,0:T(8,128)(2,1)S(1)} %get-tuple-element.26.source_ref.features_ref, bf16[128,128]{1,0:T(8,128)(2,1)S(1)} %get-tuple-element.27.near_ref, bf16[32,3,2,768]{3,2,1,0:T(2,128)(2,1)S(1)} %all_to_all.16.answer_ref, ...), custom_call_target="tpu_custom_call" | custom-call | flops 100663296 | bytes 1411072 | tf_op jit(solution)/shard_map/layer_one/pallas_call | solution.py:55
  30.7 2.6 %all-to-all-start.2 = ((bf16[32,3,2,768]{3,2,1,0:T(2,128)(2,1)}), bf16[32,3,2,768]{3,2,1,0:T(2,128)(2,1)S(1)}, u32[]{:S(2)}, u32[]{:S(2)}) async-start(bf16[32,3,2,768]{3,2,1,0:T(2,128)(2,1)} %get-tuple-element.40), calls=%async_computation.2 | async-start | bytes 589824 | tf_op jit(solution)/shard_map/all_to_all | solution.py:374
  33.3 5.0 %between.1 = (bf16[128,1024]{1,0:T(8,128)(2,1)}, bf16[128,128]{1,0:T(8,128)(2,1)}, bf16[96,1024]{1,0:T(8,128)(2,1)S(1)}, bf16[128,104]{1,0:T(8,128)(2,1)S(1)}, b...) custom-call(bf16[768,1024]{1,0:T(8,128)(2,1)} %self_one_hbm.1, ...), custom_call_target="tpu_custom_call" | custom-call | flops 1275068416 | bytes 11436544 | tf_op jit(solution)/shard_map/between/pallas_call | solution.py:55
  38.3 6.3 %all-to-all-done.2.answer_ref = bf16[32,3,2,768]{3,2,1,0:T(2,128)(2,1)S(1)} async-done(((bf16[32,3,2,768]{3,2,1,0:T(2,128)(2,1)}), bf16[32,3,2,768]{3,2,1,0:T(2,128)(2,1)S(1)}, u32[]{:S(2)}, u32[]{:S(2)}) %all-to-all-start.2) | async-done | bytes 294944 | tf_op jit(solution)/shard_map/all_to_all | solution.py:374
  44.6 0.0 copy-start
  44.7 1.8 %layer_two.1 = (bf16[32,1024]{1,0:T(8,128)(2,1)S(1)}, bf16[32,1024]{1,0:T(8,128)(2,1)S(1)}, bf16[32,1024]{1,0:T(8,128)(2,1)S(1)}, bf16[32,1024]{1,0:T(8,128)(2,1)S(1)}) custom-call(bf16[1024,1024]{1,0:T(8,128)(2,1)} %neigh_two_hbm.3, bf16[128,1024]{1,0:T(8,128)(2,1)} %get-tuple-element.36.final_hbm, bf16[768,1024]{1,0:T(8,128)(2,1)S(1)} %get-tuple-element.37.neigh_one_ref, ...), custom_call_target="tpu_custom_call" | custom-call | flops 620756992 | bytes 5928960 | tf_op jit(solution)/shard_map/layer_two/pallas_call | solution.py:55
  46.4 0.1 collective-permute-start
  46.5 0.3 collective-permute-start.1
  46.8 3.6 %collective-permute-start.2 = (bf16[32,1024]{1,0:T(8,128)(2,1)S(1)}, bf16[32,1024]{1,0:T(8,128)(2,1)S(1)}, u32[]{:S(2)}, u32[]{:S(2)}) collective-permute-start(bf16[32,1024]{1,0:T(8,128)(2,1)S(1)} %get-tuple-element.46), channel_id=1, source_target_pairs={{0,6},{1,7},{2,0},{3,1},{4,2},{5,3},{6,4},{7,5},{8,14},{9,15},{10,... | collective-permute-start | bytes 196616 | tf_op jit(solution)/shard_map/ppermute | solution.py:417
  50.3 3.0 %collective-permute-done.refs_1_ = bf16[32,1024]{1,0:T(8,128)(2,1)S(1)} collective-permute-done((bf16[32,1024]{1,0:T(8,128)(2,1)S(1)}, bf16[32,1024]{1,0:T(8,128)(2,1)S(1)}, u32[]{:S(2)}, u32[]{:S(2)}) %collective-permute-start) | collective-permute-done | bytes 65568 | tf_op jit(solution)/shard_map/ppermute | solution.py:417
  53.3 1.8 %collective-permute-done.1.refs_2_ = bf16[32,1024]{1,0:T(8,128)(2,1)S(1)} collective-permute-done((bf16[32,1024]{1,0:T(8,128)(2,1)S(1)}, bf16[32,1024]{1,0:T(8,128)(2,1)S(1)}, u32[]{:S(2)}, u32[]{:S(2)}) %collective-permute-start.1) | collective-permute-done | bytes 65568 | tf_op jit(solution)/shard_map/ppermute | solution.py:417
  55.1 0.0 collective-permute-done.2.refs_3_
  55.1 0.0 copy-done
  55.1 0.9 %scatter.1 = bf16[128,1024]{1,0:T(8,128)(2,1)} custom-call(bf16[128,128]{1,0:T(8,128)(2,1)S(1)} %copy-done, bf16[32,1024]{1,0:T(8,128)(2,1)S(1)} %get-tuple-element.43.refs_0_, bf16[32,1024]{1,0:T(8,128)(2,1)S(1)} %collective-permute-done.refs_1_, bf16[32,1024]{1,0:T(8,128)(2,1)S(1)} %collective-permute-done.1.refs_2_, ...), custom_call_target="tpu_custom_call" | custom-call | flops 33554432 | bytes 557056 | tf_op jit(solution)/shard_map/scatter/pallas_call | solution.py:55
Async XLA Ops:
  30.7 13.9 %all-to-all-start.2 = ((bf16[32,3,2,768]{3,2,1,0:T(2,128)(2,1)}), bf16[32,3,2,768]{3,2,1,0:T(2,128)(2,1)S(1)}, u32[]{:S(2)}, u32[]{:S(2)}) async-start(bf16[32,3,2,768]{3,2,1,0:T(2,128)(2,1)} %get-tuple-element.40), calls=%async_computation.2 | async-start | bytes 589824 | tf_op jit(solution)/shard_map/all_to_all | solution.py:374
  44.6 10.5 %copy-start = (bf16[128,128]{1,0:T(8,128)(2,1)S(1)}, bf16[128,128]{1,0:T(8,128)(2,1)}, u32[]{:S(2)}) copy-start(bf16[128,128]{1,0:T(8,128)(2,1)} %get-tuple-element.35.place_ref) | copy-start | bytes 98308
  46.4 6.9 %collective-permute-start = (bf16[32,1024]{1,0:T(8,128)(2,1)S(1)}, bf16[32,1024]{1,0:T(8,128)(2,1)S(1)}, u32[]{:S(2)}, u32[]{:S(2)}) collective-permute-start(bf16[32,1024]{1,0:T(8,128)(2,1)S(1)} %get-tuple-element.44), channel_id=1, source_target_pairs={{0,2},{1,3},{2,4},{3,5},{4,6},{5,7},{6,0},{7,1},{8,10},{9,11},{10,... | collective-permute-start | bytes 196616 | tf_op jit(solution)/shard_map/ppermute | solution.py:417
  46.5 8.6 %collective-permute-start.1 = (bf16[32,1024]{1,0:T(8,128)(2,1)S(1)}, bf16[32,1024]{1,0:T(8,128)(2,1)S(1)}, u32[]{:S(2)}, u32[]{:S(2)}) collective-permute-start(bf16[32,1024]{1,0:T(8,128)(2,1)S(1)} %get-tuple-element.45), channel_id=1, source_target_pairs={{0,4},{1,5},{2,6},{3,7},{4,0},{5,1},{6,2},{7,3},{8,12},{9,13},{10,... | collective-permute-start | bytes 196616 | tf_op jit(solution)/shard_map/ppermute | solution.py:417
  46.8 8.4 %collective-permute-start.2 = (bf16[32,1024]{1,0:T(8,128)(2,1)S(1)}, bf16[32,1024]{1,0:T(8,128)(2,1)S(1)}, u32[]{:S(2)}, u32[]{:S(2)}) collective-permute-start(bf16[32,1024]{1,0:T(8,128)(2,1)S(1)} %get-tuple-element.46), channel_id=1, source_target_pairs={{0,6},{1,7},{2,0},{3,1},{4,2},{5,3},{6,4},{7,5},{8,14},{9,15},{10,... | collective-permute-start | bytes 196616 | tf_op jit(solution)/shard_map/ppermute | solution.py:417

commit v10 on v9

--- a/solution.py
+++ b/solution.py
@@ -137,11 +137,13 @@
     place = jnp.where(divide(pos, rows) == peer, pos - divide(pos, rows) * rows + 1, 0)
     ask_ref[...] = (place + wanted * (2 * rows)).reshape(peers, 1, rows)
     local = jnp.where(live & here, row, -1)
-    node = iota((rows, rows), 0)
-    near = jnp.zeros((rows, rows), F32)
+    node = iota((rows, rows), 0).astype(F32).astype(BF16)
+    local = local.astype(F32).astype(BF16)
+    one, none = jnp.ones((rows, rows), BF16), jnp.zeros((rows, rows), BF16)
+    near = none
     for s in range(degree):
-        near += bits(local[s : s + 1] == node)
-    near_ref[...] = near.T.astype(BF16)
+        near += jnp.where(local[s : s + 1] == node, one, none)
+    near_ref[...] = near.astype(F32).T.astype(BF16)
     far = [bits((before <= k) & (k < before + total)).astype(BF16) for k in range(CAP)]
     far = jnp.concatenate(far, axis=0)
     size = peers * CAP
@@ -281,18 +283,19 @@
 
 
 def layer_two_kernel(neigh_two_hbm, final_hbm, neigh_one_ref, ready_ref, base_ref, answer_ref, far_ref, dense_ref, *refs):
-    outs, held, final_ref, sems = refs[:-3], refs[-3], refs[-2], refs[-1]
+    outs, (held, final_ref, mean_ref, sum_ref, sems) = refs[:-5], refs[-5:]
     ready = ready_ref.shape[0]
     pieces = sems.shape[0] - 1
-    copies = fetches(neigh_two_hbm.at[pl.ds(ready, held.shape[0])], held, sems.at[pl.ds(0, pieces)])
     last = pltpu.make_async_copy(final_hbm, final_ref, sems.at[pieces])
-
     depth = held.shape[0] // pieces
+
+    def fetch(i):
+        piece = pl.ds(pl.multiple_of(i * depth, 16), depth)
+        return pltpu.make_async_copy(neigh_two_hbm.at[pl.ds(ready, held.shape[0])].at[piece], held.at[piece], sems.at[i])
 
     @pl.loop(0, pieces)
     def _(i):
-        piece = pl.ds(pl.multiple_of(i * depth, 16), depth)
-        pltpu.make_async_copy(neigh_two_hbm.at[pl.ds(ready, held.shape[0])].at[piece], held.at[piece], sems.at[i]).start()
+        fetch(i).start()
 
         @pl.when(i == pieces - 1)
         def _():
@@ -302,7 +305,14 @@
     answer = dot(dense_ref[...], load_rows(answer_ref)).astype(BF16)
     other = jnp.maximum(base_ref[...].astype(F32) + dot(answer, neigh_one_ref[...]), 0.0).astype(BF16)
     mean = over_count(dot(far[:, : other.shape[0]], other), far)
-    final = dot(mean[:, :ready], ready_ref[...]) + dot_fetched(mean[:, ready:], held, copies)
+    mean_ref[...] = mean[:, ready:]
+    sum_ref[...] = dot(mean[:, :ready], ready_ref[...])
+
+    @pl.loop(0, pieces)
+    def _(i):
+        fetch(i).wait()
+
+    final = sum_ref[...] + dot(mean_ref[...], held[...])
     last.wait()
     final = (final + final_ref[...].astype(F32)).astype(BF16)
     capacity = outs[0].shape[0]
@@ -407,7 +417,13 @@
         tuple(shape((capacity, width), BF16) for _ in range(steps)),
         (neigh_weight2, final),
         (weight, ready, base, answer_two, far_moved, dense),
-        [pltpu.VMEM((width - early, width), BF16), pltpu.VMEM((rows, width), BF16), copies((3,))],
+        [
+            pltpu.VMEM((width - early, width), BF16),
+            pltpu.VMEM((rows, width), BF16),
+            pltpu.VMEM((rows, width - early), BF16),
+            pltpu.VMEM((rows, width), F32),
+            copies((3,)),
+        ],
         2 * width * (size * width_in + rows * (size + width)),
         "layer_two",
         limit=48 << 20,

time: 56.4 us -> 56.1 us (level)
  no operation moved by 1% of the time
where the time goes in v10:
time: 56.1 us; the launch traced here: 55.7 us
  blocking collectives  27.3 us (49%)
  waiting for transfers between devices  11.1 us (20%)
  Pallas kernels  10.7 us (19%)
  starting transfers between devices  6.48 us (12%)
    all_to_all x1, blocking collectives, body(): asked = lax.all_to_all(ask, BOTH, 0, 0, tiled=True)  14.3 us
    all_to_all x1, blocking collectives, body(): answer = lax.all_to_all(reply, BOTH, 0, 0, tiled=True)  13 us
    pallas_call x6, Pallas kernels, call(): pl.pallas_call(kernel, out_shape=outs if single else (*(pltpu.HBM(a.shape...  10.7 us
    all_to_all x1, waiting for transfers between devices, body(): answer_two = lax.all_to_all(reply_two, BOTH, 0, 0, tiled=True)  6.31 us
    ppermute x3, waiting for transfers between devices, body(): lax.ppermute(finals[q], 'dev', [(i, (i + 2 * q) % members) for i in range...  4.78 us
    ppermute x3, starting transfers between devices, body(): lax.ppermute(finals[q], 'dev', [(i, (i + 2 * q) % members) for i in range...  3.87 us
    all_to_all x1, starting transfers between devices, body(): answer_two = lax.all_to_all(reply_two, BOTH, 0, 0, tiled=True)  2.6 us
  transfers between devices with their start and end apart: 4, of which 3 were waited for; matrix products, arithmetic and copies ran while one was open for 0% of the time, Pallas kernels for 9%

profile of v10, /device:TPU:0, one launch (start us, length us, event | category | flops | bytes accessed | tf_op | source)
XLA Modules:
  0.0 55.7 jit_solution(2882850525121943986)
XLA Ops:
  0.0 1.4 %ask.1 = (s32[32,1,128]{2,1,0:T(1,128)S(1)}, bf16[128,128]{1,0:T(8,128)(2,1)S(1)}, bf16[128,200]{1,0:T(8,128)(2,1)S(1)}, bf16[192,192]{1,0:T(8,128)(2,1)S(1)}, bf16[128,768]{1,0:T(8,128)(2,1)S(1)}) custom-call(s32[25,128]{1,0:T(8,128)} %bitcast.3, s32[25,128]{1,0:T(8,128)} %bitcast.4, s32[1,128]{1,0:T(1,128)} %bitcast.5, bf16[128,768]{1,0:T(8,128)(2,1)} %features_hbm.3), custom_call_target="tpu_custom_call" | custom-call | flops 9437184 | bytes 593408 | tf_op jit(solution)/shard_map/ask/pallas_call | solution.py:55
  1.4 14.3 %all_to_all.15.asked_ref = s32[32,1,128]{2,1,0:T(1,128)S(1)} all-to-all(s32[32,1,128]{2,1,0:T(1,128)S(1)} %get-tuple-element.28), channel_id=1, replica_groups=mesh['grp'=4,'dev'=8] {'grp','dev'}, dimensions={0} | all-to-all | bytes 32768 | tf_op jit(solution)/shard_map/all_to_all | solution.py:359
  15.7 0.6 %serve.1 = (bf16[32,3,2,768]{3,2,1,0:T(2,128)(2,1)S(1)}, bf16[192,128]{1,0:T(8,128)(2,1)S(1)}) custom-call(s32[32,1,128]{2,1,0:T(1,128)S(1)} %all_to_all.15.asked_ref, bf16[192,192]{1,0:T(8,128)(2,1)S(1)} %get-tuple-element.29.order_ref, bf16[128,768]{1,0:T(8,128)(2,1)S(1)} %get-tuple-element.26.source_ref.features_ref), custom_call_target="tpu_custom_call" | custom-call | flops 37748736 | bytes 630784 | tf_op jit(solution)/shard_map/serve/pallas_call | solution.py:55
  16.3 13.0 %all_to_all.16.answer_ref = bf16[32,3,2,768]{3,2,1,0:T(2,128)(2,1)S(1)} all-to-all(bf16[32,3,2,768]{3,2,1,0:T(2,128)(2,1)S(1)} %get-tuple-element.30), channel_id=1, replica_groups=mesh['grp'=4,'dev'=8] {'grp','dev'}, dimensions={0} | all-to-all | bytes 589824 | tf_op jit(solution)/shard_map/all_to_all | solution.py:369
  29.4 1.3 %layer_one.1 = (bf16[32,3,2,768]{3,2,1,0:T(2,128)(2,1)}, bf16[128,768]{1,0:T(8,128)(2,1)}, bf16[32,3,2,768]{3,2,1,0:T(2,128)(2,1)}) custom-call(bf16[128,768]{1,0:T(8,128)(2,1)S(1)} %get-tuple-element.26.source_ref.features_ref, bf16[128,128]{1,0:T(8,128)(2,1)S(1)} %get-tuple-element.27.near_ref, bf16[32,3,2,768]{3,2,1,0:T(2,128)(2,1)S(1)} %all_to_all.16.answer_ref, ...), custom_call_target="tpu_custom_call" | custom-call | flops 100663296 | bytes 1411072 | tf_op jit(solution)/shard_map/layer_one/pallas_call | solution.py:55
  30.6 2.6 %all-to-all-start.2 = ((bf16[32,3,2,768]{3,2,1,0:T(2,128)(2,1)}), bf16[32,3,2,768]{3,2,1,0:T(2,128)(2,1)S(1)}, u32[]{:S(2)}, u32[]{:S(2)}) async-start(bf16[32,3,2,768]{3,2,1,0:T(2,128)(2,1)} %get-tuple-element.40), calls=%async_computation.2 | async-start | bytes 589824 | tf_op jit(solution)/shard_map/all_to_all | solution.py:384
  33.2 5.0 %between.1 = (bf16[128,1024]{1,0:T(8,128)(2,1)}, bf16[128,128]{1,0:T(8,128)(2,1)}, bf16[96,1024]{1,0:T(8,128)(2,1)S(1)}, bf16[128,104]{1,0:T(8,128)(2,1)S(1)}, b...) custom-call(bf16[768,1024]{1,0:T(8,128)(2,1)} %self_one_hbm.1, ...), custom_call_target="tpu_custom_call" | custom-call | flops 1275068416 | bytes 11436544 | tf_op jit(solution)/shard_map/between/pallas_call | solution.py:55
  38.3 6.3 %all-to-all-done.2.answer_ref = bf16[32,3,2,768]{3,2,1,0:T(2,128)(2,1)S(1)} async-done(((bf16[32,3,2,768]{3,2,1,0:T(2,128)(2,1)}), bf16[32,3,2,768]{3,2,1,0:T(2,128)(2,1)S(1)}, u32[]{:S(2)}, u32[]{:S(2)}) %all-to-all-start.2) | async-done | bytes 294944 | tf_op jit(solution)/shard_map/all_to_all | solution.py:384
  44.6 0.0 copy-start
  44.6 1.6 %layer_two.1 = (bf16[32,1024]{1,0:T(8,128)(2,1)S(1)}, bf16[32,1024]{1,0:T(8,128)(2,1)S(1)}, bf16[32,1024]{1,0:T(8,128)(2,1)S(1)}, bf16[32,1024]{1,0:T(8,128)(2,1)S(1)}) custom-call(bf16[1024,1024]{1,0:T(8,128)(2,1)} %neigh_two_hbm.3, bf16[128,1024]{1,0:T(8,128)(2,1)} %get-tuple-element.36.final_hbm, bf16[768,1024]{1,0:T(8,128)(2,1)S(1)} %get-tuple-element.37.neigh_one_ref, ...), custom_call_target="tpu_custom_call" | custom-call | flops 620756992 | bytes 5928960 | tf_op jit(solution)/shard_map/layer_two/pallas_call | solution.py:55
  46.1 0.1 collective-permute-start
  46.2 0.2 collective-permute-start.1
  46.4 3.6 %collective-permute-start.2 = (bf16[32,1024]{1,0:T(8,128)(2,1)S(1)}, bf16[32,1024]{1,0:T(8,128)(2,1)S(1)}, u32[]{:S(2)}, u32[]{:S(2)}) collective-permute-start(bf16[32,1024]{1,0:T(8,128)(2,1)S(1)} %get-tuple-element.46), channel_id=1, source_target_pairs={{0,6},{1,7},{2,0},{3,1},{4,2},{5,3},{6,4},{7,5},{8,14},{9,15},{10,... | collective-permute-start | bytes 196616 | tf_op jit(solution)/shard_map/ppermute | solution.py:433
  50.0 3.0 %collective-permute-done.refs_1_ = bf16[32,1024]{1,0:T(8,128)(2,1)S(1)} collective-permute-done((bf16[32,1024]{1,0:T(8,128)(2,1)S(1)}, bf16[32,1024]{1,0:T(8,128)(2,1)S(1)}, u32[]{:S(2)}, u32[]{:S(2)}) %collective-permute-start) | collective-permute-done | bytes 65568 | tf_op jit(solution)/shard_map/ppermute | solution.py:433
  53.0 1.8 %collective-permute-done.1.refs_2_ = bf16[32,1024]{1,0:T(8,128)(2,1)S(1)} collective-permute-done((bf16[32,1024]{1,0:T(8,128)(2,1)S(1)}, bf16[32,1024]{1,0:T(8,128)(2,1)S(1)}, u32[]{:S(2)}, u32[]{:S(2)}) %collective-permute-start.1) | collective-permute-done | bytes 65568 | tf_op jit(solution)/shard_map/ppermute | solution.py:433
  54.8 0.0 collective-permute-done.2.refs_3_
  54.8 0.0 copy-done
  54.8 0.9 %scatter.1 = bf16[128,1024]{1,0:T(8,128)(2,1)} custom-call(bf16[128,128]{1,0:T(8,128)(2,1)S(1)} %copy-done, bf16[32,1024]{1,0:T(8,128)(2,1)S(1)} %get-tuple-element.43.refs_0_, bf16[32,1024]{1,0:T(8,128)(2,1)S(1)} %collective-permute-done.refs_1_, bf16[32,1024]{1,0:T(8,128)(2,1)S(1)} %collective-permute-done.1.refs_2_, ...), custom_call_target="tpu_custom_call" | custom-call | flops 33554432 | bytes 557056 | tf_op jit(solution)/shard_map/scatter/pallas_call | solution.py:55
Async XLA Ops:
  30.6 13.9 %all-to-all-start.2 = ((bf16[32,3,2,768]{3,2,1,0:T(2,128)(2,1)}), bf16[32,3,2,768]{3,2,1,0:T(2,128)(2,1)S(1)}, u32[]{:S(2)}, u32[]{:S(2)}) async-start(bf16[32,3,2,768]{3,2,1,0:T(2,128)(2,1)} %get-tuple-element.40), calls=%async_computation.2 | async-start | bytes 589824 | tf_op jit(solution)/shard_map/all_to_all | solution.py:384
  44.6 10.2 %copy-start = (bf16[128,128]{1,0:T(8,128)(2,1)S(1)}, bf16[128,128]{1,0:T(8,128)(2,1)}, u32[]{:S(2)}) copy-start(bf16[128,128]{1,0:T(8,128)(2,1)} %get-tuple-element.35.place_ref) | copy-start | bytes 98308
  46.1 6.9 %collective-permute-start = (bf16[32,1024]{1,0:T(8,128)(2,1)S(1)}, bf16[32,1024]{1,0:T(8,128)(2,1)S(1)}, u32[]{:S(2)}, u32[]{:S(2)}) collective-permute-start(bf16[32,1024]{1,0:T(8,128)(2,1)S(1)} %get-tuple-element.44), channel_id=1, source_target_pairs={{0,2},{1,3},{2,4},{3,5},{4,6},{5,7},{6,0},{7,1},{8,10},{9,11},{10,... | collective-permute-start | bytes 196616 | tf_op jit(solution)/shard_map/ppermute | solution.py:433
  46.2 8.6 %collective-permute-start.1 = (bf16[32,1024]{1,0:T(8,128)(2,1)S(1)}, bf16[32,1024]{1,0:T(8,128)(2,1)S(1)}, u32[]{:S(2)}, u32[]{:S(2)}) collective-permute-start(bf16[32,1024]{1,0:T(8,128)(2,1)S(1)} %get-tuple-element.45), channel_id=1, source_target_pairs={{0,4},{1,5},{2,6},{3,7},{4,0},{5,1},{6,2},{7,3},{8,12},{9,13},{10,... | collective-permute-start | bytes 196616 | tf_op jit(solution)/shard_map/ppermute | solution.py:433
  46.4 8.4 %collective-permute-start.2 = (bf16[32,1024]{1,0:T(8,128)(2,1)S(1)}, bf16[32,1024]{1,0:T(8,128)(2,1)S(1)}, u32[]{:S(2)}, u32[]{:S(2)}) collective-permute-start(bf16[32,1024]{1,0:T(8,128)(2,1)S(1)} %get-tuple-element.46), channel_id=1, source_target_pairs={{0,6},{1,7},{2,0},{3,1},{4,2},{5,3},{6,4},{7,5},{8,14},{9,15},{10,... | collective-permute-start | bytes 196616 | tf_op jit(solution)/shard_map/ppermute | solution.py:433

commit v11 on v10

--- a/solution.py
+++ b/solution.py
@@ -202,6 +202,11 @@
     sent.wait()
 
 
+def wrap(value, size):
+    value = jnp.where(value < 0, value + size, value)
+    return jnp.where(value >= size, value - size, value)
+
+
 def between_kernel(
     members, self_one_hbm, neigh_one_hbm, self_two_hbm, neigh_two_hbm, pos_hbm, features_hbm, answer_hbm, mean_hbm,
     near_ref, far_ref, asked_ref,
@@ -231,8 +236,8 @@
     line = iota((rows, rows), 0)
     step = divide(line, capacity)
     rank = line - step * capacity
-    target = me + 2 * step
-    target = jnp.where(target >= members, target - members, target)
+    sense = 2 - 4 * (me & 1)
+    target = wrap(me + sense * step, members)
     prefix = earlier(rows)
     copies[0].wait()
     goes = target == divide(pos_ref[...], rows) - first
@@ -251,8 +256,7 @@
     far_moved_ref[:, held:] = far[:, size:]
     place = jnp.zeros((rows, rows), F32)
     for q in range(members // 2):
-        source = me - 2 * q
-        source = first + jnp.where(source < 0, source + members, source)
+        source = first + wrap(me - sense * q, members)
         sent = asked_ref[source] & (2 * rows - 1)
         valid = jnp.broadcast_to(sent > 0, (rows, rows))
         before = dot(bits(valid).astype(BF16), prefix).astype(I32)
@@ -430,7 +434,7 @@
     )
     arrived = [finals[0]]
     for q in range(1, steps):
-        arrived.append(lax.ppermute(finals[q], "dev", [(i, (i + 2 * q) % members) for i in range(members)]))
+        arrived.append(lax.ppermute(finals[q], "dev", [(i, (i + (2 - 4 * (i & 1)) * q) % members) for i in range(members)]))
     return call(
         scatter_kernel,
         shape((rows, width), BF16),

time: 56.1 us -> 56.1 us (level)
  no operation moved by 1% of the time
where the time goes in v11:
time: 56.1 us; the launch traced here: 55.7 us
  blocking collectives  27.3 us (49%)
  waiting for transfers between devices  11.1 us (20%)
  Pallas kernels  10.8 us (19%)
  starting transfers between devices  6.48 us (12%)
    all_to_all x1, blocking collectives, body(): asked = lax.all_to_all(ask, BOTH, 0, 0, tiled=True)  14.3 us
    all_to_all x1, blocking collectives, body(): answer = lax.all_to_all(reply, BOTH, 0, 0, tiled=True)  13 us
    pallas_call x6, Pallas kernels, call(): pl.pallas_call(kernel, out_shape=outs if single else (*(pltpu.HBM(a.shape...  10.8 us
    all_to_all x1, waiting for transfers between devices, body(): answer_two = lax.all_to_all(reply_two, BOTH, 0, 0, tiled=True)  6.31 us
    ppermute x3, waiting for transfers between devices, body(): lax.ppermute(finals[q], 'dev', [(i, (i + (2 - 4 * (i & 1)) * q) % members...  4.81 us
    ppermute x3, starting transfers between devices, body(): lax.ppermute(finals[q], 'dev', [(i, (i + (2 - 4 * (i & 1)) * q) % members...  3.87 us
    all_to_all x1, starting transfers between devices, body(): answer_two = lax.all_to_all(reply_two, BOTH, 0, 0, tiled=True)  2.6 us
  transfers between devices with their start and end apart: 4, of which 3 were waited for; matrix products, arithmetic and copies ran while one was open for 0% of the time, Pallas kernels for 9%

profile of v11, /device:TPU:0, one launch (start us, length us, event | category | flops | bytes accessed | tf_op | source)
XLA Modules:
  0.0 55.7 jit_solution(11066966389639966397)
XLA Ops:
  0.0 1.4 %ask.1 = (s32[32,1,128]{2,1,0:T(1,128)S(1)}, bf16[128,128]{1,0:T(8,128)(2,1)S(1)}, bf16[128,200]{1,0:T(8,128)(2,1)S(1)}, bf16[192,192]{1,0:T(8,128)(2,1)S(1)}, bf16[128,768]{1,0:T(8,128)(2,1)S(1)}) custom-call(s32[25,128]{1,0:T(8,128)} %bitcast.3, s32[25,128]{1,0:T(8,128)} %bitcast.4, s32[1,128]{1,0:T(1,128)} %bitcast.5, bf16[128,768]{1,0:T(8,128)(2,1)} %features_hbm.3), custom_call_target="tpu_custom_call" | custom-call | flops 9437184 | bytes 593408 | tf_op jit(solution)/shard_map/ask/pallas_call | solution.py:55
  1.4 14.3 %all_to_all.15.asked_ref = s32[32,1,128]{2,1,0:T(1,128)S(1)} all-to-all(s32[32,1,128]{2,1,0:T(1,128)S(1)} %get-tuple-element.28), channel_id=1, replica_groups=mesh['grp'=4,'dev'=8] {'grp','dev'}, dimensions={0} | all-to-all | bytes 32768 | tf_op jit(solution)/shard_map/all_to_all | solution.py:363
  15.7 0.6 %serve.1 = (bf16[32,3,2,768]{3,2,1,0:T(2,128)(2,1)S(1)}, bf16[192,128]{1,0:T(8,128)(2,1)S(1)}) custom-call(s32[32,1,128]{2,1,0:T(1,128)S(1)} %all_to_all.15.asked_ref, bf16[192,192]{1,0:T(8,128)(2,1)S(1)} %get-tuple-element.29.order_ref, bf16[128,768]{1,0:T(8,128)(2,1)S(1)} %get-tuple-element.26.source_ref.features_ref), custom_call_target="tpu_custom_call" | custom-call | flops 37748736 | bytes 630784 | tf_op jit(solution)/shard_map/serve/pallas_call | solution.py:55
  16.3 13.0 %all_to_all.16.answer_ref = bf16[32,3,2,768]{3,2,1,0:T(2,128)(2,1)S(1)} all-to-all(bf16[32,3,2,768]{3,2,1,0:T(2,128)(2,1)S(1)} %get-tuple-element.30), channel_id=1, replica_groups=mesh['grp'=4,'dev'=8] {'grp','dev'}, dimensions={0} | all-to-all | bytes 589824 | tf_op jit(solution)/shard_map/all_to_all | solution.py:373
  29.4 1.3 %layer_one.1 = (bf16[32,3,2,768]{3,2,1,0:T(2,128)(2,1)}, bf16[128,768]{1,0:T(8,128)(2,1)}, bf16[32,3,2,768]{3,2,1,0:T(2,128)(2,1)}) custom-call(bf16[128,768]{1,0:T(8,128)(2,1)S(1)} %get-tuple-element.26.source_ref.features_ref, bf16[128,128]{1,0:T(8,128)(2,1)S(1)} %get-tuple-element.27.near_ref, bf16[32,3,2,768]{3,2,1,0:T(2,128)(2,1)S(1)} %all_to_all.16.answer_ref, ...), custom_call_target="tpu_custom_call" | custom-call | flops 100663296 | bytes 1411072 | tf_op jit(solution)/shard_map/layer_one/pallas_call | solution.py:55
  30.6 2.6 %all-to-all-start.2 = ((bf16[32,3,2,768]{3,2,1,0:T(2,128)(2,1)}), bf16[32,3,2,768]{3,2,1,0:T(2,128)(2,1)S(1)}, u32[]{:S(2)}, u32[]{:S(2)}) async-start(bf16[32,3,2,768]{3,2,1,0:T(2,128)(2,1)} %get-tuple-element.40), calls=%async_computation.2 | async-start | bytes 589824 | tf_op jit(solution)/shard_map/all_to_all | solution.py:388
  33.2 5.0 %between.1 = (bf16[128,1024]{1,0:T(8,128)(2,1)}, bf16[128,128]{1,0:T(8,128)(2,1)}, bf16[96,1024]{1,0:T(8,128)(2,1)S(1)}, bf16[128,104]{1,0:T(8,128)(2,1)S(1)}, b...) custom-call(bf16[768,1024]{1,0:T(8,128)(2,1)} %self_one_hbm.1, ...), custom_call_target="tpu_custom_call" | custom-call | flops 1275068416 | bytes 11436544 | tf_op jit(solution)/shard_map/between/pallas_call | solution.py:55
  38.3 6.3 %all-to-all-done.2.answer_ref = bf16[32,3,2,768]{3,2,1,0:T(2,128)(2,1)S(1)} async-done(((bf16[32,3,2,768]{3,2,1,0:T(2,128)(2,1)}), bf16[32,3,2,768]{3,2,1,0:T(2,128)(2,1)S(1)}, u32[]{:S(2)}, u32[]{:S(2)}) %all-to-all-start.2) | async-done | bytes 294944 | tf_op jit(solution)/shard_map/all_to_all | solution.py:388
  44.6 0.0 copy-start
  44.6 1.6 %layer_two.1 = (bf16[32,1024]{1,0:T(8,128)(2,1)S(1)}, bf16[32,1024]{1,0:T(8,128)(2,1)S(1)}, bf16[32,1024]{1,0:T(8,128)(2,1)S(1)}, bf16[32,1024]{1,0:T(8,128)(2,1)S(1)}) custom-call(bf16[1024,1024]{1,0:T(8,128)(2,1)} %neigh_two_hbm.3, bf16[128,1024]{1,0:T(8,128)(2,1)} %get-tuple-element.36.final_hbm, bf16[768,1024]{1,0:T(8,128)(2,1)S(1)} %get-tuple-element.37.neigh_one_ref, ...), custom_call_target="tpu_custom_call" | custom-call | flops 620756992 | bytes 5928960 | tf_op jit(solution)/shard_map/layer_two/pallas_call | solution.py:55
  46.1 0.1 collective-permute-start
  46.2 0.2 collective-permute-start.1
  46.4 3.6 %collective-permute-start.2 = (bf16[32,1024]{1,0:T(8,128)(2,1)S(1)}, bf16[32,1024]{1,0:T(8,128)(2,1)S(1)}, u32[]{:S(2)}, u32[]{:S(2)}) collective-permute-start(bf16[32,1024]{1,0:T(8,128)(2,1)S(1)} %get-tuple-element.46), channel_id=1, source_target_pairs={{0,6},{1,3},{2,0},{3,5},{4,2},{5,7},{6,4},{7,1},{8,14},{9,11},{10,... | collective-permute-start | bytes 196616 | tf_op jit(solution)/shard_map/ppermute | solution.py:437
  50.0 3.1 %collective-permute-done.refs_1_ = bf16[32,1024]{1,0:T(8,128)(2,1)S(1)} collective-permute-done((bf16[32,1024]{1,0:T(8,128)(2,1)S(1)}, bf16[32,1024]{1,0:T(8,128)(2,1)S(1)}, u32[]{:S(2)}, u32[]{:S(2)}) %collective-permute-start) | collective-permute-done | bytes 65568 | tf_op jit(solution)/shard_map/ppermute | solution.py:437
  53.1 1.7 %collective-permute-done.1.refs_2_ = bf16[32,1024]{1,0:T(8,128)(2,1)S(1)} collective-permute-done((bf16[32,1024]{1,0:T(8,128)(2,1)S(1)}, bf16[32,1024]{1,0:T(8,128)(2,1)S(1)}, u32[]{:S(2)}, u32[]{:S(2)}) %collective-permute-start.1) | collective-permute-done | bytes 65568 | tf_op jit(solution)/shard_map/ppermute | solution.py:437
  54.8 0.0 collective-permute-done.2.refs_3_
  54.8 0.0 copy-done
  54.8 0.9 %scatter.1 = bf16[128,1024]{1,0:T(8,128)(2,1)} custom-call(bf16[128,128]{1,0:T(8,128)(2,1)S(1)} %copy-done, bf16[32,1024]{1,0:T(8,128)(2,1)S(1)} %get-tuple-element.43.refs_0_, bf16[32,1024]{1,0:T(8,128)(2,1)S(1)} %collective-permute-done.refs_1_, bf16[32,1024]{1,0:T(8,128)(2,1)S(1)} %collective-permute-done.1.refs_2_, ...), custom_call_target="tpu_custom_call" | custom-call | flops 33554432 | bytes 557056 | tf_op jit(solution)/shard_map/scatter/pallas_call | solution.py:55
Async XLA Ops:
  30.6 13.9 %all-to-all-start.2 = ((bf16[32,3,2,768]{3,2,1,0:T(2,128)(2,1)}), bf16[32,3,2,768]{3,2,1,0:T(2,128)(2,1)S(1)}, u32[]{:S(2)}, u32[]{:S(2)}) async-start(bf16[32,3,2,768]{3,2,1,0:T(2,128)(2,1)} %get-tuple-element.40), calls=%async_computation.2 | async-start | bytes 589824 | tf_op jit(solution)/shard_map/all_to_all | solution.py:388
  44.6 10.3 %copy-start = (bf16[128,128]{1,0:T(8,128)(2,1)S(1)}, bf16[128,128]{1,0:T(8,128)(2,1)}, u32[]{:S(2)}) copy-start(bf16[128,128]{1,0:T(8,128)(2,1)} %get-tuple-element.35.place_ref) | copy-start | bytes 98308
  46.1 7.0 %collective-permute-start = (bf16[32,1024]{1,0:T(8,128)(2,1)S(1)}, bf16[32,1024]{1,0:T(8,128)(2,1)S(1)}, u32[]{:S(2)}, u32[]{:S(2)}) collective-permute-start(bf16[32,1024]{1,0:T(8,128)(2,1)S(1)} %get-tuple-element.44), channel_id=1, source_target_pairs={{0,2},{1,7},{2,4},{3,1},{4,6},{5,3},{6,0},{7,5},{8,10},{9,15},{10,... | collective-permute-start | bytes 196616 | tf_op jit(solution)/shard_map/ppermute | solution.py:437
  46.2 8.6 %collective-permute-start.1 = (bf16[32,1024]{1,0:T(8,128)(2,1)S(1)}, bf16[32,1024]{1,0:T(8,128)(2,1)S(1)}, u32[]{:S(2)}, u32[]{:S(2)}) collective-permute-start(bf16[32,1024]{1,0:T(8,128)(2,1)S(1)} %get-tuple-element.45), channel_id=1, source_target_pairs={{0,4},{1,5},{2,6},{3,7},{4,0},{5,1},{6,2},{7,3},{8,12},{9,13},{10,... | collective-permute-start | bytes 196616 | tf_op jit(solution)/shard_map/ppermute | solution.py:437
  46.4 8.4 %collective-permute-start.2 = (bf16[32,1024]{1,0:T(8,128)(2,1)S(1)}, bf16[32,1024]{1,0:T(8,128)(2,1)S(1)}, u32[]{:S(2)}, u32[]{:S(2)}) collective-permute-start(bf16[32,1024]{1,0:T(8,128)(2,1)S(1)} %get-tuple-element.46), channel_id=1, source_target_pairs={{0,6},{1,3},{2,0},{3,5},{4,2},{5,7},{6,4},{7,1},{8,14},{9,11},{10,... | collective-permute-start | bytes 196616 | tf_op jit(solution)/shard_map/ppermute | solution.py:437

commit v12 on v10

--- a/solution.py
+++ b/solution.py
@@ -99,9 +99,23 @@
         copy.start()
     own = lax.axis_index("grp") * members + lax.axis_index("dev")
     peer = iota((peers, rows), 0)
+    size = peers * CAP
+    line = iota((size, size), 0)
+    device = divide(line, CAP)
+    order_ref[...] = bits(iota((size, size), 1) == (line - device * CAP) * peers + device).astype(BF16)
+
+    @pl.loop(0, 2)
+    def _(i):
+        @pl.when(i == 0)
+        def _():
+            copies[0].wait()
+            copies[1].wait()
+
+        @pl.when(i == 1)
+        def _():
+            copies[2].wait()
+
     prefix = earlier(rows)
-    for copy in copies:
-        copy.wait()
     slots = jnp.where(mask[...] > 0, ids[...], -1)
     owner = divide(jnp.maximum(slots, 0), rows)
     row = slots - owner * rows
@@ -146,12 +160,7 @@
     near_ref[...] = near.astype(F32).T.astype(BF16)
     far = [bits((before <= k) & (k < before + total)).astype(BF16) for k in range(CAP)]
     far = jnp.concatenate(far, axis=0)
-    size = peers * CAP
-    line = iota((size, size), 0)
-    device = divide(line, CAP)
-    order = bits(iota((size, size), 1) == (line - device * CAP) * peers + device).astype(BF16)
-    order_ref[...] = order
-    far_ref[:, :size] = dot(order, far).T.astype(BF16)
+    far_ref[:, :size] = dot(order_ref[...], far).T.astype(BF16)
     count = jnp.broadcast_to(jnp.sum(bits(live), axis=0, keepdims=True), (rows, rows)).T.astype(BF16)
     far_ref[:, size:] = count[:, : far_ref.shape[1] - size]
     table.wait()
@@ -203,19 +212,18 @@
 
 
 def between_kernel(
-    members, self_one_hbm, neigh_one_hbm, self_two_hbm, neigh_two_hbm, pos_hbm, features_hbm, answer_hbm, mean_hbm,
-    near_ref, far_ref, asked_ref,
-    final_hbm, place_hbm, base_ref, far_moved_ref, dense_ref, neigh_one_ref, ready_ref,
+    members, self_one_hbm, self_two_hbm, neigh_two_hbm, pos_hbm, features_hbm, answer_hbm, mean_hbm,
+    neigh_one_ref, near_ref, far_ref, asked_ref,
+    final_hbm, place_hbm, base_ref, far_moved_ref, dense_ref, ready_ref,
     held_one, held_two, rest, features_ref, answer_ref, mean_ref, final_ref, place_ref, pos_ref, sems,
 ):
     ready = ready_ref.shape[0]
     copies = [
         pltpu.make_async_copy(pos_hbm, pos_ref, sems.at[0]),
         pltpu.make_async_copy(self_one_hbm, held_one, sems.at[1]),
-        pltpu.make_async_copy(neigh_one_hbm, neigh_one_ref, sems.at[2]),
-        pltpu.make_async_copy(self_two_hbm, held_two, sems.at[3]),
-        pltpu.make_async_copy(neigh_two_hbm.at[pl.ds(0, ready)], ready_ref, sems.at[4]),
-        pltpu.make_async_copy(neigh_two_hbm.at[pl.ds(ready, rest.shape[0])], rest, sems.at[5]),
+        pltpu.make_async_copy(self_two_hbm, held_two, sems.at[2]),
+        pltpu.make_async_copy(neigh_two_hbm.at[pl.ds(0, ready)], ready_ref, sems.at[3]),
+        pltpu.make_async_copy(neigh_two_hbm.at[pl.ds(ready, rest.shape[0])], rest, sems.at[4]),
     ]
     inputs = [
         pltpu.make_async_copy(features_hbm, features_ref, sems.at[6]),
@@ -266,15 +274,14 @@
         copy.wait()
     own = dot(features_ref[...], held_one[...])
     base_ref[...] = dot(dot(dense, load_rows(answer_ref)).astype(BF16), held_one[...]).astype(BF16)
-    copies[2].wait()
     hidden = jnp.maximum(own + dot(mean_ref[...], neigh_one_ref[...]), 0.0).astype(BF16)
     mean = over_count(dot(near, hidden), far)
     moved = dot(move, hidden).astype(BF16)
+    copies[2].wait()
+    final = dot(moved, held_two[...])
     copies[3].wait()
-    final = dot(moved, held_two[...])
+    final += dot(mean[:, :ready], ready_ref[...])
     copies[4].wait()
-    final += dot(mean[:, :ready], ready_ref[...])
-    copies[5].wait()
     final_ref[...] = (final + dot(mean[:, ready:], rest[...])).astype(BF16)
     away = pltpu.make_async_copy(final_ref, final_hbm, sems.at[10])
     away.start()
@@ -382,7 +389,7 @@
         away=3,
     )
     answer_two = lax.all_to_all(reply_two, BOTH, 0, 0, tiled=True)
-    final, place, base, far_moved, dense, weight, ready = call(
+    final, place, base, far_moved, dense, ready = call(
         functools.partial(between_kernel, members),
         (
             shape((rows, width), BF16),
@@ -390,11 +397,10 @@
             shape((held, width), BF16),
             shape((rows, held + 8), BF16),
             shape((held, size), BF16),
-            shape((width_in, width), BF16),
             shape((early, width), BF16),
         ),
-        (self_weight1, neigh_weight1, self_weight2, neigh_weight2, pos, features, kept, mean),
-        (near, far, asked),
+        (self_weight1, self_weight2, neigh_weight2, pos, features, kept, mean),
+        (neigh_weight1, near, far, asked),
         [
             pltpu.VMEM((width_in, width), BF16),
             pltpu.VMEM((width, width), BF16),
@@ -416,7 +422,7 @@
         layer_two_kernel,
         tuple(shape((capacity, width), BF16) for _ in range(steps)),
         (neigh_weight2, final),
-        (weight, ready, base, answer_two, far_moved, dense),
+        (neigh_weight1, ready, base, answer_two, far_moved, dense),
         [
             pltpu.VMEM((width - early, width), BF16),
             pltpu.VMEM((rows, width), BF16),

time: 56.1 us -> 56.1 us (level)
  no operation moved by 1% of the time
where the time goes in v12:
time: 56.1 us; the launch traced here: 55.8 us
  blocking collectives  27.3 us (49%)
  waiting for transfers between devices  11.3 us (20%)
  Pallas kernels  10.7 us (19%)
  starting transfers between devices  6.48 us (12%)
    all_to_all x1, blocking collectives, body(): asked = lax.all_to_all(ask, BOTH, 0, 0, tiled=True)  14.3 us
    all_to_all x1, blocking collectives, body(): answer = lax.all_to_all(reply, BOTH, 0, 0, tiled=True)  13 us
    pallas_call x6, Pallas kernels, call(): pl.pallas_call(kernel, out_shape=outs if single else (*(pltpu.HBM(a.shape...  10.7 us
    all_to_all x1, waiting for transfers between devices, body(): answer_two = lax.all_to_all(reply_two, BOTH, 0, 0, tiled=True)  6.47 us
    ppermute x3, waiting for transfers between devices, body(): lax.ppermute(finals[q], 'dev', [(i, (i + 2 * q) % members) for i in range...  4.8 us
    ppermute x3, starting transfers between devices, body(): lax.ppermute(finals[q], 'dev', [(i, (i + 2 * q) % members) for i in range...  3.87 us
    all_to_all x1, starting transfers between devices, body(): answer_two = lax.all_to_all(reply_two, BOTH, 0, 0, tiled=True)  2.6 us
  transfers between devices with their start and end apart: 4, of which 3 were waited for; matrix products, arithmetic and copies ran while one was open for 0% of the time, Pallas kernels for 9%

profile of v12, /device:TPU:0, one launch (start us, length us, event | category | flops | bytes accessed | tf_op | source)
XLA Modules:
  0.0 55.8 jit_solution(4170477171243369966)
XLA Ops:
  0.0 0.0 copy-start
  0.0 1.5 %ask.1 = (s32[32,1,128]{2,1,0:T(1,128)S(1)}, bf16[128,128]{1,0:T(8,128)(2,1)S(1)}, bf16[128,200]{1,0:T(8,128)(2,1)S(1)}, bf16[192,192]{1,0:T(8,128)(2,1)S(1)}, bf16[128,768]{1,0:T(8,128)(2,1)S(1)}) custom-call(s32[25,128]{1,0:T(8,128)} %bitcast.3, s32[25,128]{1,0:T(8,128)} %bitcast.4, s32[1,128]{1,0:T(1,128)} %bitcast.5, bf16[128,768]{1,0:T(8,128)(2,1)} %features_hbm.3), custom_call_target="tpu_custom_call" | custom-call | flops 9437184 | bytes 593408 | tf_op jit(solution)/shard_map/ask/pallas_call | solution.py:55
  1.5 14.3 %all_to_all.15.asked_ref = s32[32,1,128]{2,1,0:T(1,128)S(1)} all-to-all(s32[32,1,128]{2,1,0:T(1,128)S(1)} %get-tuple-element.27), channel_id=1, replica_groups=mesh['grp'=4,'dev'=8] {'grp','dev'}, dimensions={0} | all-to-all | bytes 32768 | tf_op jit(solution)/shard_map/all_to_all | solution.py:366
  15.8 0.6 %serve.1 = (bf16[32,3,2,768]{3,2,1,0:T(2,128)(2,1)S(1)}, bf16[192,128]{1,0:T(8,128)(2,1)S(1)}) custom-call(s32[32,1,128]{2,1,0:T(1,128)S(1)} %all_to_all.15.asked_ref, bf16[192,192]{1,0:T(8,128)(2,1)S(1)} %get-tuple-element.28.order_ref, bf16[128,768]{1,0:T(8,128)(2,1)S(1)} %get-tuple-element.25.source_ref.features_ref), custom_call_target="tpu_custom_call" | custom-call | flops 37748736 | bytes 630784 | tf_op jit(solution)/shard_map/serve/pallas_call | solution.py:55
  16.5 13.0 %all_to_all.16.answer_ref = bf16[32,3,2,768]{3,2,1,0:T(2,128)(2,1)S(1)} all-to-all(bf16[32,3,2,768]{3,2,1,0:T(2,128)(2,1)S(1)} %get-tuple-element.29), channel_id=1, replica_groups=mesh['grp'=4,'dev'=8] {'grp','dev'}, dimensions={0} | all-to-all | bytes 589824 | tf_op jit(solution)/shard_map/all_to_all | solution.py:376
  29.5 1.3 %layer_one.1 = (bf16[32,3,2,768]{3,2,1,0:T(2,128)(2,1)}, bf16[128,768]{1,0:T(8,128)(2,1)}, bf16[32,3,2,768]{3,2,1,0:T(2,128)(2,1)}) custom-call(bf16[128,768]{1,0:T(8,128)(2,1)S(1)} %get-tuple-element.25.source_ref.features_ref, bf16[128,128]{1,0:T(8,128)(2,1)S(1)} %get-tuple-element.26.near_ref, bf16[32,3,2,768]{3,2,1,0:T(2,128)(2,1)S(1)} %all_to_all.16.answer_ref, ...), custom_call_target="tpu_custom_call" | custom-call | flops 100663296 | bytes 1411072 | tf_op jit(solution)/shard_map/layer_one/pallas_call | solution.py:55
  30.7 2.6 %all-to-all-start.2 = ((bf16[32,3,2,768]{3,2,1,0:T(2,128)(2,1)}), bf16[32,3,2,768]{3,2,1,0:T(2,128)(2,1)S(1)}, u32[]{:S(2)}, u32[]{:S(2)}) async-start(bf16[32,3,2,768]{3,2,1,0:T(2,128)(2,1)} %get-tuple-element.38), calls=%async_computation.2 | async-start | bytes 589824 | tf_op jit(solution)/shard_map/all_to_all | solution.py:391
  33.4 0.0 copy-done
  33.4 4.8 %between.1 = (bf16[128,1024]{1,0:T(8,128)(2,1)}, bf16[128,128]{1,0:T(8,128)(2,1)}, bf16[96,1024]{1,0:T(8,128)(2,1)S(1)}, bf16[128,104]{1,0:T(8,128)(2,1)S(1)}, b...) custom-call(bf16[768,1024]{1,0:T(8,128)(2,1)} %self_one_hbm.1, bf16[1024,1024]{1,0:T(8,128)(2,1)} %self_two_hbm.1, ...), custom_call_target="tpu_custom_call" | custom-call | flops 1275068416 | bytes 9863680 | tf_op jit(solution)/shard_map/between/pallas_call | solution.py:55
  38.2 6.5 %all-to-all-done.2.answer_ref = bf16[32,3,2,768]{3,2,1,0:T(2,128)(2,1)S(1)} async-done(((bf16[32,3,2,768]{3,2,1,0:T(2,128)(2,1)}), bf16[32,3,2,768]{3,2,1,0:T(2,128)(2,1)S(1)}, u32[]{:S(2)}, u32[]{:S(2)}) %all-to-all-start.2) | async-done | bytes 294944 | tf_op jit(solution)/shard_map/all_to_all | solution.py:391
  44.7 0.0 copy-start.1
  44.7 1.5 %layer_two.1 = (bf16[32,1024]{1,0:T(8,128)(2,1)S(1)}, bf16[32,1024]{1,0:T(8,128)(2,1)S(1)}, bf16[32,1024]{1,0:T(8,128)(2,1)S(1)}, bf16[32,1024]{1,0:T(8,128)(2,1)S(1)}) custom-call(bf16[1024,1024]{1,0:T(8,128)(2,1)} %neigh_two_hbm.3, bf16[128,1024]{1,0:T(8,128)(2,1)} %get-tuple-element.35.final_hbm, bf16[768,1024]{1,0:T(8,128)(2,1)S(1)} %copy-done, ...), custom_call_target="tpu_custom_call" | custom-call | flops 620756992 | bytes 5928960 | tf_op jit(solution)/shard_map/layer_two/pallas_call | solution.py:55
  46.2 0.1 collective-permute-start
  46.3 0.3 collective-permute-start.1
  46.6 3.5 %collective-permute-start.2 = (bf16[32,1024]{1,0:T(8,128)(2,1)S(1)}, bf16[32,1024]{1,0:T(8,128)(2,1)S(1)}, u32[]{:S(2)}, u32[]{:S(2)}) collective-permute-start(bf16[32,1024]{1,0:T(8,128)(2,1)S(1)} %get-tuple-element.44), channel_id=1, source_target_pairs={{0,6},{1,7},{2,0},{3,1},{4,2},{5,3},{6,4},{7,5},{8,14},{9,15},{10,... | collective-permute-start | bytes 196616 | tf_op jit(solution)/shard_map/ppermute | solution.py:439
  50.1 3.0 %collective-permute-done.refs_1_ = bf16[32,1024]{1,0:T(8,128)(2,1)S(1)} collective-permute-done((bf16[32,1024]{1,0:T(8,128)(2,1)S(1)}, bf16[32,1024]{1,0:T(8,128)(2,1)S(1)}, u32[]{:S(2)}, u32[]{:S(2)}) %collective-permute-start) | collective-permute-done | bytes 65568 | tf_op jit(solution)/shard_map/ppermute | solution.py:439
  53.1 1.8 %collective-permute-done.1.refs_2_ = bf16[32,1024]{1,0:T(8,128)(2,1)S(1)} collective-permute-done((bf16[32,1024]{1,0:T(8,128)(2,1)S(1)}, bf16[32,1024]{1,0:T(8,128)(2,1)S(1)}, u32[]{:S(2)}, u32[]{:S(2)}) %collective-permute-start.1) | collective-permute-done | bytes 65568 | tf_op jit(solution)/shard_map/ppermute | solution.py:439
  54.9 0.0 collective-permute-done.2.refs_3_
  54.9 0.0 copy-done.1
  54.9 0.9 %scatter.1 = bf16[128,1024]{1,0:T(8,128)(2,1)} custom-call(bf16[128,128]{1,0:T(8,128)(2,1)S(1)} %copy-done.1, bf16[32,1024]{1,0:T(8,128)(2,1)S(1)} %get-tuple-element.41.refs_0_, bf16[32,1024]{1,0:T(8,128)(2,1)S(1)} %collective-permute-done.refs_1_, bf16[32,1024]{1,0:T(8,128)(2,1)S(1)} %collective-permute-done.1.refs_2_, ...), custom_call_target="tpu_custom_call" | custom-call | flops 33554432 | bytes 557056 | tf_op jit(solution)/shard_map/scatter/pallas_call | solution.py:55
Async XLA Ops:
  0.0 33.4 %copy-start = (bf16[768,1024]{1,0:T(8,128)(2,1)S(1)}, bf16[768,1024]{1,0:T(8,128)(2,1)}, u32[]{:S(2)}) copy-start(bf16[768,1024]{1,0:T(8,128)(2,1)} %neigh_one_ref.3) | copy-start | bytes 4718596
  30.7 13.9 %all-to-all-start.2 = ((bf16[32,3,2,768]{3,2,1,0:T(2,128)(2,1)}), bf16[32,3,2,768]{3,2,1,0:T(2,128)(2,1)S(1)}, u32[]{:S(2)}, u32[]{:S(2)}) async-start(bf16[32,3,2,768]{3,2,1,0:T(2,128)(2,1)} %get-tuple-element.38), calls=%async_computation.2 | async-start | bytes 589824 | tf_op jit(solution)/shard_map/all_to_all | solution.py:391
  44.7 10.2 %copy-start.1 = (bf16[128,128]{1,0:T(8,128)(2,1)S(1)}, bf16[128,128]{1,0:T(8,128)(2,1)}, u32[]{:S(2)}) copy-start(bf16[128,128]{1,0:T(8,128)(2,1)} %get-tuple-element.34.place_ref) | copy-start | bytes 98308
  46.2 6.9 %collective-permute-start = (bf16[32,1024]{1,0:T(8,128)(2,1)S(1)}, bf16[32,1024]{1,0:T(8,128)(2,1)S(1)}, u32[]{:S(2)}, u32[]{:S(2)}) collective-permute-start(bf16[32,1024]{1,0:T(8,128)(2,1)S(1)} %get-tuple-element.42), channel_id=1, source_target_pairs={{0,2},{1,3},{2,4},{3,5},{4,6},{5,7},{6,0},{7,1},{8,10},{9,11},{10,... | collective-permute-start | bytes 196616 | tf_op jit(solution)/shard_map/ppermute | solution.py:439
  46.3 8.6 %collective-permute-start.1 = (bf16[32,1024]{1,0:T(8,128)(2,1)S(1)}, bf16[32,1024]{1,0:T(8,128)(2,1)S(1)}, u32[]{:S(2)}, u32[]{:S(2)}) collective-permute-start(bf16[32,1024]{1,0:T(8,128)(2,1)S(1)} %get-tuple-element.43), channel_id=1, source_target_pairs={{0,4},{1,5},{2,6},{3,7},{4,0},{5,1},{6,2},{7,3},{8,12},{9,13},{10,... | collective-permute-start | bytes 196616 | tf_op jit(solution)/shard_map/ppermute | solution.py:439
  46.6 8.4 %collective-permute-start.2 = (bf16[32,1024]{1,0:T(8,128)(2,1)S(1)}, bf16[32,1024]{1,0:T(8,128)(2,1)S(1)}, u32[]{:S(2)}, u32[]{:S(2)}) collective-permute-start(bf16[32,1024]{1,0:T(8,128)(2,1)S(1)} %get-tuple-element.44), channel_id=1, source_target_pairs={{0,6},{1,7},{2,0},{3,1},{4,2},{5,3},{6,4},{7,5},{8,14},{9,15},{10,... | collective-permute-start | bytes 196616 | tf_op jit(solution)/shard_map/ppermute | solution.py:439

commit v13 on v10

--- a/solution.py
+++ b/solution.py
@@ -7,6 +7,7 @@
 from jax.experimental.pallas import tpu as pltpu
 from jax.sharding import PartitionSpec as P
 
+
 CAP = 6
 BOTH = ("grp", "dev")
 F32 = jnp.float32
@@ -48,7 +49,7 @@
     return [pl.BlockSpec(memory_space=pltpu.HBM)] * n
 
 
-def call(kernel, outs, remote, operands, scratch, flops, name, limit=24 << 20, away=0):
+def call(kernel, outs, remote, operands, scratch, flops, limit=24 << 20, away=0):
     single = not isinstance(outs, tuple)
     leaves = (outs,) if single else outs
     moved = sum(a.size * a.dtype.itemsize for a in (*remote, *operands, *leaves))
@@ -60,29 +61,7 @@
         scratch_shapes=scratch,
         compiler_params=pltpu.CompilerParams(vmem_limit_bytes=limit),
         cost_estimate=pl.CostEstimate(flops=flops, bytes_accessed=moved, transcendentals=0),
-        name=name,
     )(*(pltpu.with_memory_space_constraint(a, pltpu.HBM) for a in remote), *operands)
-
-
-def fetches(weight_ref, held, sems):
-    pieces = sems.shape[0]
-    depth = weight_ref.shape[0] // pieces
-    return [
-        pltpu.make_async_copy(
-            weight_ref.at[pl.ds(i * depth, depth)], held.at[pl.ds(i * depth, depth)], sems.at[i]
-        )
-        for i in range(pieces)
-    ]
-
-
-def dot_fetched(left, held, copies):
-    depth = held.shape[0] // len(copies)
-    result = None
-    for i, copy in enumerate(copies):
-        copy.wait()
-        part = dot(left[:, i * depth : (i + 1) * depth], held[i * depth : (i + 1) * depth])
-        result = part if result is None else result + part
-    return result
 
 
 def ask_kernel(
@@ -231,8 +210,7 @@
     line = iota((rows, rows), 0)
     step = divide(line, capacity)
     rank = line - step * capacity
-    target = me + 2 * step
-    target = jnp.where(target >= members, target - members, target)
+    target = me ^ (2 * step)
     prefix = earlier(rows)
     copies[0].wait()
     goes = target == divide(pos_ref[...], rows) - first
@@ -251,8 +229,7 @@
     far_moved_ref[:, held:] = far[:, size:]
     place = jnp.zeros((rows, rows), F32)
     for q in range(members // 2):
-        source = me - 2 * q
-        source = first + jnp.where(source < 0, source + members, source)
+        source = first + (me ^ (2 * q))
         sent = asked_ref[source] & (2 * rows - 1)
         valid = jnp.broadcast_to(sent > 0, (rows, rows))
         before = dot(bits(valid).astype(BF16), prefix).astype(I32)
@@ -326,7 +303,7 @@
     out_ref[...] = dot(place_ref[...], arrived).astype(BF16)
 
 
-def body(features, neighbours, neighbour_mask, layer2_position, self_weight1, neigh_weight1, self_weight2, neigh_weight2):
+def compute(features, neighbours, neighbour_mask, layer2_position, self_weight1, neigh_weight1, self_weight2, neigh_weight2):
     rows, degree = neighbours.shape
     members = lax.axis_size("dev")
     peers = lax.axis_size("grp") * members
@@ -353,7 +330,6 @@
         (),
         [pltpu.VMEM((degree, rows), I32), pltpu.VMEM((degree, rows), I32), pltpu.VMEM((1, rows), I32), copies((4,))],
         2 * size * size * rows,
-        "ask",
         limit=40 << 20,
     )
     asked = lax.all_to_all(ask, BOTH, 0, 0, tiled=True)
@@ -364,7 +340,6 @@
         (asked, order, table),
         [],
         2 * size * rows * width_in,
-        "serve",
     )
     answer = lax.all_to_all(reply, BOTH, 0, 0, tiled=True)
     kept, mean, reply_two = call(
@@ -378,7 +353,6 @@
         (table, near, answer, far, pick),
         [pltpu.VMEM((rows, width_in), BF16), pltpu.VMEM((peers, CAP // 2, 2, width_in), BF16), copies((3,))],
         2 * rows * width_in * (size + rows) + 2 * size * rows * width_in,
-        "layer_one",
         away=3,
     )
     answer_two = lax.all_to_all(reply_two, BOTH, 0, 0, tiled=True)
@@ -408,7 +382,6 @@
             copies((11,)),
         ],
         2 * width * (rows * (2 * width_in + rows + 2 * width) + size * width_in),
-        "between",
         limit=48 << 20,
         away=2,
     )
@@ -425,26 +398,17 @@
             copies((3,)),
         ],
         2 * width * (size * width_in + rows * (size + width)),
-        "layer_two",
         limit=48 << 20,
     )
     arrived = [finals[0]]
     for q in range(1, steps):
-        arrived.append(lax.ppermute(finals[q], "dev", [(i, (i + 2 * q) % members) for i in range(members)]))
-    return call(
-        scatter_kernel,
-        shape((rows, width), BF16),
-        (),
-        (place, *arrived),
-        [],
-        2 * rows * rows * width,
-        "scatter",
-    )
+        arrived.append(lax.ppermute(finals[q], "dev", [(i, i ^ (2 * q)) for i in range(members)]))
+    return call(scatter_kernel, shape((rows, width), BF16), (), (place, *arrived), [], 2 * rows * rows * width)
 
 
 def solution(mesh):
     return jax.shard_map(
-        body,
+        compute,
         mesh=mesh,
         in_specs=(
             P(BOTH, None),

time: 56.1 us -> 56.1 us (level)
  waiting for transfers between devices: 11.1 us -> 10.5 us
  starting transfers between devices: 6.48 us -> 7.05 us
    ppermute x3, waiting for transfers between devices: 4.78 us -> 4.2 us  [compute(): lax.ppermute(finals[q], 'dev', [(i, i ^ 2 * q) for i in range(members)])]
    ppermute x3, starting transfers between devices: 3.87 us -> 4.44 us  [compute(): lax.ppermute(finals[q], 'dev', [(i, i ^ 2 * q) for i in range(members)])]
where the time goes in v13:
time: 56.1 us; the launch traced here: 55.7 us
  blocking collectives  27.3 us (49%)
  Pallas kernels  10.8 us (19%)
  waiting for transfers between devices  10.5 us (19%)
  starting transfers between devices  7.05 us (13%)
    all_to_all x1, blocking collectives, compute(): asked = lax.all_to_all(ask, BOTH, 0, 0, tiled=True)  14.3 us
    all_to_all x1, blocking collectives, compute(): answer = lax.all_to_all(reply, BOTH, 0, 0, tiled=True)  13 us
    pallas_call x6, Pallas kernels, call(): pl.pallas_call(kernel, out_shape=outs if single else (*(pltpu.HBM(a.shape...  10.8 us
    all_to_all x1, waiting for transfers between devices, compute(): answer_two = lax.all_to_all(reply_two, BOTH, 0, 0, tiled=True)  6.31 us
    ppermute x3, starting transfers between devices, compute(): lax.ppermute(finals[q], 'dev', [(i, i ^ 2 * q) for i in range(members)])  4.44 us
    ppermute x3, waiting for transfers between devices, compute(): lax.ppermute(finals[q], 'dev', [(i, i ^ 2 * q) for i in range(members)])  4.2 us
    all_to_all x1, starting transfers between devices, compute(): answer_two = lax.all_to_all(reply_two, BOTH, 0, 0, tiled=True)  2.6 us
  transfers between devices with their start and end apart: 4, of which 3 were waited for; matrix products, arithmetic and copies ran while one was open for 0% of the time, Pallas kernels for 9%

profile of v13, /device:TPU:0, one launch (start us, length us, event | category | flops | bytes accessed | tf_op | source)
XLA Modules:
  0.0 55.7 jit_solution(1784032748611346453)
XLA Ops:
  0.0 1.4 %shard_map.82 = (s32[32,1,128]{2,1,0:T(1,128)S(1)}, bf16[128,128]{1,0:T(8,128)(2,1)S(1)}, bf16[128,200]{1,0:T(8,128)(2,1)S(1)}, bf16[192,192]{1,0:T(8,128)(2,1)S(1)}, bf16[128,768]{1,0:T(8,128)(2,1)S(1)}) custom-call(s32[25,128]{1,0:T(8,128)} %bitcast.3, s32[25,128]{1,0:T(8,128)} %bitcast.4, s32[1,128]{1,0:T(1,128)} %bitcast.5, bf16[128,768]{1,0:T(8,128)(2,1)} %features_hbm.3), custom_call_target="tpu_custom_call" | custom-call | flops 9437184 | bytes 593408 | tf_op jit(solution)/shard_map/pallas_call | solution.py:56
  1.4 14.3 %all_to_all.15.asked_ref = s32[32,1,128]{2,1,0:T(1,128)S(1)} all-to-all(s32[32,1,128]{2,1,0:T(1,128)S(1)} %get-tuple-element.28), channel_id=1, replica_groups=mesh['grp'=4,'dev'=8] {'grp','dev'}, dimensions={0} | all-to-all | bytes 32768 | tf_op jit(solution)/shard_map/all_to_all | solution.py:335
  15.7 0.6 %shard_map.83 = (bf16[32,3,2,768]{3,2,1,0:T(2,128)(2,1)S(1)}, bf16[192,128]{1,0:T(8,128)(2,1)S(1)}) custom-call(s32[32,1,128]{2,1,0:T(1,128)S(1)} %all_to_all.15.asked_ref, bf16[192,192]{1,0:T(8,128)(2,1)S(1)} %get-tuple-element.29.order_ref, bf16[128,768]{1,0:T(8,128)(2,1)S(1)} %get-tuple-element.26.source_ref.features_ref), custom_call_target="tpu_custom_call" | custom-call | flops 37748736 | bytes 630784 | tf_op jit(solution)/shard_map/pallas_call | solution.py:56
  16.3 13.0 %all_to_all.16.answer_ref = bf16[32,3,2,768]{3,2,1,0:T(2,128)(2,1)S(1)} all-to-all(bf16[32,3,2,768]{3,2,1,0:T(2,128)(2,1)S(1)} %get-tuple-element.30), channel_id=1, replica_groups=mesh['grp'=4,'dev'=8] {'grp','dev'}, dimensions={0} | all-to-all | bytes 589824 | tf_op jit(solution)/shard_map/all_to_all | solution.py:344
  29.4 1.3 %shard_map.84 = (bf16[32,3,2,768]{3,2,1,0:T(2,128)(2,1)}, bf16[128,768]{1,0:T(8,128)(2,1)}, bf16[32,3,2,768]{3,2,1,0:T(2,128)(2,1)}) custom-call(bf16[128,768]{1,0:T(8,128)(2,1)S(1)} %get-tuple-element.26.source_ref.features_ref, bf16[128,128]{1,0:T(8,128)(2,1)S(1)} %get-tuple-element.27.near_ref, bf16[32,3,2,768]{3,2,1,0:T(2,128)(2,1)S(1)} %all_to_all.16.answer_ref, ...), custom_call_target="tpu_custom_call" | custom-call | flops 100663296 | bytes 1411072 | tf_op jit(solution)/shard_map/pallas_call | solution.py:56
  30.6 2.6 %all-to-all-start.2 = ((bf16[32,3,2,768]{3,2,1,0:T(2,128)(2,1)}), bf16[32,3,2,768]{3,2,1,0:T(2,128)(2,1)S(1)}, u32[]{:S(2)}, u32[]{:S(2)}) async-start(bf16[32,3,2,768]{3,2,1,0:T(2,128)(2,1)} %get-tuple-element.40), calls=%async_computation.2 | async-start | bytes 589824 | tf_op jit(solution)/shard_map/all_to_all | solution.py:358
  33.2 5.0 %shard_map.85 = (bf16[128,1024]{1,0:T(8,128)(2,1)}, bf16[128,128]{1,0:T(8,128)(2,1)}, bf16[96,1024]{1,0:T(8,128)(2,1)S(1)}, bf16[128,104]{1,0:T(8,128)(2,1)S(1)}...) custom-call(bf16[768,1024]{1,0:T(8,128)(2,1)} %self_one_hbm.1, ...), custom_call_target="tpu_custom_call" | custom-call | flops 1275068416 | bytes 11436544 | tf_op jit(solution)/shard_map/pallas_call | solution.py:56
  38.3 6.3 %all-to-all-done.2.answer_ref = bf16[32,3,2,768]{3,2,1,0:T(2,128)(2,1)S(1)} async-done(((bf16[32,3,2,768]{3,2,1,0:T(2,128)(2,1)}), bf16[32,3,2,768]{3,2,1,0:T(2,128)(2,1)S(1)}, u32[]{:S(2)}, u32[]{:S(2)}) %all-to-all-start.2) | async-done | bytes 294944 | tf_op jit(solution)/shard_map/all_to_all | solution.py:358
  44.6 0.0 copy-start
  44.6 1.6 %shard_map.86 = (bf16[32,1024]{1,0:T(8,128)(2,1)S(1)}, bf16[32,1024]{1,0:T(8,128)(2,1)S(1)}, bf16[32,1024]{1,0:T(8,128)(2,1)S(1)}, bf16[32,1024]{1,0:T(8,128)(2,1)S(1)}) custom-call(bf16[1024,1024]{1,0:T(8,128)(2,1)} %neigh_two_hbm.3, bf16[128,1024]{1,0:T(8,128)(2,1)} %get-tuple-element.36.final_hbm, bf16[768,1024]{1,0:T(8,128)(2,1)S(1)} %get-tuple-element.37.neigh_one_ref, ...), custom_call_target="tpu_custom_call" | custom-call | flops 620756992 | bytes 5928960 | tf_op jit(solution)/shard_map/pallas_call | solution.py:56
  46.1 0.1 collective-permute-start
  46.2 0.2 collective-permute-start.1
  46.4 4.1 %collective-permute-start.2 = (bf16[32,1024]{1,0:T(8,128)(2,1)S(1)}, bf16[32,1024]{1,0:T(8,128)(2,1)S(1)}, u32[]{:S(2)}, u32[]{:S(2)}) collective-permute-start(bf16[32,1024]{1,0:T(8,128)(2,1)S(1)} %get-tuple-element.46), channel_id=1, source_target_pairs={{0,6},{1,7},{2,4},{3,5},{4,2},{5,3},{6,0},{7,1},{8,14},{9,15},{10,... | collective-permute-start | bytes 196616 | tf_op jit(solution)/shard_map/ppermute | solution.py:405
  50.6 0.7 %collective-permute-done.refs_1_ = bf16[32,1024]{1,0:T(8,128)(2,1)S(1)} collective-permute-done((bf16[32,1024]{1,0:T(8,128)(2,1)S(1)}, bf16[32,1024]{1,0:T(8,128)(2,1)S(1)}, u32[]{:S(2)}, u32[]{:S(2)}) %collective-permute-start) | collective-permute-done | bytes 65568 | tf_op jit(solution)/shard_map/ppermute | solution.py:405
  51.3 3.5 %collective-permute-done.1.refs_2_ = bf16[32,1024]{1,0:T(8,128)(2,1)S(1)} collective-permute-done((bf16[32,1024]{1,0:T(8,128)(2,1)S(1)}, bf16[32,1024]{1,0:T(8,128)(2,1)S(1)}, u32[]{:S(2)}, u32[]{:S(2)}) %collective-permute-start.1) | collective-permute-done | bytes 65568 | tf_op jit(solution)/shard_map/ppermute | solution.py:405
  54.8 0.0 collective-permute-done.2.refs_3_
  54.8 0.0 copy-done
  54.8 0.9 %shard_map.87 = bf16[128,1024]{1,0:T(8,128)(2,1)} custom-call(bf16[128,128]{1,0:T(8,128)(2,1)S(1)} %copy-done, bf16[32,1024]{1,0:T(8,128)(2,1)S(1)} %get-tuple-element.43.refs_0_, bf16[32,1024]{1,0:T(8,128)(2,1)S(1)} %collective-permute-done.refs_1_, bf16[32,1024]{1,0:T(8,128)(2,1)S(1)} %collective-permute-done.1.refs_2_, ...), custom_call_target="tpu_custom_call" | custom-call | flops 33554432 | bytes 557056 | tf_op jit(solution)/shard_map/pallas_call | solution.py:56
Async XLA Ops:
  30.6 13.9 %all-to-all-start.2 = ((bf16[32,3,2,768]{3,2,1,0:T(2,128)(2,1)}), bf16[32,3,2,768]{3,2,1,0:T(2,128)(2,1)S(1)}, u32[]{:S(2)}, u32[]{:S(2)}) async-start(bf16[32,3,2,768]{3,2,1,0:T(2,128)(2,1)} %get-tuple-element.40), calls=%async_computation.2 | async-start | bytes 589824 | tf_op jit(solution)/shard_map/all_to_all | solution.py:358
  44.6 10.2 %copy-start = (bf16[128,128]{1,0:T(8,128)(2,1)S(1)}, bf16[128,128]{1,0:T(8,128)(2,1)}, u32[]{:S(2)}) copy-start(bf16[128,128]{1,0:T(8,128)(2,1)} %get-tuple-element.35.place_ref) | copy-start | bytes 98308
  46.1 5.2 %collective-permute-start = (bf16[32,1024]{1,0:T(8,128)(2,1)S(1)}, bf16[32,1024]{1,0:T(8,128)(2,1)S(1)}, u32[]{:S(2)}, u32[]{:S(2)}) collective-permute-start(bf16[32,1024]{1,0:T(8,128)(2,1)S(1)} %get-tuple-element.44), channel_id=1, source_target_pairs={{0,2},{1,3},{2,0},{3,1},{4,6},{5,7},{6,4},{7,5},{8,10},{9,11},{10,... | collective-permute-start | bytes 196616 | tf_op jit(solution)/shard_map/ppermute | solution.py:405
  46.2 8.6 %collective-permute-start.1 = (bf16[32,1024]{1,0:T(8,128)(2,1)S(1)}, bf16[32,1024]{1,0:T(8,128)(2,1)S(1)}, u32[]{:S(2)}, u32[]{:S(2)}) collective-permute-start(bf16[32,1024]{1,0:T(8,128)(2,1)S(1)} %get-tuple-element.45), channel_id=1, source_target_pairs={{0,4},{1,5},{2,6},{3,7},{4,0},{5,1},{6,2},{7,3},{8,12},{9,13},{10,... | collective-permute-start | bytes 196616 | tf_op jit(solution)/shard_map/ppermute | solution.py:405
  46.4 8.3 %collective-permute-start.2 = (bf16[32,1024]{1,0:T(8,128)(2,1)S(1)}, bf16[32,1024]{1,0:T(8,128)(2,1)S(1)}, u32[]{:S(2)}, u32[]{:S(2)}) collective-permute-start(bf16[32,1024]{1,0:T(8,128)(2,1)S(1)} %get-tuple-element.46), channel_id=1, source_target_pairs={{0,6},{1,7},{2,4},{3,5},{4,2},{5,3},{6,0},{7,1},{8,14},{9,15},{10,... | collective-permute-start | bytes 196616 | tf_op jit(solution)/shard_map/ppermute | solution.py:405

commit v14 on v10

--- a/solution.py
+++ b/solution.py
@@ -99,9 +99,23 @@
         copy.start()
     own = lax.axis_index("grp") * members + lax.axis_index("dev")
     peer = iota((peers, rows), 0)
+    size = peers * CAP
+    line = iota((size, size), 0)
+    device = divide(line, CAP)
+    order_ref[...] = bits(iota((size, size), 1) == (line - device * CAP) * peers + device).astype(BF16)
+
+    @pl.loop(0, 2)
+    def _(i):
+        @pl.when(i == 0)
+        def _():
+            copies[0].wait()
+            copies[1].wait()
+
+        @pl.when(i == 1)
+        def _():
+            copies[2].wait()
+
     prefix = earlier(rows)
-    for copy in copies:
-        copy.wait()
     slots = jnp.where(mask[...] > 0, ids[...], -1)
     owner = divide(jnp.maximum(slots, 0), rows)
     row = slots - owner * rows
@@ -146,12 +160,7 @@
     near_ref[...] = near.astype(F32).T.astype(BF16)
     far = [bits((before <= k) & (k < before + total)).astype(BF16) for k in range(CAP)]
     far = jnp.concatenate(far, axis=0)
-    size = peers * CAP
-    line = iota((size, size), 0)
-    device = divide(line, CAP)
-    order = bits(iota((size, size), 1) == (line - device * CAP) * peers + device).astype(BF16)
-    order_ref[...] = order
-    far_ref[:, :size] = dot(order, far).T.astype(BF16)
+    far_ref[:, :size] = dot(order_ref[...], far).T.astype(BF16)
     count = jnp.broadcast_to(jnp.sum(bits(live), axis=0, keepdims=True), (rows, rows)).T.astype(BF16)
     far_ref[:, size:] = count[:, : far_ref.shape[1] - size]
     table.wait()
@@ -194,12 +203,16 @@
     mean_ref[...] = mean
     saved = pltpu.make_async_copy(mean_ref, mean_hbm, sems.at[1])
     saved.start()
-    store_rows(reply_ref, dot(pick_ref[...], mean).astype(BF16))
-    sent = pltpu.make_async_copy(reply_ref, reply_hbm, sems.at[2])
-    sent.start()
-    kept.wait()
-    saved.wait()
-    sent.wait()
+    half = reply_ref.shape[0] // 2
+    depth = pick_ref.shape[0] // 2
+    sent = []
+    for i in range(2):
+        piece = pl.ds(i * half, half)
+        store_rows(reply_ref.at[piece], dot(pick_ref[i * depth : (i + 1) * depth], mean).astype(BF16))
+        sent.append(pltpu.make_async_copy(reply_ref.at[piece], reply_hbm.at[piece], sems.at[2 + i]))
+        sent[-1].start()
+    for copy in (kept, saved, *sent):
+        copy.wait()
 
 
 def between_kernel(
@@ -376,7 +389,7 @@
         ),
         (),
         (table, near, answer, far, pick),
-        [pltpu.VMEM((rows, width_in), BF16), pltpu.VMEM((peers, CAP // 2, 2, width_in), BF16), copies((3,))],
+        [pltpu.VMEM((rows, width_in), BF16), pltpu.VMEM((peers, CAP // 2, 2, width_in), BF16), copies((4,))],
         2 * rows * width_in * (size + rows) + 2 * size * rows * width_in,
         "layer_one",
         away=3,

time: 56.1 us -> 56 us (level)
  no operation moved by 1% of the time
where the time goes in v14:
time: 56 us; the launch traced here: 55.7 us
  blocking collectives  27.3 us (49%)
  waiting for transfers between devices  11.1 us (20%)
  Pallas kernels  10.7 us (19%)
  starting transfers between devices  6.48 us (12%)
    all_to_all x1, blocking collectives, body(): asked = lax.all_to_all(ask, BOTH, 0, 0, tiled=True)  14.3 us
    all_to_all x1, blocking collectives, body(): answer = lax.all_to_all(reply, BOTH, 0, 0, tiled=True)  13 us
    pallas_call x6, Pallas kernels, call(): pl.pallas_call(kernel, out_shape=outs if single else (*(pltpu.HBM(a.shape...  10.7 us
    all_to_all x1, waiting for transfers between devices, body(): answer_two = lax.all_to_all(reply_two, BOTH, 0, 0, tiled=True)  6.31 us
    ppermute x3, waiting for transfers between devices, body(): lax.ppermute(finals[q], 'dev', [(i, (i + 2 * q) % members) for i in range...  4.8 us
    ppermute x3, starting transfers between devices, body(): lax.ppermute(finals[q], 'dev', [(i, (i + 2 * q) % members) for i in range...  3.87 us
    all_to_all x1, starting transfers between devices, body(): answer_two = lax.all_to_all(reply_two, BOTH, 0, 0, tiled=True)  2.6 us
  transfers between devices with their start and end apart: 4, of which 3 were waited for; matrix products, arithmetic and copies ran while one was open for 0% of the time, Pallas kernels for 9%

profile of v14, /device:TPU:0, one launch (start us, length us, event | category | flops | bytes accessed | tf_op | source)
XLA Modules:
  0.0 55.7 jit_solution(13208964918304218549)
XLA Ops:
  0.0 1.4 %ask.1 = (s32[32,1,128]{2,1,0:T(1,128)S(1)}, bf16[128,128]{1,0:T(8,128)(2,1)S(1)}, bf16[128,200]{1,0:T(8,128)(2,1)S(1)}, bf16[192,192]{1,0:T(8,128)(2,1)S(1)}, bf16[128,768]{1,0:T(8,128)(2,1)S(1)}) custom-call(s32[25,128]{1,0:T(8,128)} %bitcast.3, s32[25,128]{1,0:T(8,128)} %bitcast.4, s32[1,128]{1,0:T(1,128)} %bitcast.5, bf16[128,768]{1,0:T(8,128)(2,1)} %features_hbm.3), custom_call_target="tpu_custom_call" | custom-call | flops 9437184 | bytes 593408 | tf_op jit(solution)/shard_map/ask/pallas_call | solution.py:55
  1.4 14.3 %all_to_all.15.asked_ref = s32[32,1,128]{2,1,0:T(1,128)S(1)} all-to-all(s32[32,1,128]{2,1,0:T(1,128)S(1)} %get-tuple-element.28), channel_id=1, replica_groups=mesh['grp'=4,'dev'=8] {'grp','dev'}, dimensions={0} | all-to-all | bytes 32768 | tf_op jit(solution)/shard_map/all_to_all | solution.py:372
  15.7 0.6 %serve.1 = (bf16[32,3,2,768]{3,2,1,0:T(2,128)(2,1)S(1)}, bf16[192,128]{1,0:T(8,128)(2,1)S(1)}) custom-call(s32[32,1,128]{2,1,0:T(1,128)S(1)} %all_to_all.15.asked_ref, bf16[192,192]{1,0:T(8,128)(2,1)S(1)} %get-tuple-element.29.order_ref, bf16[128,768]{1,0:T(8,128)(2,1)S(1)} %get-tuple-element.26.source_ref.features_ref), custom_call_target="tpu_custom_call" | custom-call | flops 37748736 | bytes 630784 | tf_op jit(solution)/shard_map/serve/pallas_call | solution.py:55
  16.3 13.0 %all_to_all.16.answer_ref = bf16[32,3,2,768]{3,2,1,0:T(2,128)(2,1)S(1)} all-to-all(bf16[32,3,2,768]{3,2,1,0:T(2,128)(2,1)S(1)} %get-tuple-element.30), channel_id=1, replica_groups=mesh['grp'=4,'dev'=8] {'grp','dev'}, dimensions={0} | all-to-all | bytes 589824 | tf_op jit(solution)/shard_map/all_to_all | solution.py:382
  29.4 1.2 %layer_one.1 = (bf16[32,3,2,768]{3,2,1,0:T(2,128)(2,1)}, bf16[128,768]{1,0:T(8,128)(2,1)}, bf16[32,3,2,768]{3,2,1,0:T(2,128)(2,1)}) custom-call(bf16[128,768]{1,0:T(8,128)(2,1)S(1)} %get-tuple-element.26.source_ref.features_ref, bf16[128,128]{1,0:T(8,128)(2,1)S(1)} %get-tuple-element.27.near_ref, bf16[32,3,2,768]{3,2,1,0:T(2,128)(2,1)S(1)} %all_to_all.16.answer_ref, ...), custom_call_target="tpu_custom_call" | custom-call | flops 100663296 | bytes 1411072 | tf_op jit(solution)/shard_map/layer_one/pallas_call | solution.py:55
  30.6 2.6 %all-to-all-start.2 = ((bf16[32,3,2,768]{3,2,1,0:T(2,128)(2,1)}), bf16[32,3,2,768]{3,2,1,0:T(2,128)(2,1)S(1)}, u32[]{:S(2)}, u32[]{:S(2)}) async-start(bf16[32,3,2,768]{3,2,1,0:T(2,128)(2,1)} %get-tuple-element.40), calls=%async_computation.2 | async-start | bytes 589824 | tf_op jit(solution)/shard_map/all_to_all | solution.py:397
  33.2 5.0 %between.1 = (bf16[128,1024]{1,0:T(8,128)(2,1)}, bf16[128,128]{1,0:T(8,128)(2,1)}, bf16[96,1024]{1,0:T(8,128)(2,1)S(1)}, bf16[128,104]{1,0:T(8,128)(2,1)S(1)}, b...) custom-call(bf16[768,1024]{1,0:T(8,128)(2,1)} %self_one_hbm.1, ...), custom_call_target="tpu_custom_call" | custom-call | flops 1275068416 | bytes 11436544 | tf_op jit(solution)/shard_map/between/pallas_call | solution.py:55
  38.2 6.3 %all-to-all-done.2.answer_ref = bf16[32,3,2,768]{3,2,1,0:T(2,128)(2,1)S(1)} async-done(((bf16[32,3,2,768]{3,2,1,0:T(2,128)(2,1)}), bf16[32,3,2,768]{3,2,1,0:T(2,128)(2,1)S(1)}, u32[]{:S(2)}, u32[]{:S(2)}) %all-to-all-start.2) | async-done | bytes 294944 | tf_op jit(solution)/shard_map/all_to_all | solution.py:397
  44.5 0.0 copy-start
  44.5 1.5 %layer_two.1 = (bf16[32,1024]{1,0:T(8,128)(2,1)S(1)}, bf16[32,1024]{1,0:T(8,128)(2,1)S(1)}, bf16[32,1024]{1,0:T(8,128)(2,1)S(1)}, bf16[32,1024]{1,0:T(8,128)(2,1)S(1)}) custom-call(bf16[1024,1024]{1,0:T(8,128)(2,1)} %neigh_two_hbm.3, bf16[128,1024]{1,0:T(8,128)(2,1)} %get-tuple-element.36.final_hbm, bf16[768,1024]{1,0:T(8,128)(2,1)S(1)} %get-tuple-element.37.neigh_one_ref, ...), custom_call_target="tpu_custom_call" | custom-call | flops 620756992 | bytes 5928960 | tf_op jit(solution)/shard_map/layer_two/pallas_call | solution.py:55
  46.1 0.1 collective-permute-start
  46.2 0.3 collective-permute-start.1
  46.4 3.5 %collective-permute-start.2 = (bf16[32,1024]{1,0:T(8,128)(2,1)S(1)}, bf16[32,1024]{1,0:T(8,128)(2,1)S(1)}, u32[]{:S(2)}, u32[]{:S(2)}) collective-permute-start(bf16[32,1024]{1,0:T(8,128)(2,1)S(1)} %get-tuple-element.46), channel_id=1, source_target_pairs={{0,6},{1,7},{2,0},{3,1},{4,2},{5,3},{6,4},{7,5},{8,14},{9,15},{10,... | collective-permute-start | bytes 196616 | tf_op jit(solution)/shard_map/ppermute | solution.py:446
  50.0 3.0 %collective-permute-done.refs_1_ = bf16[32,1024]{1,0:T(8,128)(2,1)S(1)} collective-permute-done((bf16[32,1024]{1,0:T(8,128)(2,1)S(1)}, bf16[32,1024]{1,0:T(8,128)(2,1)S(1)}, u32[]{:S(2)}, u32[]{:S(2)}) %collective-permute-start) | collective-permute-done | bytes 65568 | tf_op jit(solution)/shard_map/ppermute | solution.py:446
  53.0 1.8 %collective-permute-done.1.refs_2_ = bf16[32,1024]{1,0:T(8,128)(2,1)S(1)} collective-permute-done((bf16[32,1024]{1,0:T(8,128)(2,1)S(1)}, bf16[32,1024]{1,0:T(8,128)(2,1)S(1)}, u32[]{:S(2)}, u32[]{:S(2)}) %collective-permute-start.1) | collective-permute-done | bytes 65568 | tf_op jit(solution)/shard_map/ppermute | solution.py:446
  54.8 0.0 collective-permute-done.2.refs_3_
  54.8 0.0 copy-done
  54.8 0.9 %scatter.1 = bf16[128,1024]{1,0:T(8,128)(2,1)} custom-call(bf16[128,128]{1,0:T(8,128)(2,1)S(1)} %copy-done, bf16[32,1024]{1,0:T(8,128)(2,1)S(1)} %get-tuple-element.43.refs_0_, bf16[32,1024]{1,0:T(8,128)(2,1)S(1)} %collective-permute-done.refs_1_, bf16[32,1024]{1,0:T(8,128)(2,1)S(1)} %collective-permute-done.1.refs_2_, ...), custom_call_target="tpu_custom_call" | custom-call | flops 33554432 | bytes 557056 | tf_op jit(solution)/shard_map/scatter/pallas_call | solution.py:55
Async XLA Ops:
  30.6 13.9 %all-to-all-start.2 = ((bf16[32,3,2,768]{3,2,1,0:T(2,128)(2,1)}), bf16[32,3,2,768]{3,2,1,0:T(2,128)(2,1)S(1)}, u32[]{:S(2)}, u32[]{:S(2)}) async-start(bf16[32,3,2,768]{3,2,1,0:T(2,128)(2,1)} %get-tuple-element.40), calls=%async_computation.2 | async-start | bytes 589824 | tf_op jit(solution)/shard_map/all_to_all | solution.py:397
  44.5 10.2 %copy-start = (bf16[128,128]{1,0:T(8,128)(2,1)S(1)}, bf16[128,128]{1,0:T(8,128)(2,1)}, u32[]{:S(2)}) copy-start(bf16[128,128]{1,0:T(8,128)(2,1)} %get-tuple-element.35.place_ref) | copy-start | bytes 98308
  46.1 6.9 %collective-permute-start = (bf16[32,1024]{1,0:T(8,128)(2,1)S(1)}, bf16[32,1024]{1,0:T(8,128)(2,1)S(1)}, u32[]{:S(2)}, u32[]{:S(2)}) collective-permute-start(bf16[32,1024]{1,0:T(8,128)(2,1)S(1)} %get-tuple-element.44), channel_id=1, source_target_pairs={{0,2},{1,3},{2,4},{3,5},{4,6},{5,7},{6,0},{7,1},{8,10},{9,11},{10,... | collective-permute-start | bytes 196616 | tf_op jit(solution)/shard_map/ppermute | solution.py:446
  46.2 8.6 %collective-permute-start.1 = (bf16[32,1024]{1,0:T(8,128)(2,1)S(1)}, bf16[32,1024]{1,0:T(8,128)(2,1)S(1)}, u32[]{:S(2)}, u32[]{:S(2)}) collective-permute-start(bf16[32,1024]{1,0:T(8,128)(2,1)S(1)} %get-tuple-element.45), channel_id=1, source_target_pairs={{0,4},{1,5},{2,6},{3,7},{4,0},{5,1},{6,2},{7,3},{8,12},{9,13},{10,... | collective-permute-start | bytes 196616 | tf_op jit(solution)/shard_map/ppermute | solution.py:446
  46.4 8.4 %collective-permute-start.2 = (bf16[32,1024]{1,0:T(8,128)(2,1)S(1)}, bf16[32,1024]{1,0:T(8,128)(2,1)S(1)}, u32[]{:S(2)}, u32[]{:S(2)}) collective-permute-start(bf16[32,1024]{1,0:T(8,128)(2,1)S(1)} %get-tuple-element.46), channel_id=1, source_target_pairs={{0,6},{1,7},{2,0},{3,1},{4,2},{5,3},{6,4},{7,5},{8,14},{9,15},{10,... | collective-permute-start | bytes 196616 | tf_op jit(solution)/shard_map/ppermute | solution.py:446
